TPU v7x, 32 devices: a whole 2x2x4 slice. The times are simulated.
32 devices in a mesh: seq: 8 (over y, x, core), dp: 4 (over z).
Axes of the slice: x: 2, y: 2, z: 4, core: 2. Of those that a mesh axis runs over, the one named last changes fastest.
Arguments:
- tokens: bfloat16 [4, 1024, 2048], P('dp', 'seq'), may hold values from -6 to 6
- valid_mask: int32 [4, 1024], P('dp', 'seq'), may hold values from 0 to 1, as said below
- teacher: bfloat16 [4, 1024, 2048], P('dp', 'seq'), may hold values from -6 to 6
- norm_one: bfloat16 [2048], P(('seq', 'dp')), may hold values from 0.5 to 1.5
- proj_gelu: bfloat16 [2048, 2560], P(('seq', 'dp')), may hold values from -0.125 to 0.125
- proj_rec: bfloat16 [2048, 2560], P(('seq', 'dp')), may hold values from -0.125 to 0.125
- conv_taps: bfloat16 [4, 2560], P(None, ('seq', 'dp')), may hold values from -3 to 3
- conv_bias: bfloat16 [2560], P(('seq', 'dp')), may hold values from -3 to 3
- gate_rec_w: bfloat16 [2560, 256], P(('seq', 'dp')), may hold values from -0.375 to 0.375
- gate_rec_b: bfloat16 [2560], P(('seq', 'dp')), may hold values from -4 to 4
- gate_inp_w: bfloat16 [2560, 256], P(('seq', 'dp')), may hold values from -0.375 to 0.375
- gate_inp_b: bfloat16 [2560], P(('seq', 'dp')), may hold values from -4 to 4
- rec_param: bfloat16 [2560], P(('seq', 'dp')), may hold values from 4 to 16
- proj_out: bfloat16 [2560, 2048], P(None, ('seq', 'dp')), may hold values from -0.25 to 0.25
- norm_two: bfloat16 [2048], P(('seq', 'dp')), may hold values from 0.5 to 1.5
- mlp_gate: bfloat16 [2048, 6144], P(('seq', 'dp')), may hold values from -0.125 to 0.125
- mlp_up: bfloat16 [2048, 6144], P(('seq', 'dp')), may hold values from -0.125 to 0.125
- mlp_down: bfloat16 [6144, 2048], P(None, ('seq', 'dp')), may hold values from -0.15625 to 0.15625
Outputs:
- output: bfloat16 [4, 1024, 2048], P('dp', 'seq')
- mean_loss: float32 [], replicated
- grad_tokens: bfloat16 [4, 1024, 2048], P('dp', 'seq')
- grad_norm_one: float32 [2048], P(('seq', 'dp'))
- grad_proj_gelu: float32 [2048, 2560], P(('seq', 'dp'))
- grad_proj_rec: float32 [2048, 2560], P(('seq', 'dp'))
- grad_conv_taps: float32 [4, 2560], P(None, ('seq', 'dp'))
- grad_conv_bias: float32 [2560], P(('seq', 'dp'))
- grad_gate_rec_w: float32 [2560, 256], P(('seq', 'dp'))
- grad_gate_rec_b: float32 [2560], P(('seq', 'dp'))
- grad_gate_inp_w: float32 [2560, 256], P(('seq', 'dp'))
- grad_gate_inp_b: float32 [2560], P(('seq', 'dp'))
- grad_rec_param: float32 [2560], P(('seq', 'dp'))
- grad_proj_out: float32 [2560, 2048], P(None, ('seq', 'dp'))
- grad_norm_two: float32 [2048], P(('seq', 'dp'))
- grad_mlp_gate: float32 [2048, 6144], P(('seq', 'dp'))
- grad_mlp_up: float32 [2048, 6144], P(('seq', 'dp'))
- grad_mlp_down: float32 [6144, 2048], P(None, ('seq', 'dp'))
Inputs may be any that keep to these rules, and one draw needn't show every extreme that they name: `valid_mask`: the last token of every sequence has 1.
All inputs are finite; a program needn't handle non-finite values.
Results may differ from a plain program's by a relative error of at most 0.0075.
Values may be sent and summed in bfloat16 or wider, within the bound.
A program may use at most 384 MiB of HBM per device.

v0:
```python
import jax
import jax.numpy as jnp
from jax import lax
from jax.sharding import PartitionSpec as P

NB = 10
BW = 256
CONV = 4


norm_eps = 1e-06
gate_power = 8.0
floor_square = 0.0001


def from_behind(value, axis, steps):
    count = lax.axis_size(axis)
    first, last = (max(0, -steps), min(count, count - steps))
    return lax.ppermute(value, axis, [(source, source + steps) for source in range(first, last)])


def rms_norm(values, gain_vec):
    return (
        values * lax.rsqrt(jnp.mean(values * values, axis=-1, keepdims=True) + norm_eps) * gain_vec
    )


def gate_terms(gate_rec, gate_inp, conv_val, rec_vals):
    recur_gate = jax.nn.sigmoid(gate_rec)
    admit_gate = jax.nn.sigmoid(gate_inp)
    log_decay = -gate_power * recur_gate * jax.nn.softplus(-rec_vals)
    decays = jnp.exp(log_decay)
    scaler = jnp.sqrt(jnp.maximum(-jnp.expm1(2.0 * log_decay), floor_square))
    return (decays, scaler * admit_gate * conv_val)


def compose(earlier, later_pair):
    return (earlier[0] * later_pair[0], later_pair[0] * earlier[1] + later_pair[1])


def contract_rows(left, right):
    return lax.dot_general(
        left, right, (((0,), (0,)), ((), ())), preferred_element_type=jnp.float32
    )


def times_trans(left, right):
    return lax.dot_general(
        left, right, (((1,), (1,)), ((), ())), preferred_element_type=jnp.float32
    )


def gelu_product(first, second):
    return jax.nn.gelu(first, approximate=True) * second


def on_device(
    tokens,
    valid_mask,
    teacher,
    norm_one,
    proj_gelu,
    proj_rec,
    conv_taps,
    conv_bias,
    gate_rec_w,
    gate_rec_b,
    gate_inp_w,
    gate_inp_b,
    rec_param,
    proj_out,
    norm_two,
    mlp_gate,
    mlp_up,
    mlp_down,
):
    full_w = (
        lax.all_gather(norm_one, ("seq", "dp"), axis=0, tiled=True),
        lax.all_gather(proj_gelu, ("seq", "dp"), axis=0, tiled=True),
        lax.all_gather(proj_rec, ("seq", "dp"), axis=0, tiled=True),
        lax.all_gather(conv_taps, ("seq", "dp"), axis=1, tiled=True),
        lax.all_gather(conv_bias, ("seq", "dp"), axis=0, tiled=True),
        lax.all_gather(gate_rec_w, ("seq", "dp"), axis=0, tiled=True),
        lax.all_gather(gate_rec_b, ("seq", "dp"), axis=0, tiled=True),
        lax.all_gather(gate_inp_w, ("seq", "dp"), axis=0, tiled=True),
        lax.all_gather(gate_inp_b, ("seq", "dp"), axis=0, tiled=True),
        lax.all_gather(rec_param, ("seq", "dp"), axis=0, tiled=True),
        lax.all_gather(proj_out, ("seq", "dp"), axis=1, tiled=True),
        lax.all_gather(norm_two, ("seq", "dp"), axis=0, tiled=True),
        lax.all_gather(mlp_gate, ("seq", "dp"), axis=0, tiled=True),
        lax.all_gather(mlp_up, ("seq", "dp"), axis=0, tiled=True),
        lax.all_gather(mlp_down, ("seq", "dp"), axis=1, tiled=True),
    )
    seq_count, local_len, model_width = tokens.shape
    row_count = seq_count * local_len
    rec_width = full_w[2].shape[1]
    fp32 = jnp.float32
    half = jnp.bfloat16
    flat_in = tokens.reshape(row_count, model_width).astype(fp32)
    gain_one = full_w[0].astype(fp32)
    normed_low = rms_norm(flat_in, gain_one).astype(half)
    gelu_pre = jnp.dot(normed_low, full_w[1], preferred_element_type=fp32)
    rec_pre = jnp.dot(normed_low, full_w[2], preferred_element_type=fp32)
    rec_seq = rec_pre.reshape(seq_count, local_len, rec_width)
    prev_edge = from_behind(rec_seq[:, local_len - (CONV - 1) :, :], "seq", 1)
    padded = jnp.concatenate([prev_edge, rec_seq], axis=1)
    tap_vals = full_w[3].astype(fp32)
    conv_sum = full_w[4].astype(fp32) + jnp.zeros_like(rec_seq)
    for offset in range(CONV):
        conv_sum = (
            conv_sum
            + tap_vals[offset] * padded[:, CONV - 1 - offset : CONV - 1 - offset + local_len]
        )
    conv_low = conv_sum.astype(half)
    conv_val = conv_low.astype(fp32)
    blocks = conv_low.reshape(row_count, NB, BW)
    rec_mat = full_w[5].reshape(NB, BW, BW)
    inp_mat = full_w[7].reshape(NB, BW, BW)
    gate_rec = jnp.einsum("tki,kij->tkj", blocks, rec_mat, preferred_element_type=fp32).reshape(
        seq_count, local_len, rec_width
    ) + full_w[6].astype(fp32)
    gate_inp = jnp.einsum("tki,kij->tkj", blocks, inp_mat, preferred_element_type=fp32).reshape(
        seq_count, local_len, rec_width
    ) + full_w[8].astype(fp32)
    rec_vals = full_w[9].astype(fp32)
    decays, drives = gate_terms(gate_rec, gate_inp, conv_val, rec_vals)
    cum_decay, local_state = lax.associative_scan(compose, (decays, drives), axis=1)
    total_decay = cum_decay[:, -1]
    total_state = local_state[:, -1]

    def forward_turn(turn_index, incoming):
        return from_behind(total_decay * incoming + total_state, "seq", 1)

    entering = lax.fori_loop(0, lax.axis_size("seq") - 1, forward_turn, jnp.zeros_like(total_state))
    states = local_state + cum_decay * entering[:, None, :]
    flat_states = states.reshape(row_count, rec_width)
    mixed_low = gelu_product(gelu_pre, flat_states).astype(half)
    middle = flat_in + jnp.dot(mixed_low, full_w[10], preferred_element_type=fp32)
    gain_two = full_w[11].astype(fp32)
    normed_two_low = rms_norm(middle, gain_two).astype(half)
    gate_pre = jnp.dot(normed_two_low, full_w[12], preferred_element_type=fp32)
    up_pre = jnp.dot(normed_two_low, full_w[13], preferred_element_type=fp32)
    hidden_low = gelu_product(gate_pre, up_pre).astype(half)
    result = middle + jnp.dot(hidden_low, full_w[14], preferred_element_type=fp32)
    target = teacher.reshape(row_count, model_width).astype(fp32)
    differ = result - target
    mask_val = valid_mask.reshape(row_count).astype(fp32)
    totals = lax.psum(
        (jnp.sum(mask_val), 0.5 * jnp.sum(mask_val[:, None] * differ * differ)), ("seq", "dp")
    )
    token_total = row_count * lax.axis_size("seq") * lax.axis_size("dp")
    mean_loss = totals[1] / (totals[0] * model_width)
    back_w = (
        lax.all_gather(norm_one, ("seq", "dp"), axis=0, tiled=True),
        lax.all_gather(proj_gelu, ("seq", "dp"), axis=0, tiled=True),
        lax.all_gather(proj_rec, ("seq", "dp"), axis=0, tiled=True),
        lax.all_gather(conv_taps, ("seq", "dp"), axis=1, tiled=True),
        lax.all_gather(conv_bias, ("seq", "dp"), axis=0, tiled=True),
        lax.all_gather(gate_rec_w, ("seq", "dp"), axis=0, tiled=True),
        lax.all_gather(gate_rec_b, ("seq", "dp"), axis=0, tiled=True),
        lax.all_gather(gate_inp_w, ("seq", "dp"), axis=0, tiled=True),
        lax.all_gather(gate_inp_b, ("seq", "dp"), axis=0, tiled=True),
        lax.all_gather(rec_param, ("seq", "dp"), axis=0, tiled=True),
        lax.all_gather(proj_out, ("seq", "dp"), axis=1, tiled=True),
        lax.all_gather(norm_two, ("seq", "dp"), axis=0, tiled=True),
        lax.all_gather(mlp_gate, ("seq", "dp"), axis=0, tiled=True),
        lax.all_gather(mlp_up, ("seq", "dp"), axis=0, tiled=True),
        lax.all_gather(mlp_down, ("seq", "dp"), axis=1, tiled=True),
    )
    grad_result = mask_val[:, None] * (token_total / totals[0]) * differ
    down_low = grad_result.astype(half)
    grad_mlp_down = contract_rows(hidden_low, down_low)
    grad_hidden = times_trans(down_low, back_w[14])
    _, pull_mlp = jax.vjp(gelu_product, gate_pre, up_pre)
    grad_gate_pre, grad_up_pre = pull_mlp(grad_hidden)
    gate_low = grad_gate_pre.astype(half)
    up_low = grad_up_pre.astype(half)
    grad_mlp_gate = contract_rows(normed_two_low, gate_low)
    grad_mlp_up = contract_rows(normed_two_low, up_low)
    grad_normed_two = times_trans(gate_low, back_w[12]) + times_trans(up_low, back_w[13])
    _, pull_norm_two = jax.vjp(rms_norm, middle, gain_two)
    grad_middle_norm, grad_norm_two = pull_norm_two(grad_normed_two)
    grad_middle = grad_result + grad_middle_norm
    middle_low = grad_middle.astype(half)
    grad_proj_out = contract_rows(mixed_low, middle_low)
    grad_mixed = times_trans(middle_low, back_w[10])
    _, pull_mix = jax.vjp(gelu_product, gelu_pre, flat_states)
    grad_gelu_pre, grad_states = pull_mix(grad_mixed)
    grad_states = grad_states.reshape(seq_count, local_len, rec_width)
    later_decay = jnp.concatenate([decays[:, 1:], jnp.ones_like(decays[:, :1])], axis=1)
    tail_decay, local_adj = lax.associative_scan(
        compose, (later_decay, grad_states), reverse=True, axis=1
    )
    head_term = decays[:, 0] * local_adj[:, 0]

    def backward_turn(turn_index, incoming):
        return from_behind(total_decay * incoming + head_term, "seq", -1)

    leaving = lax.fori_loop(0, lax.axis_size("seq") - 1, backward_turn, jnp.zeros_like(head_term))
    adjoint = local_adj + tail_decay * leaving[:, None, :]
    prior_state = jnp.concatenate([entering[:, None, :], states[:, :-1]], axis=1)
    _, pull_gates = jax.vjp(gate_terms, gate_rec, gate_inp, conv_val, rec_vals)
    grad_rec_gate, grad_inp_gate, grad_conv_direct, grad_rec_param = pull_gates(
        (adjoint * prior_state, adjoint)
    )
    rec_gate_low = grad_rec_gate.astype(half).reshape(row_count, NB, BW)
    inp_gate_low = grad_inp_gate.astype(half).reshape(row_count, NB, BW)
    grad_gate_rec_b = jnp.sum(rec_gate_low.reshape(row_count, rec_width).astype(fp32), axis=0)
    grad_gate_inp_b = jnp.sum(inp_gate_low.reshape(row_count, rec_width).astype(fp32), axis=0)
    grad_gate_rec_w = jnp.einsum(
        "tki,tkj->kij", blocks, rec_gate_low, preferred_element_type=fp32
    ).reshape(rec_width, BW)
    grad_gate_inp_w = jnp.einsum(
        "tki,tkj->kij", blocks, inp_gate_low, preferred_element_type=fp32
    ).reshape(rec_width, BW)
    back_rec_mat = back_w[5].reshape(NB, BW, BW)
    back_inp_mat = back_w[7].reshape(NB, BW, BW)
    gate_back = jnp.einsum(
        "tkj,kij->tki", rec_gate_low, back_rec_mat, preferred_element_type=fp32
    ) + jnp.einsum("tkj,kij->tki", inp_gate_low, back_inp_mat, preferred_element_type=fp32)
    grad_conv = grad_conv_direct + gate_back.reshape(seq_count, local_len, rec_width)
    grad_conv_bias = jnp.sum(grad_conv, axis=(0, 1))
    back_taps = back_w[3].astype(fp32)
    tap_grads = []
    grad_padded = jnp.zeros((seq_count, local_len + CONV - 1, rec_width), fp32)
    for offset in range(CONV):
        window = padded[:, CONV - 1 - offset : CONV - 1 - offset + local_len]
        tap_grads.append(jnp.sum(grad_conv * window, axis=(0, 1)))
        grad_padded = grad_padded + jnp.pad(
            back_taps[offset] * grad_conv, ((0, 0), (CONV - 1 - offset, offset), (0, 0))
        )
    grad_conv_taps = jnp.stack(tap_grads, axis=0)
    from_next = from_behind(grad_padded[:, : CONV - 1], "seq", -1)
    grad_rec_seq = grad_padded[:, CONV - 1 :] + jnp.pad(
        from_next, ((0, 0), (local_len - (CONV - 1), 0), (0, 0))
    )
    rec_back_low = grad_rec_seq.reshape(row_count, rec_width).astype(half)
    gelu_low = grad_gelu_pre.astype(half)
    grad_proj_rec = contract_rows(normed_low, rec_back_low)
    grad_proj_gelu = contract_rows(normed_low, gelu_low)
    grad_normed = times_trans(rec_back_low, back_w[2]) + times_trans(gelu_low, back_w[1])
    _, pull_norm_one = jax.vjp(rms_norm, flat_in, back_w[0].astype(fp32))
    grad_in_norm, grad_norm_one = pull_norm_one(grad_normed)
    grad_tokens = (grad_middle + grad_in_norm).reshape(tokens.shape).astype(half)
    summed = (
        lax.psum_scatter(grad_norm_one, ("seq", "dp"), scatter_dimension=0, tiled=True),
        lax.psum_scatter(grad_proj_gelu, ("seq", "dp"), scatter_dimension=0, tiled=True),
        lax.psum_scatter(grad_proj_rec, ("seq", "dp"), scatter_dimension=0, tiled=True),
        lax.psum_scatter(grad_conv_taps, ("seq", "dp"), scatter_dimension=1, tiled=True),
        lax.psum_scatter(grad_conv_bias, ("seq", "dp"), scatter_dimension=0, tiled=True),
        lax.psum_scatter(grad_gate_rec_w, ("seq", "dp"), scatter_dimension=0, tiled=True),
        lax.psum_scatter(grad_gate_rec_b, ("seq", "dp"), scatter_dimension=0, tiled=True),
        lax.psum_scatter(grad_gate_inp_w, ("seq", "dp"), scatter_dimension=0, tiled=True),
        lax.psum_scatter(grad_gate_inp_b, ("seq", "dp"), scatter_dimension=0, tiled=True),
        lax.psum_scatter(grad_rec_param, ("seq", "dp"), scatter_dimension=0, tiled=True),
        lax.psum_scatter(grad_proj_out, ("seq", "dp"), scatter_dimension=1, tiled=True),
        lax.psum_scatter(grad_norm_two, ("seq", "dp"), scatter_dimension=0, tiled=True),
        lax.psum_scatter(grad_mlp_gate, ("seq", "dp"), scatter_dimension=0, tiled=True),
        lax.psum_scatter(grad_mlp_up, ("seq", "dp"), scatter_dimension=0, tiled=True),
        lax.psum_scatter(grad_mlp_down, ("seq", "dp"), scatter_dimension=1, tiled=True),
    )
    output = result.reshape(tokens.shape).astype(half)
    return (
        output,
        mean_loss,
        grad_tokens,
        summed[0],
        summed[1],
        summed[2],
        summed[3],
        summed[4],
        summed[5],
        summed[6],
        summed[7],
        summed[8],
        summed[9],
        summed[10],
        summed[11],
        summed[12],
        summed[13],
        summed[14],
    )


def solution(mesh):
    in_specs = (
        P("dp", "seq", None),
        P("dp", "seq"),
        P("dp", "seq", None),
        P(("seq", "dp")),
        P(("seq", "dp"), None),
        P(("seq", "dp"), None),
        P(None, ("seq", "dp")),
        P(("seq", "dp")),
        P(("seq", "dp"), None),
        P(("seq", "dp")),
        P(("seq", "dp"), None),
        P(("seq", "dp")),
        P(("seq", "dp")),
        P(None, ("seq", "dp")),
        P(("seq", "dp")),
        P(("seq", "dp"), None),
        P(("seq", "dp"), None),
        P(None, ("seq", "dp")),
    )
    out_specs = (
        P("dp", "seq", None),
        P(),
        P("dp", "seq", None),
        P(("seq", "dp")),
        P(("seq", "dp"), None),
        P(("seq", "dp"), None),
        P(None, ("seq", "dp")),
        P(("seq", "dp")),
        P(("seq", "dp"), None),
        P(("seq", "dp")),
        P(("seq", "dp"), None),
        P(("seq", "dp")),
        P(("seq", "dp")),
        P(None, ("seq", "dp")),
        P(("seq", "dp")),
        P(("seq", "dp"), None),
        P(("seq", "dp"), None),
        P(None, ("seq", "dp")),
    )
    return jax.shard_map(
        on_device, mesh=mesh, in_specs=in_specs, out_specs=out_specs, check_vma=False
    )
```

profile of v0, /device:TPU:11, one launch (start us, length us, event | category | flops | bytes accessed | tf_op | source)
XLA Modules:
  0.0 4292.8 jit_solution(4317977598982749582)
XLA Ops:
  13.4 40.2 psum.15
  55.1 42.5 all-reduce.76
  97.6 59.6 %all-gather = bf16[32,80,4]{1,2,0:T(4,128)(2,1)S(1)} all-gather(bf16[1,80,4]{1,2,0:T(4,128)(2,1)S(1)} %bitcast.182), channel_id=1, replica_groups=mesh['seq'=8,'dp'=4] {'seq','dp'}, dimensions={0}, use_global_device_ids=true | all-gather | bytes 21120 | tf_op jit(solution)/shard_map/all_gather | solution.py:81
  159.3 5.6 fusion.90
  164.9 10.3 collective-permute-start.2
  185.3 26.0 all-gather.16.cloned.1.call-done
  219.8 4.5 convert_multiply_fusion.1
  323.3 9.9 slice.541
  333.2 9.9 slice.546
  343.2 9.9 slice.539
  405.9 4.9 pad.206
  410.9 4.8 pad.207
  417.7 4.8 pad.220
  422.5 4.9 pad.221
  429.3 40.4 while.20
  433.5 5.3 collective-permute-start
  439.6 5.3 collective-permute-start
  445.7 5.3 collective-permute-start
  451.8 5.1 collective-permute-start
  457.7 5.1 collective-permute-start
  463.6 5.1 collective-permute-start
  469.8 11.0 fusion.28
  480.8 7.9 multiply_reduce_fusion.7
  490.6 52.5 %all-gather.20.cloned.1.call-done = bf16[2048,6144]{1,0:T(8,128)(2,1)} async-done(((bf16[64,6144]{1,0:T(8,128)(2,1)}), bf16[2048,6144]{1,0:T(8,128)(2,1)}) %all-gather.20.cloned.1.call-update) | async-done | bytes 25165840 | tf_op jit(solution)/shard_map/all_gather | solution.py:90
  543.1 13.4 fusion.106
  556.5 142.3 %all-gather.22.cloned.1.call-done = bf16[2048,6144]{1,0:T(8,128)(2,1)} async-done(((bf16[64,6144]{1,0:T(8,128)(2,1)}), bf16[2048,6144]{1,0:T(8,128)(2,1)}) %all-gather.22.cloned.1.call-update) | async-done | bytes 25165840 | tf_op jit(solution)/shard_map/all_gather | solution.py:91
  698.8 15.7 multiply_convert_fusion.1
  714.6 140.0 %all-gather.24.cloned.1.call-done = bf16[6144,2048]{0,1:T(8,128)(2,1)} async-done(((bf16[6144,64]{0,1:T(8,128)(2,1)}), bf16[6144,2048]{0,1:T(8,128)(2,1)}) %all-gather.24.cloned.1.call-update) | async-done | bytes 25165840 | tf_op jit(solution)/shard_map/all_gather | solution.py:92
  854.6 15.1 multiply_convert_fusion.3
  869.7 14.6 multiply_convert_fusion
  884.3 14.4 fusion.107
  898.7 15.8 multiply_reduce_fusion.5
  914.6 4.5 fusion.43
  919.1 8.0 fusion.50
  927.1 10.8 reverse.8
  1059.1 4.8 pad.235
  1076.9 4.9 pad.234
  1085.7 41.4 while.21
  1105.4 4.0 collective-permute-done.1
  1111.3 4.0 collective-permute-done.1
  1117.2 4.0 collective-permute-done.1
  1129.2 4.9 pad.249
  1134.1 4.8 pad.248
  1141.8 10.8 rev.12
  1152.6 11.0 rev.11
  1163.6 4.9 multiply_reduce_fusion
  1189.4 5.1 multiply_reduce_fusion.3
  1202.7 8.6 fusion.59
  1212.5 8.7 fusion.88
  1229.5 8.8 fusion.53
  1239.7 20.5 fusion.114
  1261.2 20.9 fusion.112
  1282.3 20.9 fusion.113
  1304.6 7.4 fusion.109
  1312.1 8.7 fusion.37
  1320.8 40.3 all-reduce.75
  1369.1 97.8 %reduce-scatter.16.cloned.1.call-done = f32[80,256]{1,0:T(8,128)} async-done(((f32[2560,256]{1,0:T(8,128)}), f32[80,256]{1,0:T(8,128)}) %reduce-scatter.16.cloned.1.call-update) | async-done | bytes 81936 | tf_op jit(solution)/shard_map/reduce_scatter | solution.py:251
  1467.0 141.5 %reduce-scatter.18.cloned.1.call-done = f32[80,256]{1,0:T(8,128)} async-done(((f32[2560,256]{1,0:T(8,128)}), f32[80,256]{1,0:T(8,128)}) %reduce-scatter.18.cloned.1.call-update) | async-done | bytes 81936 | tf_op jit(solution)/shard_map/reduce_scatter | solution.py:253
  1608.4 454.1 %reduce-scatter.20.cloned.1.call-done = f32[2560,64]{0,1:T(8,128)} async-done(((f32[2560,2048]{0,1:T(8,128)}), f32[2560,64]{0,1:T(8,128)}) %reduce-scatter.20.cloned.1.call-update) | async-done | bytes 655376 | tf_op jit(solution)/shard_map/reduce_scatter | solution.py:256
  2062.6 452.5 %reduce-scatter.12.cloned.1.call-done = f32[64,2560]{1,0:T(8,128)} async-done(((f32[2048,2560]{1,0:T(8,128)}), f32[64,2560]{1,0:T(8,128)}) %reduce-scatter.12.cloned.1.call-update) | async-done | bytes 655376 | tf_op jit(solution)/shard_map/reduce_scatter | solution.py:247
  2515.0 452.3 %reduce-scatter.14.cloned.1.call-done = f32[64,2560]{1,0:T(8,128)} async-done(((f32[2048,2560]{1,0:T(8,128)}), f32[64,2560]{1,0:T(8,128)}) %reduce-scatter.14.cloned.1.call-update) | async-done | bytes 655376 | tf_op jit(solution)/shard_map/reduce_scatter | solution.py:248
  2967.4 440.5 %reduce-scatter.26.cloned.1.call-done = f32[6144,64]{0,1:T(8,128)} async-done(((f32[6144,2048]{0,1:T(8,128)}), f32[6144,64]{0,1:T(8,128)}) %reduce-scatter.26.cloned.1.call-update) | async-done | bytes 1572880 | tf_op jit(solution)/shard_map/reduce_scatter | solution.py:260
  3407.8 438.6 %reduce-scatter.22.cloned.1.call-done = f32[64,6144]{1,0:T(8,128)} async-done(((f32[2048,6144]{1,0:T(8,128)}), f32[64,6144]{1,0:T(8,128)}) %reduce-scatter.22.cloned.1.call-update) | async-done | bytes 1572880 | tf_op jit(solution)/shard_map/reduce_scatter | solution.py:258
  3846.5 438.5 %reduce-scatter.24.cloned.1.call-done = f32[64,6144]{1,0:T(8,128)} async-done(((f32[2048,6144]{1,0:T(8,128)}), f32[64,6144]{1,0:T(8,128)}) %reduce-scatter.24.cloned.1.call-update) | async-done | bytes 1572880 | tf_op jit(solution)/shard_map/reduce_scatter | solution.py:259
  (553 shorter events, 414.3 us)
Async XLA Ops:
  7.2 152.1 %all-gather.12.cloned.1.call-start = ((), (), s32[]{:S(2)}) async-start(), calls=%async_computation.10 | async-start | bytes 10813440 | tf_op jit(solution)/shard_map/all_gather | solution.py:80
  7.9 169.9 %all-gather.14.cloned.1.call-start = ((), (), s32[]{:S(2)}) async-start(), calls=%async_computation.11 | async-start | bytes 1351680 | tf_op jit(solution)/shard_map/all_gather | solution.py:83
  8.7 202.6 %all-gather.16.cloned.1.call-start = ((), (), s32[]{:S(2)}) async-start(), calls=%async_computation.12 | async-start | bytes 1351680 | tf_op jit(solution)/shard_map/all_gather | solution.py:85
  9.4 460.4 %all-gather.10.cloned.1.call-start = ((), (), s32[]{:S(2)}) async-start(), calls=%async_computation.9 | async-start | bytes 10813440 | tf_op jit(solution)/shard_map/all_gather | solution.py:79
  10.0 43.6 %copy-start.94 = (bf16[80]{0:T(256)(128)(2,1)S(1)}, bf16[80]{0:T(256)(128)(2,1)}, u32[]{:S(2)}) copy-start(bf16[80]{0:T(256)(128)(2,1)} %param.29) | copy-start | bytes 484
  10.0 43.8 %copy-start.95 = (bf16[80]{0:T(256)(128)(2,1)S(1)}, bf16[80]{0:T(256)(128)(2,1)}, u32[]{:S(2)}) copy-start(bf16[80]{0:T(256)(128)(2,1)} %param.31) | copy-start | bytes 484
  10.0 44.0 %copy-start.96 = (bf16[80]{0:T(256)(128)(2,1)S(1)}, bf16[80]{0:T(256)(128)(2,1)}, u32[]{:S(2)}) copy-start(bf16[80]{0:T(256)(128)(2,1)} %param.34) | copy-start | bytes 484
  10.0 44.3 %copy-start.97 = (bf16[80]{0:T(256)(128)(2,1)S(1)}, bf16[80]{0:T(256)(128)(2,1)}, u32[]{:S(2)}) copy-start(bf16[80]{0:T(256)(128)(2,1)} %param.33) | copy-start | bytes 484
  10.0 44.5 %copy-start.98 = (bf16[64]{0:T(256)(128)(2,1)S(1)}, bf16[64]{0:T(256)(128)(2,1)}, u32[]{:S(2)}) copy-start(bf16[64]{0:T(256)(128)(2,1)} %param.25) | copy-start | bytes 388
  10.0 44.8 %copy-start.99 = (bf16[64]{0:T(256)(128)(2,1)S(1)}, bf16[64]{0:T(256)(128)(2,1)}, u32[]{:S(2)}) copy-start(bf16[64]{0:T(256)(128)(2,1)} %param.36) | copy-start | bytes 388
  10.1 470.7 %all-gather.18.cloned.1.call-start = ((), (), s32[]{:S(2)}) async-start(), calls=%async_computation.13 | async-start | bytes 10813440 | tf_op jit(solution)/shard_map/all_gather | solution.py:88
  10.6 87.0 %copy-start.90 = (bf16[4,80]{1,0:T(4,128)(2,1)S(1)}, bf16[4,80]{1,0:T(4,128)(2,1)}, u32[]{:S(2)}) copy-start(bf16[4,80]{1,0:T(4,128)(2,1)} %param.28) | copy-start | bytes 1924
  10.7 147.4 %copy-start = (bf16[1,128,2048]{2,1,0:T(8,128)(2,1)S(1)}, bf16[1,128,2048]{2,1,0:T(8,128)(2,1)}, u32[]{:S(2)}) copy-start(bf16[1,128,2048]{2,1,0:T(8,128)(2,1)} %param.22) | copy-start | bytes 1572868
  10.7 532.4 %all-gather.20.cloned.1.call-start = ((), (), s32[]{:S(2)}) async-start(), calls=%async_computation.14 | async-start | bytes 25952256 | tf_op jit(solution)/shard_map/all_gather | solution.py:90
  11.2 687.6 %all-gather.22.cloned.1.call-start = ((), (), s32[]{:S(2)}) async-start(), calls=%async_computation.15 | async-start | bytes 25952256 | tf_op jit(solution)/shard_map/all_gather | solution.py:91
  12.0 842.6 %all-gather.24.cloned.1.call-start = ((), (), s32[]{:S(2)}) async-start(), calls=%async_computation.16 | async-start | bytes 25952256 | tf_op jit(solution)/shard_map/all_gather | solution.py:92
  12.7 1355.0 %reduce-scatter.28.cloned.1.call-start = ((), (), s32[]{:S(2)}) async-start(), calls=%async_computation.25 | async-start | bytes 1351680
  97.6 67.3 %copy-start.87 = (bf16[2560]{0:T(1024)(128)(2,1)}, bf16[2560]{0:T(1024)(128)(2,1)S(1)}, u32[]{:S(2)}) copy-start(bf16[2560]{0:T(1024)(128)(2,1)S(1)} %get-tuple-element.100) | copy-start | bytes 15364
  164.9 11.2 collective-permute-start.2
  333.2 19.9 copy-start.60
  333.2 19.9 copy-start.61
  333.2 19.9 copy-start.62
  333.2 19.9 copy-start.63
  333.2 20.1 copy-start.42
  333.2 20.1 copy-start.43
  343.2 11.6 copy-start.44
  343.2 11.6 copy-start.45
  422.5 47.2 %copy-start.65 = (f32[128]{0:T(128)S(1)}, f32[128]{0:T(128)}, u32[]{:S(2)}) copy-start(f32[128]{0:T(128)} %copy-done.64) | copy-start | bytes 1540
  429.4 4.1 collective-permute-start
  433.5 6.1 collective-permute-start
  439.6 6.1 collective-permute-start
  445.7 6.1 collective-permute-start
  451.8 5.9 collective-permute-start
  457.7 5.9 collective-permute-start
  463.6 5.9 collective-permute-start
  556.5 298.0 %copy-start.89 = (f32[128]{0:T(128)S(1)}, f32[128]{0:T(128)}, u32[]{:S(2)}) copy-start(f32[128]{0:T(128)} %broadcast_multiply_fusion.5) | copy-start | bytes 1540
  898.7 15.8 copy-start.93
  1004.7 11.6 copy-start.76
  1004.7 11.6 copy-start.77
  1004.7 11.7 copy-start.58
  1004.7 11.7 copy-start.74
  1004.7 11.7 copy-start.75
  1006.6 9.9 copy-start.59
  1006.6 11.2 copy-start.46
  1006.6 11.2 copy-start.47
  1085.7 5.9 collective-permute-start.1
  1091.7 5.9 collective-permute-start.1
  1097.6 5.9 collective-permute-start.1
  1103.5 5.9 collective-permute-start.1
  1109.4 5.9 collective-permute-start.1
  1115.3 5.9 collective-permute-start.1
  1121.2 5.9 collective-permute-start.1
  1196.2 270.7 %reduce-scatter.16.cloned.1.call-start = ((), (), s32[]{:S(2)}) async-start(), calls=%async_computation.19 | async-start | bytes 2703360 | tf_op jit(solution)/shard_map/reduce_scatter | solution.py:251
  1198.3 410.2 %reduce-scatter.18.cloned.1.call-start = ((), (), s32[]{:S(2)}) async-start(), calls=%async_computation.20 | async-start | bytes 2703360 | tf_op jit(solution)/shard_map/reduce_scatter | solution.py:253
  1201.3 861.2 %reduce-scatter.20.cloned.1.call-start = ((), (), s32[]{:S(2)}) async-start(), calls=%async_computation.21 | async-start | bytes 21626880 | tf_op jit(solution)/shard_map/reduce_scatter | solution.py:256
  1211.4 1303.6 %reduce-scatter.12.cloned.1.call-start = ((), (), s32[]{:S(2)}) async-start(), calls=%async_computation.17 | async-start | bytes 21626880 | tf_op jit(solution)/shard_map/reduce_scatter | solution.py:247
  1221.3 1746.1 %reduce-scatter.14.cloned.1.call-start = ((), (), s32[]{:S(2)}) async-start(), calls=%async_computation.18 | async-start | bytes 21626880 | tf_op jit(solution)/shard_map/reduce_scatter | solution.py:248
  1223.3 6.2 collective-permute-start.3
  1238.3 2169.5 %reduce-scatter.26.cloned.1.call-start = ((), (), s32[]{:S(2)}) async-start(), calls=%async_computation.24 | async-start | bytes 51904512 | tf_op jit(solution)/shard_map/reduce_scatter | solution.py:260
  1260.2 2586.2 %reduce-scatter.22.cloned.1.call-start = ((), (), s32[]{:S(2)}) async-start(), calls=%async_computation.22 | async-start | bytes 51904512 | tf_op jit(solution)/shard_map/reduce_scatter | solution.py:258
  1282.1 3002.8 %reduce-scatter.24.cloned.1.call-start = ((), (), s32[]{:S(2)}) async-start(), calls=%async_computation.23 | async-start | bytes 51904512 | tf_op jit(solution)/shard_map/reduce_scatter | solution.py:259
  1312.0 8.7 copy-start.67
  1312.1 53.2 %copy-start.92 = (f32[128]{0:T(128)S(1)}, f32[128]{0:T(128)}, u32[]{:S(2)}) copy-start(f32[128]{0:T(128)} %copy-done.91) | copy-start | bytes 1540
  1312.1 53.2 %copy-start.12 = (f32[128,2048]{1,0:T(8,128)S(1)}, f32[128,2048]{1,0:T(8,128)}, u32[]{:S(2)}) copy-start(f32[128,2048]{1,0:T(8,128)} %copy-done.10) | copy-start | bytes 3145732
  (70 other events, 249.7 us)
Sparse Core Ops, SparseCore 0:
  10.9 88.7 all-gather.11
  102.5 52.5 all-gather.13
  157.9 53.2 all-gather.15
  213.9 86.3 all-gather.9
  303.0 85.2 all-gather.17
  391.1 151.9 all-gather.19
  546.0 152.8 all-gather.21
  701.7 152.8 all-gather.23
  1196.3 129.2 reduce-scatter.27
  1328.4 138.4 reduce-scatter.15
  1469.9 138.4 reduce-scatter.17
  1611.3 451.2 reduce-scatter.19
  2065.6 449.4 reduce-scatter.11
  2517.9 449.4 reduce-scatter.13
  2975.3 432.4 reduce-scatter.25
  3415.8 430.5 reduce-scatter.21
  3854.4 430.4 reduce-scatter.23
where the time goes:
time: 4310 us; the launch traced here: 4290 us
  waiting for transfers between devices  3320 us (77%)
  local copies, waits for them, and re-layouts  348 us (8%)
  matrix products  243 us (6%)
  blocking collectives  183 us (4%)
  other arithmetic  119 us (3%)
  starting transfers between devices  61.6 us (1%)
    reduce_scatter x1, waiting for transfers between devices, on_device(): lax.psum_scatter(grad_proj_out, ('seq', 'dp'), scatter_dimension=1, tiled...  454 us
    reduce_scatter x1, waiting for transfers between devices, on_device(): lax.psum_scatter(grad_proj_gelu, ('seq', 'dp'), scatter_dimension=0, tile...  452 us
    reduce_scatter x1, waiting for transfers between devices, on_device(): lax.psum_scatter(grad_proj_rec, ('seq', 'dp'), scatter_dimension=0, tiled...  452 us
    reduce_scatter x1, waiting for transfers between devices, on_device(): lax.psum_scatter(grad_mlp_down, ('seq', 'dp'), scatter_dimension=1, tiled...  440 us
    reduce_scatter x1, waiting for transfers between devices, on_device(): lax.psum_scatter(grad_mlp_gate, ('seq', 'dp'), scatter_dimension=0, tiled...  439 us
    reduce_scatter x1, waiting for transfers between devices, on_device(): lax.psum_scatter(grad_mlp_up, ('seq', 'dp'), scatter_dimension=0, tiled=T...  438 us
    all_gather x1, waiting for transfers between devices, on_device(): lax.all_gather(mlp_up, ('seq', 'dp'), axis=0, tiled=True)  142 us
    reduce_scatter x1, waiting for transfers between devices, on_device(): lax.psum_scatter(grad_gate_inp_w, ('seq', 'dp'), scatter_dimension=0, til...  141 us
  transfers between devices with their start and end apart: 33, of which 28 were waited for; matrix products, arithmetic and copies ran while one was open for 9% of the time, Pallas kernels for 0%

commit v1 on v0

v1 whole, which is shorter than its diff:
```python
import functools
import itertools

import jax
import jax.numpy as jnp
from jax import lax
from jax.experimental import pallas as pl
from jax.experimental.pallas import tpu as pltpu
from jax.sharding import PartitionSpec as P

NB = 10
BW = 256
CONV = 4
LANES = 128

norm_eps = 1e-06
gate_power = 8.0
floor_square = 0.0001

fp32 = jnp.float32
half = jnp.bfloat16


def flip(index, mask):
    return index + mask - 2 * mask * ((index // mask) % 2)


def bit_values(bits):
    return [(lax.axis_index(axis) // mask) % 2 for axis, mask, _ in bits]


def slot_number(bits, vals, flipped):
    total = 0
    for place, (_, _, weight) in enumerate(bits):
        total = total + weight * (1 - vals[place] if place in flipped else vals[place])
    return total


def partner(bit):
    axis, mask, _ = bit
    return {axis: flip(lax.axis_index(axis), mask)}


def greet(bits):
    barrier = pltpu.get_barrier_semaphore()
    for bit in bits:
        pl.semaphore_signal(
            barrier, inc=1, device_id=partner(bit), device_id_type=pl.DeviceIdType.MESH
        )
    pl.semaphore_wait(barrier, len(bits))


def masks_of(size):
    return [2**place for place in reversed(range(size.bit_length() - 1))]


def plane_bits():
    return tuple(("seq", mask, mask) for mask in masks_of(lax.axis_size("seq")))


def pair_count():
    return 2 if lax.axis_size("dp") > 1 and 2 * lax.axis_size("seq") <= 16 else 1


def cube_bits():
    pair = (("dp", 1, lax.axis_size("seq")),) if pair_count() == 2 else ()
    return (*pair, *plane_bits())


def world_bits():
    dps = lax.axis_size("dp")
    return tuple(("dp", mask, mask) for mask in masks_of(dps)) + tuple(
        ("seq", mask, mask * dps) for mask in masks_of(lax.axis_size("seq"))
    )


def subsets(items):
    for size in range(len(items) + 1):
        yield from itertools.combinations(items, size)


def splits(width, count):
    tiles = width // LANES
    if tiles * LANES != width or tiles < count:
        return [(0, width)]
    cuts = [tiles * i // count * LANES for i in range(count + 1)]
    return [(cuts[i], cuts[i + 1] - cuts[i]) for i in range(count)]


def rotations(bits, width):
    slow, last = list(range(len(bits) - 1)), [len(bits) - 1]
    pieces = splits(width, len(slow))
    return [
        (first, size, tuple(slow[turn:] + slow[:turn] + last))
        for turn, (first, size) in enumerate(pieces)
    ]


class Gathering:
    def __init__(self, bits, width, x_ref, o_ref, sems):
        self.bits, self.x_ref, self.o_ref = bits, x_ref, o_ref
        self.send_sems, self.recv_sems, self.local_sem = sems
        self.vals = bit_values(bits)
        self.parts = rotations(bits, width)
        self.numbers = {}
        for which in range(len(self.parts)):
            for stage in range(len(bits)):
                for held in subsets(range(stage)):
                    self.numbers[which, stage, held] = len(self.numbers)

    @staticmethod
    def semaphores(bits, width):
        copies = len(rotations(bits, width)) * (2 ** len(bits) - 1)
        return [
            pltpu.SemaphoreType.DMA((copies,)),
            pltpu.SemaphoreType.DMA((copies,)),
            pltpu.SemaphoreType.DMA,
        ]

    def own(self):
        slot = slot_number(self.bits, self.vals, ())
        return pltpu.make_async_copy(self.x_ref, self.o_ref.at[slot], self.local_sem)

    def transfer(self, which, stage, held):
        first, width, order = self.parts[which]
        cols = pl.ds(first, width)
        slot = slot_number(self.bits, self.vals, [order[place] for place in held])
        dst = self.o_ref.at[slot, :, cols]
        number = self.numbers[which, stage, held]
        return pltpu.make_async_remote_copy(
            src_ref=dst if held else self.x_ref.at[:, cols],
            dst_ref=dst,
            send_sem=self.send_sems.at[number],
            recv_sem=self.recv_sems.at[number],
            device_id=partner(self.bits[order[stage]]),
            device_id_type=pl.DeviceIdType.MESH,
        )

    def begin(self):
        self.own().start()
        for stage in range(len(self.bits)):
            for which in range(len(self.parts)):
                self.transfer(which, stage, ()).start()

    def level(self, size):
        depth = len(self.bits)
        for held in itertools.combinations(range(depth), size):
            for which in range(len(self.parts)):
                self.transfer(which, held[-1], held[:-1]).wait_recv()
                for stage in range(held[-1] + 1, depth):
                    self.transfer(which, stage, held).start()

    def finish(self):
        for key in self.numbers:
            self.transfer(*key).wait_send()
        self.own().wait()


class Scattering:
    def __init__(self, bits, x_ref, o_ref, scratch):
        self.bits, self.x_ref, self.o_ref = bits, x_ref, o_ref
        self.held, self.outgoing, self.incoming, self.load, self.send, self.recv = scratch
        self.rows, width = o_ref.shape
        self.chunk = 32 if self.rows % 32 == 0 else 16
        self.parts = [(at, size, order[::-1]) for at, size, order in rotations(bits, width)]
        self.vals = bit_values(bits)
        self.depth = len(bits)
        first_bit = self.parts[0][2][0]
        self.blocks = sorted(subsets(range(self.depth)), key=lambda s: (first_bit not in s, -len(s)))
        self.slots, self.numbers = {}, {}
        for stage in range(self.depth):
            for rest in subsets(range(stage + 1, self.depth)):
                self.slots[stage, rest] = len(self.slots)
        for which in range(len(self.parts)):
            for key in self.slots:
                self.numbers[(which, *key)] = len(self.numbers)
        self.loaded = set()

    @staticmethod
    def scratch(bits, value, wire):
        count, rows, width = value.shape
        copies = len(rotations(bits, width)) * (count - 1)
        return [
            pltpu.VMEM((count, rows, width), value.dtype),
            pltpu.VMEM((count - 1, rows, width), wire),
            pltpu.VMEM((count - 1, rows, width), wire),
            pltpu.SemaphoreType.DMA((count,)),
            pltpu.SemaphoreType.DMA((copies,)),
            pltpu.SemaphoreType.DMA((copies,)),
        ]

    def loading(self, members):
        key = sum(2**place for place in members)
        slot = slot_number(self.bits, self.vals, members)
        return pltpu.make_async_copy(self.x_ref.at[slot], self.held.at[key], self.load.at[key])

    def begin(self):
        for members in self.blocks:
            self.loading(members).start()

    def ready(self, members):
        key = sum(2**place for place in members)
        if key not in self.loaded:
            self.loaded.add(key)
            self.loading(members).wait()
        return key

    def transfer(self, which, stage, rest):
        first, width, order = self.parts[which]
        place = self.slots[stage, rest]
        number = self.numbers[which, stage, rest]
        return pltpu.make_async_remote_copy(
            src_ref=self.outgoing.at[place, :, pl.ds(first, width)],
            dst_ref=self.incoming.at[place, :, pl.ds(first, width)],
            send_sem=self.send.at[number],
            recv_sem=self.recv.at[number],
            device_id=partner(self.bits[order[stage]]),
            device_id_type=pl.DeviceIdType.MESH,
        )

    def add_up(self, which, key, arrived, store):
        first, width, _ = self.parts[which]
        cols = pl.ds(first, width)

        def body(step, carry):
            lines = pl.ds(pl.multiple_of(step * self.chunk, self.chunk), self.chunk)
            total = self.held[key, lines, cols].astype(fp32)
            for place in arrived:
                total = total + self.incoming[place, lines, cols].astype(fp32)
            store(lines, cols, total)
            return carry

        lax.fori_loop(0, self.rows // self.chunk, body, 0)

    def stage(self, stage):
        for rest in sorted(subsets(range(stage + 1, self.depth)), key=lambda s: (-len(s), s)):
            for which, (_, _, order) in enumerate(self.parts):
                going = (stage, *rest)
                key = self.ready([order[place] for place in going])
                for earlier in range(stage):
                    self.transfer(which, earlier, going).wait_recv()
                place = self.slots[stage, rest]

                def keep(lines, cols, total, place=place):
                    self.outgoing[place, lines, cols] = total.astype(self.outgoing.dtype)

                arrived = [self.slots[earlier, going] for earlier in range(stage)]
                self.add_up(which, key, arrived, keep)
                self.transfer(which, stage, rest).start()

    def finish(self):
        def keep(lines, cols, total):
            self.o_ref[lines, cols] = total

        key = self.ready(())
        for which in range(len(self.parts)):
            for stage in range(self.depth):
                self.transfer(which, stage, ()).wait_recv()
            self.add_up(which, key, [self.slots[stage, ()] for stage in range(self.depth)], keep)

    def close(self):
        for members in self.blocks:
            self.ready(members)
        for key in self.numbers:
            self.transfer(*key).wait_send()


def gather(value, bits, number):
    rows, width = value.shape

    def kernel(x_ref, o_ref, *sems):
        work = Gathering(bits, width, x_ref, o_ref, sems)
        greet(bits)
        work.begin()
        for size in range(1, len(bits) + 1):
            work.level(size)
        work.finish()

    return pl.pallas_call(
        kernel,
        out_shape=jax.ShapeDtypeStruct((2 ** len(bits), rows, width), value.dtype),
        in_specs=[pl.BlockSpec(memory_space=pltpu.VMEM)],
        out_specs=pl.BlockSpec(memory_space=pl.ANY),
        scratch_shapes=Gathering.semaphores(bits, width),
        compiler_params=pltpu.CompilerParams(collective_id=number, has_side_effects=True),
        name=f"gather_{number}",
    )(value)


def scatter_sum(value, bits, number, wire=half):
    _, rows, width = value.shape

    def kernel(x_ref, o_ref, *scratch):
        work = Scattering(bits, x_ref, o_ref, scratch)
        work.begin()
        greet(bits)
        for stage in range(len(bits)):
            work.stage(stage)
        work.finish()
        work.close()

    return pl.pallas_call(
        kernel,
        out_shape=jax.ShapeDtypeStruct((rows, width), fp32),
        in_specs=[pl.BlockSpec(memory_space=pl.ANY)],
        out_specs=pl.BlockSpec(memory_space=pltpu.VMEM),
        scratch_shapes=Scattering.scratch(bits, value, wire),
        compiler_params=pltpu.CompilerParams(
            collective_id=number, has_side_effects=True, vmem_limit_bytes=60 * 2**20
        ),
        name=f"scatter_{number}",
    )(value)


def greet_all(axes):
    barrier = pltpu.get_barrier_semaphore()
    total = 0
    for axis in axes:
        count = lax.axis_size(axis)
        for step in range(1, count):
            pl.semaphore_signal(
                barrier,
                inc=1,
                device_id={axis: lax.rem(lax.axis_index(axis) + step, count)},
                device_id_type=pl.DeviceIdType.MESH,
            )
        total += count - 1
    pl.semaphore_wait(barrier, total)


def remote(src, dst, send_sem, recv_sem, device):
    return pltpu.make_async_remote_copy(
        src_ref=src,
        dst_ref=dst,
        send_sem=send_sem,
        recv_sem=recv_sem,
        device_id=device,
        device_id_type=pl.DeviceIdType.MESH,
    )


class Exchange:
    def __init__(self, pay, place, sems):
        self.pay, self.place = pay, place
        self.send, self.recv, self.local = sems
        self.me, self.count = lax.axis_index("seq"), lax.axis_size("seq")

    @staticmethod
    def semaphores(count):
        return [
            pltpu.SemaphoreType.DMA((count,)),
            pltpu.SemaphoreType.DMA((count,)),
            pltpu.SemaphoreType.DMA,
        ]

    def own(self):
        return pltpu.make_async_copy(self.pay.at[self.me], self.place(self.me), self.local)

    def going(self, step):
        to = lax.rem(self.me + step, self.count)
        return remote(
            self.pay.at[to],
            self.place(self.me),
            self.send.at[step],
            self.recv.at[step],
            {"seq": to},
        )

    def source(self, step):
        return lax.rem(self.me - step + self.count, self.count)

    def arriving(self, step):
        block = self.place(self.source(step))
        return remote(block, block, self.send.at[step], self.recv.at[step], {"seq": self.me})


def opening(pay_in, pay_out, pay_mlp, package, tokens, number):
    seqs, dps = lax.axis_size("seq"), lax.axis_size("dp")
    plane, world = plane_bits(), world_bits()
    pays = [pay_in, pay_out]
    rows = pay_in.shape[1]
    relays = 2 * len(pays)
    x_sems = len(Exchange.semaphores(seqs))

    def kernel(*refs):
        pay_refs, refs = refs[:2], refs[2:]
        mlp_ref, package_ref, tokens_ref, refs = refs[0], refs[1], refs[2], refs[3:]
        full_refs, refs = refs[:2], refs[2:]
        mlp_all, shared_all, tokens_all, refs = refs[0], refs[1], refs[2], refs[3:]
        exchange_sems = [refs[x_sems * i : x_sems * (i + 1)] for i in range(3)]
        refs = refs[3 * x_sems :]
        line_send, line_recv, refs = refs[0], refs[1], refs[2:]
        me_d = lax.axis_index("dp")

        def slot(full):
            return lambda source: full.at[source, me_d]

        moves = [Exchange(pay, slot(full), sems) for pay, full, sems in zip(pay_refs, full_refs, exchange_sems)]
        mlp_move = Exchange(mlp_ref, lambda source: mlp_all.at[source], exchange_sems[2])
        shared = Gathering(world, package.shape[1], package_ref, shared_all, refs[:3])
        toks = Gathering(plane, tokens.shape[1], tokens_ref, tokens_all, refs[3:6])

        greet_all(("seq", "dp"))
        for move in moves:
            move.own().start()
        for step in range(1, seqs):
            for move in moves:
                move.going(step).start()
        shared.begin()
        toks.begin()
        mlp_move.own().start()
        for step in range(1, seqs):
            mlp_move.going(step).start()

        def line_copy(way, which, hop, step):
            sign = 1 if way == 0 else -1
            origin = jnp.clip(me_d - sign * hop, 0, dps - 1)
            block = full_refs[which].at[moves[which].source(step), origin]
            return remote(
                block,
                block,
                line_send.at[2 * which + way, hop, step],
                line_recv.at[2 * which + way, hop, step],
                {"dp": jnp.clip(me_d + sign, 0, dps - 1)},
            )

        def has_next(way):
            return me_d < dps - 1 if way == 0 else me_d > 0

        def has_origin(way, hop):
            return me_d >= hop if way == 0 else me_d < dps - hop

        def pass_on(hop, step):
            for which in range(2):
                for way in range(2):

                    @pl.when(has_next(way) & has_origin(way, hop))
                    def _():
                        line_copy(way, which, hop, step).start()

        def incoming_line(way, which, hop, step):
            sign = 1 if way == 0 else -1
            origin = jnp.clip(me_d - sign * hop, 0, dps - 1)
            block = full_refs[which].at[moves[which].source(step), origin]
            return remote(
                block,
                block,
                line_send.at[2 * which + way, hop - 1, step],
                line_recv.at[2 * which + way, hop - 1, step],
                {"dp": jnp.clip(me_d + sign, 0, dps - 1)},
            )

        for which in range(2):
            moves[which].own().wait()
        pass_on(0, 0)

        def first_round(step, carry):
            for move in moves:
                move.arriving(step).wait_recv()
            pass_on(0, step)
            return carry

        lax.fori_loop(1, seqs, first_round, 0)
        world_levels, plane_levels = len(world), len(plane)
        for size in range(1, world_levels + 1):
            shared.level(size)
        for hop in range(1, dps):

            def round_of(step, carry, hop=hop):
                for which in range(2):
                    for way in range(2):

                        @pl.when(has_origin(way, hop))
                        def _():
                            incoming_line(way, which, hop, step).wait_recv()

                if hop < dps - 1:
                    pass_on(hop, step)
                return carry

            lax.fori_loop(0, seqs, round_of, 0)
            if hop == 1:
                for size in range(1, plane_levels + 1):
                    toks.level(size)

        def last_round(step, carry):
            for move in [*moves, mlp_move]:
                move.going(step).wait_send()
            mlp_move.arriving(step).wait_recv()
            return carry

        lax.fori_loop(1, seqs, last_round, 0)
        mlp_move.own().wait()

        def close_round(step, carry):
            for hop in range(dps - 1):
                for which in range(2):
                    for way in range(2):

                        @pl.when(has_next(way) & has_origin(way, hop))
                        def _():
                            line_copy(way, which, hop, step).wait_send()

            return carry

        lax.fori_loop(0, seqs, close_round, 0)
        shared.finish()
        toks.finish()

    vmem, anywhere = pl.BlockSpec(memory_space=pltpu.VMEM), pl.BlockSpec(memory_space=pl.ANY)
    return pl.pallas_call(
        kernel,
        out_shape=[
            *(jax.ShapeDtypeStruct((seqs, dps, rows, pay.shape[2]), half) for pay in pays),
            jax.ShapeDtypeStruct(pay_mlp.shape, half),
            jax.ShapeDtypeStruct((seqs * dps, *package.shape), half),
            jax.ShapeDtypeStruct((seqs, *tokens.shape), half),
        ],
        in_specs=[vmem] * 5,
        out_specs=[anywhere] * 5,
        scratch_shapes=[
            *(Exchange.semaphores(seqs) * 3),
            pltpu.SemaphoreType.DMA((relays, max(dps - 1, 1), seqs)),
            pltpu.SemaphoreType.DMA((relays, max(dps - 1, 1), seqs)),
            *Gathering.semaphores(world, package.shape[1]),
            *Gathering.semaphores(plane, tokens.shape[1]),
        ],
        compiler_params=pltpu.CompilerParams(
            collective_id=number, has_side_effects=True, vmem_limit_bytes=40 * 2**20
        ),
        name="opening",
    )(pay_in, pay_out, pay_mlp, package, tokens)


def closing(in_part, grad_in, grad_out, mlp, mats, small, number):
    seqs, dps = lax.axis_size("seq"), lax.axis_size("dp")
    plane, world = plane_bits(), world_bits()
    grads = [grad_in, grad_out]
    rows = grad_in.shape[2]
    widths = [grad.shape[3] for grad in grads]
    links = max(dps - 1, 1)
    x_sems = len(Exchange.semaphores(seqs))
    jobs = [(plane, in_part, half), (world, small, fp32), (world, mats, half)]
    s_count = len(Scattering.scratch(plane, in_part, half))

    def kernel(*refs):
        part_ref, grad_refs, mlp_ref, mats_ref, small_ref = refs[0], refs[1:3], refs[3], refs[4], refs[5]
        part_out, back_refs, mlp_out, mats_out, small_out = refs[6], refs[7:9], refs[9], refs[10], refs[11]
        refs = refs[12:]
        works = []
        for (bits, _, _), x_ref, o_ref in zip(
            jobs, (part_ref, small_ref, mats_ref), (part_out, small_out, mats_out)
        ):
            works.append(Scattering(bits, x_ref, o_ref, refs[:s_count]))
            refs = refs[s_count:]
        held, refs = refs[:2], refs[2:]
        outgoing, incoming, totals, refs = refs[:2], refs[2:4], refs[4:6], refs[6:]
        load, line_send, line_recv, refs = refs[0], refs[1], refs[2], refs[3:]
        exchange_sems = [refs[x_sems * i : x_sems * (i + 1)] for i in range(3)]
        me_s, me_d = lax.axis_index("seq"), lax.axis_index("dp")
        moves = [
            Exchange(total, lambda source, back=back: back.at[source], sems)
            for total, back, sems in zip(totals, back_refs, exchange_sems)
        ]
        mlp_move = Exchange(mlp_ref, lambda source: mlp_out.at[source], exchange_sems[2])

        def loading(which, chunk):
            return pltpu.make_async_copy(
                grad_refs[which].at[chunk], held[which].at[chunk], load.at[which, chunk]
            )

        def chunk_of(step):
            return lax.rem(me_s + step, seqs)

        for step in range(seqs):
            for which in range(2):
                loading(which, chunk_of(step)).start()
        for work in works:
            work.begin()
        greet_all(("seq", "dp"))

        def ahead(way):
            return me_d < dps - 1 if way == 0 else me_d > 0

        def behind(way):
            return me_d > 0 if way == 0 else me_d < dps - 1

        def target(way, hop):
            sign = 1 if way == 0 else -1
            return jnp.clip(me_d + sign * hop, 0, dps - 1)

        def has_target(way, hop):
            return me_d < dps - hop if way == 0 else me_d >= hop

        def line_copy(way, which, hop, chunk):
            return remote(
                outgoing[which].at[way, hop % 2, chunk],
                incoming[which].at[way, hop - 1, chunk],
                line_send.at[2 * which + way, hop - 1, chunk],
                line_recv.at[2 * which + way, hop - 1, chunk],
                {"dp": target(way, 1)},
            )

        def combine(store, terms):
            def body(step, carry):
                lines = pl.ds(pl.multiple_of(step * 16, 16), 16)
                total = terms[0](lines)
                for term in terms[1:]:
                    total = total + term(lines)
                store(lines, total)
                return carry

            lax.fori_loop(0, rows // 16, body, 0)

        def own_term(which, chunk, block):
            return lambda lines: held[which][chunk, block, lines, :]

        def far_term(which, way, hop, chunk):
            return lambda lines: incoming[which][way, hop - 1, chunk, lines, :].astype(fp32)

        def line_round(hop, first):
            def body(step, carry):
                chunk = chunk_of(step)
                for which in range(2):
                    if first:
                        loading(which, chunk).wait()
                    for way in range(2):
                        if hop + 2 < dps:

                            @pl.when(has_target(way, hop + 2))
                            def _():
                                line_copy(way, which, hop + 2, chunk).wait_send()

                        def send(far, which=which, way=way):
                            def keep(lines, total):
                                outgoing[which][way, hop % 2, chunk, lines, :] = total.astype(half)

                            terms = [own_term(which, chunk, target(way, hop))]
                            if far:
                                line_copy(way, which, hop + 1, chunk).wait_recv()
                                terms.append(far_term(which, way, hop + 1, chunk))
                            combine(keep, terms)
                            line_copy(way, which, hop, chunk).start()

                        if hop == dps - 1:

                            @pl.when(has_target(way, hop))
                            def _():
                                send(False)

                        else:

                            @pl.when(has_target(way, hop) & behind(way))
                            def _():
                                send(True)

                            @pl.when(has_target(way, hop) & jnp.logical_not(behind(way)))
                            def _():
                                send(False)

                return carry

            lax.fori_loop(0, seqs, body, 0)

        def line_total(step, carry):
            chunk = chunk_of(step)
            for which in range(2):
                if dps == 1:
                    loading(which, chunk).wait()

                def keep(lines, total, which=which):
                    totals[which][chunk, lines, :] = total.astype(half)

                mine = own_term(which, chunk, me_d)
                for low, high in ((True, True), (True, False), (False, True), (False, False)):
                    test_low = behind(0) if low else jnp.logical_not(behind(0))
                    test_high = behind(1) if high else jnp.logical_not(behind(1))

                    @pl.when(test_low & test_high)
                    def _():
                        terms = [mine]
                        for way in [way for way, far in ((0, low), (1, high)) if far and dps > 1]:
                            line_copy(way, which, 1, chunk).wait_recv()
                            terms.append(far_term(which, way, 1, chunk))
                        combine(keep, terms)

                @pl.when(step > 0)
                def _():
                    moves[which].going(step).start()

                @pl.when(step == 0)
                def _():
                    moves[which].own().start()

            return carry

        depth = max(len(world), dps - 1)
        for turn in range(depth):
            if turn < dps - 1:
                line_round(dps - 1 - turn, turn == 0)
            if turn == 0:
                mlp_move.own().start()
                for step in range(1, seqs):
                    mlp_move.going(step).start()
            if turn == max(dps - 2, 0):
                lax.fori_loop(0, seqs, line_total, 0)
            for work in works:
                if turn < work.depth:
                    work.stage(turn)
        for work in works:
            work.finish()

        def last_round(step, carry):
            for move in [*moves, mlp_move]:
                move.arriving(step).wait_recv()
                move.going(step).wait_send()
            return carry

        lax.fori_loop(1, seqs, last_round, 0)
        for move in [*moves, mlp_move]:
            move.own().wait()

        def close_round(step, carry):
            for hop in range(1, min(dps, 3)):
                for which in range(2):
                    for way in range(2):

                        @pl.when(has_target(way, hop))
                        def _():
                            line_copy(way, which, hop, step).wait_send()

            return carry

        lax.fori_loop(0, seqs, close_round, 0)
        for work in works:
            work.close()

    vmem, anywhere = pl.BlockSpec(memory_space=pltpu.VMEM), pl.BlockSpec(memory_space=pl.ANY)
    shape = jax.ShapeDtypeStruct
    return pl.pallas_call(
        kernel,
        out_shape=[
            shape(in_part.shape[1:], fp32),
            *(shape((seqs, rows, width), half) for width in widths),
            shape(mlp.shape, half),
            shape(mats.shape[1:], fp32),
            shape(small.shape[1:], fp32),
        ],
        in_specs=[anywhere, anywhere, anywhere, vmem, anywhere, anywhere],
        out_specs=[vmem, anywhere, anywhere, anywhere, vmem, vmem],
        scratch_shapes=[
            *itertools.chain.from_iterable(
                Scattering.scratch(bits, value, wire) for bits, value, wire in jobs
            ),
            *(pltpu.VMEM((seqs, dps, rows, width), fp32) for width in widths),
            *(pltpu.VMEM((2, 2, seqs, rows, width), half) for width in widths),
            *(pltpu.VMEM((2, links, seqs, rows, width), half) for width in widths),
            *(pltpu.VMEM((seqs, rows, width), half) for width in widths),
            pltpu.SemaphoreType.DMA((2, seqs)),
            pltpu.SemaphoreType.DMA((4, links, seqs)),
            pltpu.SemaphoreType.DMA((4, links, seqs)),
            *(Exchange.semaphores(seqs) * 3),
        ],
        compiler_params=pltpu.CompilerParams(
            collective_id=number, has_side_effects=True, vmem_limit_bytes=63 * 2**20
        ),
        name="closing",
    )(in_part, grad_in, grad_out, mlp, mats, small)


STRETCHES = 8


def forward_scan_kernel(decay_ref, drive_ref, state_ref):
    steps, width = decay_ref.shape
    span = steps // STRETCHES

    def lines(step):
        return pl.ds(step, STRETCHES, stride=span)

    def measure(step, carry):
        state, product = carry
        decay = decay_ref[lines(step), :]
        return decay * state + drive_ref[lines(step), :], product * decay

    zero = jnp.zeros((STRETCHES, width), fp32)
    state, product = lax.fori_loop(0, span, measure, (zero, zero + 1.0), unroll=4)
    row = jnp.zeros((1, width), fp32)
    rows = []
    for place in range(STRETCHES):
        rows.append(row)
        row = product[place : place + 1] * row + state[place : place + 1]
    enter = jnp.concatenate(rows, axis=0)

    def run(step, carry):
        carry = decay_ref[lines(step), :] * carry + drive_ref[lines(step), :]
        state_ref[lines(step), :] = carry
        return carry

    lax.fori_loop(0, span, run, enter, unroll=4)


def backward_scan_kernel(decay_ref, grad_ref, adjoint_ref):
    steps, width = decay_ref.shape
    span = steps // STRETCHES

    def lines(step):
        return pl.ds(span - 1 - step, STRETCHES, stride=span)

    def measure(step, carry):
        flow, product = carry
        decay = decay_ref[lines(step), :]
        return decay * (grad_ref[lines(step), :] + flow), product * decay

    zero = jnp.zeros((STRETCHES, width), fp32)
    flow, product = lax.fori_loop(0, span, measure, (zero, zero + 1.0), unroll=4)
    row = jnp.zeros((1, width), fp32)
    rows = []
    for place in reversed(range(STRETCHES)):
        rows.append(row)
        row = product[place : place + 1] * row + flow[place : place + 1]
    enter = jnp.concatenate(rows[::-1], axis=0)

    def run(step, carry):
        adjoint = grad_ref[lines(step), :] + carry
        adjoint_ref[lines(step), :] = adjoint
        return decay_ref[lines(step), :] * adjoint

    lax.fori_loop(0, span, run, enter, unroll=4)


def time_scan(kernel, decays, other):
    steps, width = decays.shape
    padded = -(-width // LANES) * LANES
    wide = ((0, 0), (0, padded - width))
    block = pl.BlockSpec((steps, LANES), lambda place: (0, place))
    out = pl.pallas_call(
        kernel,
        grid=(padded // LANES,),
        out_shape=jax.ShapeDtypeStruct((steps, padded), fp32),
        in_specs=[block, block],
        out_specs=block,
        name=kernel.__name__,
    )(jnp.pad(decays, wide), jnp.pad(other, wide))
    return out[:, :width]


def across(value, axis, mask):
    return lax.ppermute(value, axis, [(i, i ^ mask) for i in range(lax.axis_size(axis))])


def far_masks(axis):
    mask, masks = pair_count(), []
    while mask < lax.axis_size(axis):
        masks.append(mask)
        mask *= 2
    return masks


def place_at(axis, at):
    where, mask = lax.axis_index(axis), 1
    while mask <= at:
        where = flip(where, mask) if at & mask else where
        mask *= 2
    return where


def cube_gather(value, axis):
    low = lax.axis_index(axis) % pair_count()
    mine = lax.dynamic_index_in_dim(value, low, axis=1, keepdims=False)
    pieces = [(0, mine)]
    if pair_count() == 2:
        other = lax.dynamic_index_in_dim(value, 1 - low, axis=1, keepdims=False)
        pieces.append((1, across(other, axis, 1)))
    for mask in far_masks(axis):
        pieces += [(at ^ mask, across(piece, axis, mask)) for at, piece in pieces]
    sources, rows, width = mine.shape
    out = jnp.zeros((sources, lax.axis_size(axis), rows, width), value.dtype)
    for at, piece in pieces:
        out = lax.dynamic_update_slice(out, piece[:, None], (0, place_at(axis, at), 0, 0))
    return out


def cube_scatter(values, axis):
    def block(at):
        where = place_at(axis, at)
        return jnp.concatenate(
            [lax.dynamic_index_in_dim(v, where, axis=1, keepdims=False) for v in values], axis=-1
        )

    held = {at: block(at) for at in range(lax.axis_size(axis))}
    for mask in reversed(far_masks(axis)):
        kept, before = sorted((at for at in held if not at & mask), reverse=True), None
        sums = {}
        for at in kept:
            going = held[at ^ mask].astype(half)
            if before is not None:
                going, before = lax.optimization_barrier((going, before))
                sums[at_before] = (held[at_before], before)
            before, at_before = across(going, axis, mask), at
        sums[at_before] = (held[at_before], before)
        held = {at: own + far.astype(fp32) for at, (own, far) in sums.items()}
    mine = held[0].astype(half)
    if pair_count() == 1:
        return mine[:, None]
    other = across(held[1].astype(half), axis, 1)
    low = lax.axis_index(axis) % 2
    return jnp.stack([jnp.where(low == 0, mine, other), jnp.where(low == 0, other, mine)], axis=1)


def rms_norm(values, gain_vec):
    return (
        values * lax.rsqrt(jnp.mean(values * values, axis=-1, keepdims=True) + norm_eps) * gain_vec
    )


def gate_terms(gate_rec, gate_inp, conv_val, rec_vals):
    recur_gate = jax.nn.sigmoid(gate_rec)
    admit_gate = jax.nn.sigmoid(gate_inp)
    log_decay = -gate_power * recur_gate * jax.nn.softplus(-rec_vals)
    decays = jnp.exp(log_decay)
    scaler = jnp.sqrt(jnp.maximum(-jnp.expm1(2.0 * log_decay), floor_square))
    return (decays, scaler * admit_gate * conv_val)


def contract_rows(left, right):
    return lax.dot_general(left, right, (((0,), (0,)), ((), ())), preferred_element_type=fp32)


def times_trans(left, right):
    return lax.dot_general(left, right, (((1,), (1,)), ((), ())), preferred_element_type=fp32)


def part_of_sum(left, right):
    return times_trans(left, right).astype(half)


def times(left, right):
    return jnp.dot(left, right, preferred_element_type=fp32)


def gelu_product(first, second):
    return jax.nn.gelu(first, approximate=True) * second


def turned(value, shift, axis):
    size = value.shape[axis]
    return lax.dynamic_slice_in_dim(
        jnp.concatenate([value, value], axis=axis), shift, size, axis=axis
    )


def on_device(
    tokens,
    valid_mask,
    teacher,
    norm_one,
    proj_gelu,
    proj_rec,
    conv_taps,
    conv_bias,
    gate_rec_w,
    gate_rec_b,
    gate_inp_w,
    gate_inp_b,
    rec_param,
    proj_out,
    norm_two,
    mlp_gate,
    mlp_up,
    mlp_down,
):
    seqs, dps = lax.axis_size("seq"), lax.axis_size("dp")
    everyone = seqs * dps
    me_seq = lax.axis_index("seq")
    local_len, model = tokens.shape[-2:]
    rec_width = proj_rec.shape[1]
    hidden_width = mlp_gate.shape[1]
    rows_w = proj_rec.shape[0]
    rows_c = gate_rec_w.shape[0]
    steps = seqs * local_len

    plane, cube, pairs = plane_bits(), cube_bits(), pair_count()

    width_r = rec_width // seqs
    span_blocks = max((i * width_r + width_r - 1) // BW - i * width_r // BW for i in range(seqs)) + 1
    span = span_blocks * BW

    def first_block(place):
        return jnp.minimum(place * width_r // BW, NB - span_blocks)

    first = [min(i * width_r // BW, NB - span_blocks) * BW for i in range(seqs)]
    base = first_block(me_seq) * BW
    shift = me_seq * width_r - base

    def rec_columns(place):
        begin, end = first[place], first[place] + span
        own = place * width_r
        return [proj_rec[:, own:end], proj_rec[:, begin:own]]

    pay_in = jnp.stack(
        [
            jnp.concatenate(
                [*rec_columns(i), proj_gelu[:, i * width_r : (i + 1) * width_r]], axis=1
            )
            for i in range(seqs)
        ]
    )
    out_trans = proj_out.T.reshape(rows_w, seqs, width_r).transpose(1, 0, 2)

    def by_slice(value):
        return value.reshape(rows_w, seqs, pairs, -1).transpose(1, 0, 2, 3)

    pay_mlp = jnp.concatenate([by_slice(mlp_gate), by_slice(mlp_up), by_slice(mlp_down.T)], axis=3)
    pay_mlp = pay_mlp.transpose(0, 2, 1, 3)
    cols = hidden_width // (pairs * seqs)

    mask_val = valid_mask.reshape(local_len).astype(fp32)
    own_count = jnp.sum(mask_val)
    count_high = jnp.floor(own_count / 128.0)
    count_pair = jnp.stack([count_high, own_count - 128.0 * count_high]).astype(half)

    def row_of(value):
        return jnp.pad(value, ((0, 0), (0, 2 * BW - value.shape[1])))

    block_rows = -(-rows_c // 16) * 16
    package = jnp.concatenate(
        [
            jnp.pad(
                jnp.concatenate([gate_rec_w, gate_inp_w], axis=1),
                ((0, block_rows - rows_c), (0, 0)),
            ),
            row_of(conv_taps),
            row_of(jnp.stack([conv_bias, gate_rec_b, gate_inp_b, rec_param])),
            row_of(jnp.stack([norm_one, norm_two])),
            row_of(count_pair[None, :]),
            jnp.zeros((5, 2 * BW), half),
        ],
        axis=0,
    )
    w_in, w_out, mlp_own, shared, tokens_all = opening(
        pay_in, out_trans, pay_mlp, package, tokens.reshape(local_len, model), 1
    )
    w_in = w_in.reshape(model, span + width_r)
    w_out = w_out.reshape(model, width_r)
    w_mlp = cube_gather(mlp_own, "dp").reshape(model, 3 * cols)
    w_two, w_down = w_mlp[:, : 2 * cols], w_mlp[:, 2 * cols :]
    blocks_all = shared[:, :rows_c].reshape(rec_width, 2 * BW)
    vectors = shared[:, block_rows:].astype(fp32)
    channel_vecs = vectors[:, : CONV + 4, :rows_c].transpose(1, 0, 2).reshape(CONV + 4, rec_width)
    gains = vectors[:, CONV + 4 : CONV + 6, :rows_w].transpose(1, 0, 2).reshape(2, model)
    counts = jnp.sum(vectors[:, CONV + 6, :2], axis=0)
    valid_total = 128.0 * counts[0] + counts[1]

    span_vecs = turned(
        lax.dynamic_slice(channel_vecs, (0, base), (CONV + 4, span)), shift, axis=1
    )
    tap_vals, bias_vals = span_vecs[:CONV], span_vecs[CONV]
    rec_bias, inp_bias, rec_vals = (span_vecs[CONV + 1 + i, :width_r] for i in range(3))
    span_mats = lax.dynamic_slice(blocks_all, (base, 0), (span, 2 * BW))

    def block_diagonal(value):
        rows = []
        for place in range(span_blocks):
            block = value[place * BW : (place + 1) * BW]
            rows.append(jnp.pad(block, ((0, 0), (place * BW, (span_blocks - 1 - place) * BW))))
        whole = turned(jnp.concatenate(rows, axis=0), shift, axis=0)
        return lax.dynamic_slice(whole, (0, shift), (span, width_r))

    w_gates = jnp.concatenate(
        [block_diagonal(span_mats[:, :BW]), block_diagonal(span_mats[:, BW:])], axis=1
    )
    gain_one, gain_two = gains[0], gains[1]

    flat_in = tokens.reshape(local_len, model).astype(fp32)
    tokens_all = tokens_all.reshape(steps, model).astype(fp32)
    normed_all = rms_norm(tokens_all, gain_one).astype(half)
    pre = times(normed_all, w_in)
    rec_pre, gelu_pre = pre[:, :span], pre[:, span:]
    padded = jnp.concatenate([jnp.zeros((CONV - 1, span), fp32), rec_pre], axis=0)
    conv_sum = bias_vals + jnp.zeros_like(rec_pre)
    for offset in range(CONV):
        conv_sum = conv_sum + tap_vals[offset] * padded[CONV - 1 - offset : CONV - 1 - offset + steps]
    conv_low = conv_sum.astype(half)
    conv_val = conv_low[:, :width_r].astype(fp32)
    gates = times(conv_low, w_gates)
    gate_rec = gates[:, :width_r] + rec_bias
    gate_inp = gates[:, width_r:] + inp_bias
    decays, drives = gate_terms(gate_rec, gate_inp, conv_val, rec_vals)
    states = time_scan(forward_scan_kernel, decays, drives)
    mixed_low = gelu_product(gelu_pre, states).astype(half)
    mixed_part = part_of_sum(mixed_low, w_out).reshape(seqs, local_len, model)
    middle = flat_in + scatter_sum(mixed_part, plane, 3)

    normed_two_low = rms_norm(middle, gain_two).astype(half)
    group = pairs * seqs
    tall = group * local_len
    normed_two_all = gather(normed_two_low, cube, 4).reshape(tall, model)
    pre_two = times(normed_two_all, w_two)
    gate_pre, up_pre = pre_two[:, :cols], pre_two[:, cols:]
    hidden_low = gelu_product(gate_pre, up_pre).astype(half)
    down_part = part_of_sum(hidden_low, w_down).reshape(group, local_len, model)
    result = middle + scatter_sum(down_part, cube, 5)
    differ = result - teacher.reshape(local_len, model).astype(fp32)
    own_loss = 0.5 * jnp.sum(mask_val[:, None] * differ * differ)
    token_total = local_len * everyone
    grad_result = mask_val[:, None] * (token_total / valid_total) * differ
    output = result.reshape(tokens.shape).astype(half)

    down_all = gather(grad_result.astype(half), cube, 6).reshape(tall, model)
    grad_down = contract_rows(down_all, hidden_low)
    grad_hidden = times(down_all, w_down)
    _, pull_mlp = jax.vjp(gelu_product, gate_pre, up_pre)
    two_low = jnp.concatenate(pull_mlp(grad_hidden), axis=1).astype(half)
    grad_two = contract_rows(normed_two_all, two_low)
    two_part = part_of_sum(two_low, w_two).reshape(group, local_len, model)
    grad_normed_two = scatter_sum(two_part, cube, 7)

    grad_normed_two, grad_two, grad_down = lax.optimization_barrier(
        (grad_normed_two, grad_two, grad_down)
    )
    sent_mlp = cube_scatter(
        [
            grad_two.reshape(seqs, dps, rows_w, 2 * cols),
            grad_down.reshape(seqs, dps, rows_w, cols),
        ],
        "dp",
    )
    _, pull_norm_two = jax.vjp(rms_norm, middle, gain_two)
    grad_middle_norm, grad_norm_two = pull_norm_two(grad_normed_two)
    grad_middle = grad_result + grad_middle_norm

    middle_low = gather(grad_middle.astype(half), plane, 8).reshape(steps, model)
    grad_out = contract_rows(middle_low, mixed_low)
    grad_mixed = times(middle_low, w_out)
    _, pull_mix = jax.vjp(gelu_product, gelu_pre, states)
    grad_gelu_pre, grad_states = pull_mix(grad_mixed)
    adjoint = time_scan(backward_scan_kernel, decays, grad_states)
    prior_state = jnp.concatenate([jnp.zeros_like(states[:1]), states[:-1]], axis=0)
    _, pull_gates = jax.vjp(gate_terms, gate_rec, gate_inp, conv_val, rec_vals)
    grad_rec_gate, grad_inp_gate, grad_conv_direct, grad_rec_param = pull_gates(
        (adjoint * prior_state, adjoint)
    )
    gates_low = jnp.concatenate([grad_rec_gate, grad_inp_gate], axis=1).astype(half)
    grad_gate_bias = jnp.sum(gates_low.astype(fp32), axis=0)
    grad_gates = contract_rows(conv_low, gates_low)
    grad_conv = times_trans(gates_low, w_gates) + jnp.pad(
        grad_conv_direct, ((0, 0), (0, span - width_r))
    )
    grad_conv_bias = jnp.sum(grad_conv, axis=0)
    ahead = jnp.concatenate([grad_conv, jnp.zeros((CONV - 1, span), fp32)], axis=0)
    tap_grads = []
    rec_back = jnp.zeros_like(grad_conv)
    for offset in range(CONV):
        window = padded[CONV - 1 - offset : CONV - 1 - offset + steps]
        tap_grads.append(jnp.sum(grad_conv * window, axis=0))
        rec_back = rec_back + tap_vals[offset] * ahead[offset : offset + steps]
    in_low = jnp.concatenate([rec_back.astype(half), grad_gelu_pre.astype(half)], axis=1)
    grad_in = contract_rows(normed_all, in_low)
    in_part = part_of_sum(in_low, w_in).reshape(seqs, local_len, model)
    unit_all = tokens_all * lax.rsqrt(
        jnp.mean(tokens_all * tokens_all, axis=-1, keepdims=True) + norm_eps
    )
    grad_norm_one = jnp.sum(in_part.reshape(steps, model).astype(fp32) * unit_all, axis=0)

    def spread(value):
        return lax.dynamic_update_slice(
            jnp.zeros((value.shape[0], rec_width), fp32), value, (0, base)
        )

    def unturned(value, axis):
        return turned(value, span - shift, axis)

    def diagonal_blocks(value):
        wide = unturned(unturned(jnp.pad(value, ((0, 0), (0, span - width_r))), 1), 0)
        block = lax.broadcasted_iota(jnp.int32, (span, BW), 0) // BW
        picked = wide[:, :BW]
        for i in range(1, span_blocks):
            picked = jnp.where(block == i, wide[:, i * BW : (i + 1) * BW], picked)
        return picked

    mats = jnp.concatenate(
        [diagonal_blocks(grad_gates[:, :width_r]), diagonal_blocks(grad_gates[:, width_r:])], axis=1
    )
    mats = lax.dynamic_update_slice(jnp.zeros((rec_width, 2 * BW), fp32), mats, (base, 0))
    mats = jnp.pad(
        mats.reshape(everyone, rows_c, 2 * BW), ((0, 0), (0, block_rows - rows_c), (0, 0))
    )

    def widen(value):
        return jnp.pad(value[None, :], ((0, 0), (0, span - width_r)))

    lines = jnp.concatenate(
        [
            jnp.stack(tap_grads),
            grad_conv_bias[None, :],
            widen(grad_gate_bias[:width_r]),
            widen(grad_gate_bias[width_r:]),
            widen(grad_rec_param),
        ],
        axis=0,
    )
    lines = spread(unturned(lines, 1)).reshape(CONV + 4, everyone, rows_c).transpose(1, 0, 2)
    gain_lines = jnp.stack([grad_norm_one, grad_norm_two]).reshape(2, everyone, rows_w)
    gain_lines = gain_lines.transpose(1, 0, 2)

    def lane_pad(value):
        return jnp.pad(value, ((0, 0), (0, 0), (0, LANES - value.shape[2])))

    small = jnp.concatenate(
        [
            lane_pad(lines),
            lane_pad(gain_lines),
            jnp.full((everyone, 1, LANES), own_loss),
            jnp.zeros((everyone, 5, LANES), fp32),
        ],
        axis=1,
    )
    grad_normed, back_in, back_out, back_mlp, mats, small = closing(
        in_part,
        grad_in.reshape(seqs, dps, rows_w, span + width_r),
        grad_out.reshape(seqs, dps, rows_w, width_r),
        sent_mlp,
        mats.astype(half),
        small,
        2,
    )
    mean_loss = small[CONV + 6, 0] / (valid_total * model)

    _, pull_norm_one = jax.vjp(lambda values: rms_norm(values, gain_one), flat_in)
    grad_tokens = (grad_middle + pull_norm_one(grad_normed)[0]).reshape(tokens.shape).astype(half)

    def rejoin(value):
        return value.transpose(2, 0, 1, 3).reshape(rows_w, hidden_width)

    out_gate, out_up, out_down = (rejoin(back_mlp[..., i * cols : (i + 1) * cols]) for i in range(3))
    out_gate, out_up = out_gate.astype(fp32), out_up.astype(fp32)
    out_down = out_down.T.astype(fp32)
    back_in = back_in.astype(fp32)
    out_proj_out = back_out.transpose(1, 0, 2).reshape(rows_w, rec_width).T.astype(fp32)
    out_proj_gelu = back_in[:, :, span:].transpose(1, 0, 2).reshape(rows_w, rec_width)
    out_proj_rec = jnp.zeros((rows_w, rec_width), fp32)
    for place in range(seqs):
        begin, end, own = first[place], first[place] + span, place * width_r
        piece = back_in[place]
        piece = jnp.concatenate([piece[:, end - own : span], piece[:, : end - own]], axis=1)
        out_proj_rec = out_proj_rec + jnp.pad(piece, ((0, 0), (begin, rec_width - end)))

    return (
        output,
        mean_loss,
        grad_tokens,
        small[CONV + 4, :rows_w],
        out_proj_gelu,
        out_proj_rec,
        small[:CONV, :rows_c],
        small[CONV, :rows_c],
        mats[:rows_c, :BW],
        small[CONV + 1, :rows_c],
        mats[:rows_c, BW:],
        small[CONV + 2, :rows_c],
        small[CONV + 3, :rows_c],
        out_proj_out,
        small[CONV + 5, :rows_w],
        out_gate,
        out_up,
        out_down,
    )


def solution(mesh):
    both = ("seq", "dp")
    rows, cols, flat = P(both, None), P(None, both), P(both)
    acts = P("dp", "seq", None)
    in_specs = (
        acts,
        P("dp", "seq"),
        acts,
        flat,
        rows,
        rows,
        cols,
        flat,
        rows,
        flat,
        rows,
        flat,
        flat,
        cols,
        flat,
        rows,
        rows,
        cols,
    )
    out_specs = (
        acts,
        P(),
        acts,
        flat,
        rows,
        rows,
        cols,
        flat,
        rows,
        flat,
        rows,
        flat,
        flat,
        cols,
        flat,
        rows,
        rows,
        cols,
    )
    return jax.shard_map(
        on_device, mesh=mesh, in_specs=in_specs, out_specs=out_specs, check_vma=False
    )
```

time: 4310 us -> 854 us (0.20)
  waiting for transfers between devices: 3320 us -> 99.7 us
  Pallas kernels: 0 us -> 451 us
  local copies, waits for them, and re-layouts: 348 us -> 105 us
  blocking collectives: 183 us -> 0 us
  matrix products: 243 us -> 103 us
  other arithmetic: 119 us -> 64.7 us
  starting transfers between devices: 61.6 us -> 8.97 us
    reduce_scatter x8 -> x0, waiting for transfers between devices: 2920 us -> none  [the longest x1 454 us: on_device(): lax.psum_scatter(grad_proj_out, ('seq', 'dp'), scatter_dimension=1, tiled...]
    pallas_call x0 -> x10, Pallas kernels: none -> 451 us  [the longest x1 129 us: opening(): pl.pallas_call(kernel, out_shape=[*(jax.ShapeDtypeStruct((seqs, dps, rows...]
    all_gather x8 -> x0, waiting for transfers between devices: 361 us -> none  [the longest x1 142 us: on_device(): lax.all_gather(mlp_up, ('seq', 'dp'), axis=0, tiled=True)]
    slice x93 -> x32, local copies, waits for them, and re-layouts: 182 us -> 25.9 us  [the longest x7 10.2 us: rec_columns(): return [proj_rec[:, own:end], proj_rec[:, begin:own]]]
    pad x48 -> x12, local copies, waits for them, and re-layouts: 91.9 us -> 6.57 us  [the longest x2 2.49 us: time_scan(): jnp.pad(other, wide)]
    psum x2 -> x0, blocking collectives: 80.5 us -> none  [on_device(): lax.psum((jnp.sum(mask_val), 0.5 * jnp.sum(mask_val[:, None] * differ * d...]
    ppermute x16 -> x6, waiting for transfers between devices: 37.1 us -> 99.7 us  [across(): lax.ppermute(value, axis, [(i, i ^ mask) for i in range(lax.axis_size(axi...]
    all_gather x1 -> x0, blocking collectives: 59.6 us -> none  [on_device(): lax.all_gather(conv_taps, ('seq', 'dp'), axis=1, tiled=True)]
  transfers between devices with their start and end apart: 33 -> 6, of which waited for: 28 -> 4; matrix products, arithmetic and copies ran while one was open for 9% -> 11% of each run, Pallas kernels for 0% -> 8%
where the time goes in v1:
time: 854 us; the launch traced here: 840 us
  Pallas kernels  451 us (53%)
  local copies, waits for them, and re-layouts  105 us (12%)
  matrix products  103 us (12%)
  waiting for transfers between devices  99.7 us (12%)
  other arithmetic  64.7 us (8%)
  starting transfers between devices  8.97 us (1%)
    pallas_call x1, Pallas kernels, opening(): pl.pallas_call(kernel, out_shape=[*(jax.ShapeDtypeStruct((seqs, dps, rows...  129 us
    pallas_call x1, Pallas kernels, closing(): pl.pallas_call(kernel, out_shape=[shape(in_part.shape[1:], fp32), *(shape...  119 us
    ppermute x6, waiting for transfers between devices, across(): lax.ppermute(value, axis, [(i, i ^ mask) for i in range(lax.axis_size(axi...  99.7 us
    pallas_call x3, Pallas kernels, scatter_sum(): pl.pallas_call(kernel, out_shape=jax.ShapeDtypeStruct((rows, width), fp32...  93.4 us
    pallas_call x3, Pallas kernels, gather(): pl.pallas_call(kernel, out_shape=jax.ShapeDtypeStruct((2 ** len(bits), ro...  92 us
    dot_general x5, matrix products, contract_rows(): lax.dot_general(left, right, (((0,), (0,)), ((), ())), preferred_element_...  36.5 us
    dot_general x5, matrix products, times_trans(): lax.dot_general(left, right, (((1,), (1,)), ((), ())), preferred_element_...  35 us
    dot_general x5, matrix products, times(): return jnp.dot(left, right, preferred_element_type=fp32)  31.8 us
  transfers between devices with their start and end apart: 6, of which 4 were waited for; matrix products, arithmetic and copies ran while one was open for 11% of the time, Pallas kernels for 8%

profile of v1, /device:TPU:11, one launch (start us, length us, event | category | flops | bytes accessed | tf_op | source)
XLA Modules:
  0.0 840.4 jit_solution(11470369004578030131)
XLA Ops:
  1.7 1.7 fusion.123
  8.9 1.9 fusion.118
  14.6 2.6 reshape.259
  23.7 1.5 copy_bitcast_fusion
  26.7 2.0 maximum_bitcast_fusion.refs_2_
  32.2 129.3 %opening.1 = (bf16[8,4,64,832]{3,2,1,0:T(8,128)(2,1)}, bf16[8,4,64,320]{3,2,1,0:T(8,128)(2,1)S(1)}, bf16[8,2,64,1152]{3,2,1,0:T(8,128)(2,1)S(1)}, bf16[32,96,512]{2,1,0:T(8,128)(2,1)S(1)}, bf16[8,128,2048]{2,1,0:T(8,128)(2,1)}) custom-call(bf16[8,64,832]{2,1,0:T(8,128)(2,1)S(1)} %copy-done.4, bf16[8,64,320]{2,1,0:T(8,128)(2,1)S(1)} %bitcast.248, ...), custom_call_target="tpu_custom_call" | custom-call | tf_op jit(solution)/shard_map/opening/pallas_call | solution.py:511
  163.7 2.0 dynamic-slice_bitcast_fusion.3
  165.6 2.1 copy-done.25
  167.8 2.1 collective-permute-start
  170.7 1.9 slice.373
  179.2 3.2 multiply_reduce_fusion.1
  185.0 4.5 fusion.130
  189.8 1.5 copy-done.17
  191.3 2.2 fusion.73
  193.5 2.1 fusion.70
  195.6 2.2 add_convert_fusion.1
  198.9 1.8 convert_multiply_fusion.1
  203.2 7.1 forward_scan_kernel.1
  210.4 2.6 multiply_convert_fusion.4
  212.9 4.4 convolution_convert_fusion.2
  217.3 23.5 %scatter_3.1 = f32[128,2048]{1,0:T(8,128)} custom-call(bf16[8,128,2048]{2,1,0:T(8,128)(2,1)} %bitcast.270), custom_call_target="tpu_custom_call" | custom-call | tf_op jit(solution)/shard_map/scatter_3/pallas_call | solution.py:302
  244.6 34.4 %gather_4.1 = bf16[16,128,2048]{2,1,0:T(8,128)(2,1)} custom-call(bf16[128,2048]{1,0:T(8,128)(2,1)} %multiply_convert_fusion.5.x_ref), custom_call_target="tpu_custom_call" | custom-call | tf_op jit(solution)/shard_map/gather_4/pallas_call | solution.py:279
  283.1 1.6 collective-permute-start.2
  285.2 2.4 bitcast_dynamic-update-slice_fusion.2
  287.6 2.4 bitcast_dynamic-update-slice_fusion.1
  290.0 46.0 %collective-permute-done.2 = bf16[8,64,1152]{2,1,0:T(8,128)(2,1)S(1)} collective-permute-done((bf16[8,64,1152]{2,1,0:T(8,128)(2,1)}, bf16[8,64,1152]{2,1,0:T(8,128)(2,1)S(1)}, u32[]{:S(2)}, u32[]{:S(2)}) %collective-permute-start.2) | collective-permute-done | bytes 1179680 | tf_op jit(solution)/shard_map/ppermute | solution.py:849
  337.1 10.6 %fusion.8 = f32[2048,768]{0,1:T(8,128)S(1)} fusion(bf16[2048,2048]{1,0:T(8,128)(2,1)} %bitcast.257, bf16[2048,1152]{1,0:T(8,128)(2,1)} %bitcast.263), kind=kOutput, calls=%fused_computation.23 | convolution fusion | flops 6442450944 | bytes 17825792 | tf_op jit(solution)/shard_map/dot_general | solution.py:939
  350.3 8.7 %convolution_convert_fusion.1 = bf16[2048,2048]{1,0:T(8,128)(2,1)} fusion(bf16[2048,384]{0,1:T(8,128)(2,1)S(1)} %multiply_convert_fusion.3, bf16[2048,1152]{1,0:T(8,128)(2,1)} %bitcast.264), kind=kOutput, calls=%fused_computation.6 | convolution fusion | flops 3225419776 | bytes 11534336 | tf_op jit(solution)/shard_map/dot_general | solution.py:931
  359.1 35.7 %scatter_5.1 = f32[128,2048]{1,0:T(8,128)} custom-call(bf16[16,128,2048]{2,1,0:T(8,128)(2,1)} %bitcast.256), custom_call_target="tpu_custom_call" | custom-call | tf_op jit(solution)/shard_map/scatter_5/pallas_call | solution.py:302
  394.8 2.2 multiply_convert_fusion.6.x_ref
  396.9 34.3 %gather_6.1 = bf16[16,128,2048]{2,1,0:T(8,128)(2,1)} custom-call(bf16[128,2048]{1,0:T(8,128)(2,1)} %multiply_convert_fusion.6.x_ref), custom_call_target="tpu_custom_call" | custom-call | tf_op jit(solution)/shard_map/gather_6/pallas_call | solution.py:279
  431.3 10.2 %fusion.131 = f32[2048,384]{1,0:T(8,128)} fusion(bf16[2048,2048]{1,0:T(8,128)(2,1)} %bitcast.261, bf16[2048,384]{0,1:T(8,128)(2,1)} %copy-done.32), kind=kOutput, calls=%fused_computation.324 | convolution fusion | flops 3221225472 | bytes 13107200 | tf_op jit(solution)/shard_map/dot_general | solution.py:927
  441.5 8.5 %fusion.6 = (bf16[2048,384]{0,1:T(8,128)(2,1)S(1)}, bf16[2048,384]{0,1:T(8,128)(2,1)S(1)}) fusion(f32[2048,768]{0,1:T(8,128)} %copy-done.20, bf16[2048,2048]{1,0:T(8,128)(2,1)S(1)} %bitcast.262, bf16[2048,1152]{1,0:T(8,128)(2,1)} %bitcast.265), kind=kOutput, calls=%fused_computation.17 | convolution fusion | flops 3240099840 | bytes 19398656 | tf_op jit(solution)/shard_map/dot_general | solution.py:939
  450.0 8.7 %fusion.12 = f32[2048,768]{1,0:T(8,128)} fusion(bf16[2048,2048]{1,0:T(8,128)(2,1)S(1)} %bitcast.260, bf16[2048,384]{0,1:T(8,128)(2,1)S(1)} %get-tuple-element.73, bf16[2048,384]{0,1:T(8,128)(2,1)S(1)} %get-tuple-element.72), kind=kOutput, calls=%fused_computation.51 | convolution fusion | flops 6448742400 | bytes 17825792 | tf_op jit(solution)/shard_map/dot_general | solution.py:927
  458.8 9.2 %convolution_convert_fusion = bf16[2048,2048]{1,0:T(8,128)(2,1)} fusion(bf16[2048,1152]{1,0:T(8,128)(2,1)S(1)} %bitcast.268, bf16[2048,384]{0,1:T(8,128)(2,1)S(1)} %get-tuple-element.73, bf16[2048,384]{0,1:T(8,128)(2,1)S(1)} %get-tuple-element.72), kind=kOutput, calls=%fused_computation.5 | convolution fusion | flops 6452936704 | bytes 14680064 | tf_op jit(solution)/shard_map/dot_general | solution.py:931
  468.0 34.3 %scatter_7.1 = f32[128,2048]{1,0:T(8,128)} custom-call(bf16[16,128,2048]{2,1,0:T(8,128)(2,1)} %bitcast.255), custom_call_target="tpu_custom_call" | custom-call | tf_op jit(solution)/shard_map/scatter_7/pallas_call | solution.py:302
  502.3 2.6 multiply_reduce_fusion.7
  505.0 1.8 fusion.115
  506.8 23.3 %gather_8.1 = bf16[8,128,2048]{2,1,0:T(8,128)(2,1)} custom-call(bf16[128,2048]{1,0:T(8,128)(2,1)} %get-tuple-element.66.x_ref), custom_call_target="tpu_custom_call" | custom-call | tf_op jit(solution)/shard_map/gather_8/pallas_call | solution.py:279
  530.1 7.3 fusion.64
  538.6 9.8 %backward_scan_kernel.1 = f32[1024,384]{1,0:T(8,128)} custom-call(f32[1024,384]{1,0:T(8,128)} %pad.112.decay_ref, f32[1024,384]{1,0:T(8,128)} %pad.114.grad_ref), custom_call_target="tpu_custom_call" | custom-call | tf_op jit(solution)/shard_map/backward_scan_kernel/pallas_call | solution.py:837
  548.4 4.9 multiply_reduce_fusion.6
  555.6 2.1 fusion.49
  557.7 2.0 dynamic-slice_bitcast_fusion.1
  562.5 3.0 multiply_reduce_fusion.2
  572.5 6.5 copy.66
  579.0 6.2 fusion.50.refs_2_
  587.7 2.3 dynamic-slice_bitcast_fusion.5
  590.3 11.6 %multiply_reduce_fusion = (f32[2048]{0:T(1024)S(1)}, bf16[1024,2048]{1,0:T(8,128)(2,1)}, bf16[1024,2048]{1,0:T(8,128)(2,1)}) fusion(bf16[8,128,2048]{2,1,0:T(8,128)(2,1)} %get-tuple-element.34, f32[1024]{0:T(1024)S(1)} %copy-done.89, f32[2048]{0:T(1024)S(1)} %mul.493, bf16[2048,832]{1,0:T(8,128)(2,1)} %bitcast.308, bf16[1024,320]{1,0:T(8,128)(2,1)} %get-tuple-element.80, ...), kind=kOutput, calls=%fused_computation.1 | convolution fusion | flops 3509843968 | bytes 17715200 | tf_op jit(solution)/shard_map/dot_general | solution.py:931
  601.9 21.6 %collective-permute-done.3 = bf16[8,64,1152]{2,1,0:T(8,128)(2,1)} collective-permute-done((bf16[8,64,1152]{2,1,0:T(8,128)(2,1)}, bf16[8,64,1152]{2,1,0:T(8,128)(2,1)}, u32[]{:S(2)}, u32[]{:S(2)}) %collective-permute-start.3) | collective-permute-done | bytes 1179680 | tf_op jit(solution)/shard_map/ppermute | solution.py:849
  623.5 2.6 fusion.11
  626.1 2.6 collective-permute-start.5
  630.4 6.6 copy.64
  637.8 10.3 %fusion.13.refs_1_ = f32[8,4,64,832]{3,2,1,0:T(8,128)} fusion(bf16[8,4,64,1024]{3,2,1,0:T(8,128)(2,1)} %bitcast.272, bf16[1024,320]{1,0:T(8,128)(2,1)} %get-tuple-element.80, bf16[1024,512]{1,0:T(8,128)(2,1)} %get-tuple-element.102), kind=kOutput, calls=%fused_computation.57 | convolution fusion | flops 3493068800 | bytes 12713984 | tf_op jit(solution)/shard_map/dot_general | solution.py:927
  648.1 30.3 %collective-permute-done.5 = bf16[8,64,1152]{2,1,0:T(8,128)(2,1)S(1)} collective-permute-done((bf16[8,64,1152]{2,1,0:T(8,128)(2,1)}, bf16[8,64,1152]{2,1,0:T(8,128)(2,1)S(1)}, u32[]{:S(2)}, u32[]{:S(2)}) %collective-permute-start.5) | collective-permute-done | bytes 1179680 | tf_op jit(solution)/shard_map/ppermute | solution.py:849
  678.4 1.9 collective-permute-done.4
  680.9 1.7 pad_maximum_fusion.1.refs_3_
  682.6 119.2 %closing.1 = (f32[128,2048]{1,0:T(8,128)}, bf16[8,64,832]{2,1,0:T(8,128)(2,1)}, bf16[8,64,320]{2,1,0:T(8,128)(2,1)}, bf16[8,2,64,1152]{3,2,1,0:T(8,128)(2,1)}, f32[80,512]{1,0:T(8,128)}, /*index=5*/f32[16,128]{1,0:T(8,128)}) custom-call(bf16[8,128,2048]{2,1,0:T(8,128)(2,1)} %bitcast.269, f32[8,4,64,832]{3,2,1,0:T(8,128)} %fusion.13.refs_1_, ...), custom_call_target="tpu_custom_call" | custom-call | tf_op jit(solution)/shard_map/closing/pallas_call | solution.py:740
  815.4 2.4 copy.78
  817.7 3.6 reshape.284
  821.3 2.4 copy.76
  823.7 3.4 reshape.281
  828.3 2.4 reshape.282
  834.1 1.7 fusion.126
  (355 shorter events, 85.3 us)
Async XLA Ops:
  0.7 12.8 %copy-start.35 = (bf16[64,6144]{1,0:T(8,128)(2,1)S(1)}, bf16[64,6144]{1,0:T(8,128)(2,1)}, u32[]{:S(2)}) copy-start(bf16[64,6144]{1,0:T(8,128)(2,1)} %param.34) | copy-start | bytes 2359300
  0.7 13.4 %copy-start.36 = (bf16[6144,64]{0,1:T(8,128)(2,1)S(1)}, bf16[6144,64]{0,1:T(8,128)(2,1)}, u32[]{:S(2)}) copy-start(bf16[6144,64]{0,1:T(8,128)(2,1)} %param.35) | copy-start | bytes 2359300
  14.6 3.7 copy-start.47
  18.7 6.6 copy-start.51
  18.7 6.6 copy-start.62
  18.7 6.5 copy-start.73
  18.8 6.6 copy-start.53
  18.8 6.6 copy-start.56
  18.8 6.6 copy-start.70
  18.8 6.7 copy-start.60
  18.8 6.7 copy-start.61
  18.8 6.7 copy-start.68
  18.8 6.7 copy-start.55
  26.6 3.6 copy-start.57
  26.6 3.6 copy-start.58
  26.6 3.6 copy-start.67
  26.6 4.3 copy-start.94
  26.6 4.3 copy-start.95
  26.6 4.3 copy-start.96
  26.6 4.3 copy-start.97
  26.6 4.3 copy-start.83
  26.6 4.3 copy-start.86
  26.7 4.3 copy-start.87
  26.7 4.4 copy-start
  167.8 115.3 %collective-permute-start = (bf16[8,64,1152]{2,1,0:T(8,128)(2,1)}, bf16[8,64,1152]{2,1,0:T(8,128)(2,1)}, u32[]{:S(2)}, u32[]{:S(2)}) collective-permute-start(bf16[8,64,1152]{2,1,0:T(8,128)(2,1)} %get-tuple-element.100), channel_id=1, source_target_pairs={{0,1},{1,0},{2,3},{3,2},{4,5},{5,4},{6,7},{7,6},{8,9},{9,8},{10,11... | collective-permute-start | bytes 3538952 | tf_op jit(solution)/shard_map/ppermute | solution.py:849
  169.9 117.7 %collective-permute-start.1 = (bf16[8,64,1152]{2,1,0:T(8,128)(2,1)}, bf16[8,64,1152]{2,1,0:T(8,128)(2,1)}, u32[]{:S(2)}, u32[]{:S(2)}) collective-permute-start(bf16[8,64,1152]{2,1,0:T(8,128)(2,1)} %get-tuple-element.99), channel_id=1, source_target_pairs={{0,2},{1,3},{2,0},{3,1},{4,6},{5,7},{6,4},{7,5},{8,10},{9,11},{10,... | collective-permute-start | bytes 3538952 | tf_op jit(solution)/shard_map/ppermute | solution.py:849
  176.9 14.5 %copy-start.77 = (f32[320]{0:T(512)}, f32[320]{0:T(512)S(1)}, u32[]{:S(2)}) copy-start(f32[320]{0:T(512)S(1)} %get-tuple-element.141) | copy-start | bytes 3844
  179.2 3.8 copy-start.14
  191.3 6.5 copy-start.11
  212.9 4.4 copy-start.37
  244.5 38.5 %copy-start.101 = (s32[1,128]{1,0:T(1,128)S(1)}, s32[1,128]{1,0:T(1,128)}, u32[]{:S(2)}) copy-start(s32[1,128]{1,0:T(1,128)} %param.19) | copy-start | bytes 1540
  283.1 52.9 %collective-permute-start.2 = (bf16[8,64,1152]{2,1,0:T(8,128)(2,1)}, bf16[8,64,1152]{2,1,0:T(8,128)(2,1)S(1)}, u32[]{:S(2)}, u32[]{:S(2)}) collective-permute-start(bf16[8,64,1152]{2,1,0:T(8,128)(2,1)} %collective-permute-done), channel_id=1, source_target_pairs={{0,2},{1,3},{2,0},{3,1},{4,6},{5,7},{6,4},{7,5},{8,10},{9,11},{10,... | collective-permute-start | bytes 3538952 | tf_op jit(solution)/shard_map/ppermute | solution.py:849
  350.3 8.7 %copy-start.32 = (bf16[2048,384]{0,1:T(8,128)(2,1)}, bf16[2048,384]{0,1:T(8,128)(2,1)S(1)}, u32[]{:S(2)}) copy-start(bf16[2048,384]{0,1:T(8,128)(2,1)S(1)} %multiply_convert_fusion.3) | copy-start | bytes 4718596
  359.1 35.7 %copy-start.23 = (bf16[1,128,2048]{2,1,0:T(8,128)(2,1)S(1)}, bf16[1,128,2048]{2,1,0:T(8,128)(2,1)}, u32[]{:S(2)}) copy-start(bf16[1,128,2048]{2,1,0:T(8,128)(2,1)} %param.20) | copy-start | bytes 1572868
  431.2 10.2 %copy-start.19 = (bf16[16,128,2048]{2,1,0:T(8,128)(2,1)S(1)}, bf16[16,128,2048]{2,1,0:T(8,128)(2,1)}, u32[]{:S(2)}) copy-start(bf16[16,128,2048]{2,1,0:T(8,128)(2,1)} %gather_6.1) | copy-start | bytes 25165828
  431.3 18.7 %slice-start = ((s8[8388608]{0:T(1024)(128)(4,1)}), s8[4194304]{0:T(1024)(128)(4,1)S(1)}, s32[]{:S(2)}) async-start(s8[8388608]{0:T(1024)(128)(4,1)} %bitcast.258), calls=%async_computation | async-start | bytes 8388608
  441.5 8.5 %slice-start.1 = ((s8[8388608]{0:T(1024)(128)(4,1)}), s8[4194304]{0:T(1024)(128)(4,1)S(1)}, s32[]{:S(2)}) async-start(s8[8388608]{0:T(1024)(128)(4,1)} %bitcast.258), calls=%async_computation.1 | async-start | bytes 8388608
  441.5 17.3 %slice-start.2 = ((s8[4718592]{0:T(1024)(128)(4,1)}), s8[524288]{0:T(1024)(128)(4,1)S(1)}, s32[]{:S(2)}) async-start(s8[4718592]{0:T(1024)(128)(4,1)} %bitcast.266), calls=%async_computation.2 | async-start | bytes 1048576
  450.0 8.7 %slice-start.3 = ((s8[4718592]{0:T(1024)(128)(4,1)}), s8[4194304]{0:T(1024)(128)(4,1)S(1)}, s32[]{:S(2)}) async-start(s8[4718592]{0:T(1024)(128)(4,1)} %bitcast.266), calls=%async_computation.3 | async-start | bytes 8388608
  468.0 34.3 %copy-start.13 = (f32[128,2048]{1,0:T(8,128)S(1)}, f32[128,2048]{1,0:T(8,128)}, u32[]{:S(2)}) copy-start(f32[128,2048]{1,0:T(8,128)} %scatter_5.1) | copy-start | bytes 3145732
  538.6 9.8 %copy-start.8 = (f32[1024,640]{1,0:T(8,128)S(1)}, f32[1024,640]{1,0:T(8,128)}, u32[]{:S(2)}) copy-start(f32[1024,640]{1,0:T(8,128)} %copy-done.7) | copy-start | bytes 7864324
  538.6 9.8 %copy-start.76 = (f32[320]{0:T(512)S(1)}, f32[320]{0:T(512)}, u32[]{:S(2)}) copy-start(f32[320]{0:T(512)} %get-tuple-element.62) | copy-start | bytes 3844
  548.4 4.9 copy-start.78
  553.3 4.4 slice-start.4
  571.1 52.3 %collective-permute-start.3 = (bf16[8,64,1152]{2,1,0:T(8,128)(2,1)}, bf16[8,64,1152]{2,1,0:T(8,128)(2,1)}, u32[]{:S(2)}, u32[]{:S(2)}) collective-permute-start(bf16[8,64,1152]{2,1,0:T(8,128)(2,1)} %pad_maximum_fusion.9), channel_id=1, source_target_pairs={{0,2},{1,3},{2,0},{3,1},{4,6},{5,7},{6,4},{7,5},{8,10},{9,11},{10,... | collective-permute-start | bytes 3538952 | tf_op jit(solution)/shard_map/ppermute | solution.py:849
  572.5 6.5 copy-start.38
  579.0 6.2 copy-start.88
  587.6 14.3 %copy-start.15 = (bf16[2560,512]{1,0:T(8,128)(2,1)}, bf16[2560,512]{1,0:T(8,128)(2,1)S(1)}, u32[]{:S(2)}) copy-start(bf16[2560,512]{1,0:T(8,128)(2,1)S(1)} %maximum_dynamic-update-slice_fusion) | copy-start | bytes 7864324
  590.3 33.2 %copy-start.22 = (f32[8,64,768]{2,1,0:T(8,128)S(1)}, f32[8,64,768]{2,1,0:T(8,128)}, u32[]{:S(2)}) copy-start(f32[8,64,768]{2,1,0:T(8,128)} %get-tuple-element.75) | copy-start | bytes 4718596
  623.5 6.1 copy-start.74
  626.1 52.3 %collective-permute-start.5 = (bf16[8,64,1152]{2,1,0:T(8,128)(2,1)}, bf16[8,64,1152]{2,1,0:T(8,128)(2,1)S(1)}, u32[]{:S(2)}, u32[]{:S(2)}) collective-permute-start(bf16[8,64,1152]{2,1,0:T(8,128)(2,1)} %fusion.11), channel_id=1, source_target_pairs={{0,1},{1,0},{2,3},{3,2},{4,5},{5,4},{6,7},{7,6},{8,9},{9,8},{10,11... | collective-permute-start | bytes 3538952 | tf_op jit(solution)/shard_map/ppermute | solution.py:849
  628.7 51.6 %collective-permute-start.4 = (bf16[8,64,1152]{2,1,0:T(8,128)(2,1)}, bf16[8,64,1152]{2,1,0:T(8,128)(2,1)S(1)}, u32[]{:S(2)}, u32[]{:S(2)}) collective-permute-start(bf16[8,64,1152]{2,1,0:T(8,128)(2,1)} %pad_maximum_fusion.8), channel_id=1, source_target_pairs={{0,2},{1,3},{2,0},{3,1},{4,6},{5,7},{6,4},{7,5},{8,10},{9,11},{10,... | collective-permute-start | bytes 3538952 | tf_op jit(solution)/shard_map/ppermute | solution.py:849
  630.4 6.6 copy-start.92
  637.8 42.5 %copy-start.21 = (f32[8,64,768]{2,1,0:T(8,128)S(1)}, f32[8,64,768]{2,1,0:T(8,128)}, u32[]{:S(2)}) copy-start(f32[8,64,768]{2,1,0:T(8,128)} %get-tuple-element.74) | copy-start | bytes 4718596
  803.2 8.2 copy-start.90
  803.2 11.7 %copy-start.29 = (bf16[8,2,64,1152]{3,2,1,0:T(8,128)(2,1)S(1)}, bf16[8,2,64,1152]{3,2,1,0:T(8,128)(2,1)}, u32[]{:S(2)}) copy-start(bf16[8,2,64,1152]{3,2,1,0:T(8,128)(2,1)} %get-tuple-element.49) | copy-start | bytes 7077892
  832.2 4.3 copy-start.26
  834.0 3.6 copy-start.39
  834.1 3.6 copy-start.40
  834.1 3.6 copy-start.41
  834.1 3.6 copy-start.42
  834.1 3.6 copy-start.43
  834.1 3.6 copy-start.44
  834.1 3.6 copy-start.45
  (50 other events, 99.4 us)

commit v2 on v1

v2 whole, which is shorter than its diff:
```python
import functools
import itertools

import jax
import jax.numpy as jnp
from jax import lax
from jax.experimental import pallas as pl
from jax.experimental.pallas import tpu as pltpu
from jax.sharding import PartitionSpec as P

NB = 10
BW = 256
CONV = 4
LANES = 128
MLPS = 3

norm_eps = 1e-06
gate_power = 8.0
floor_square = 0.0001

fp32 = jnp.float32
half = jnp.bfloat16


def flip(index, mask):
    return index + mask - 2 * mask * ((index // mask) % 2)


def bit_values(bits):
    return [(lax.axis_index(axis) // mask) % 2 for axis, mask, _ in bits]


def slot_number(bits, vals, flipped):
    total = 0
    for place, (_, _, weight) in enumerate(bits):
        total = total + weight * (1 - vals[place] if place in flipped else vals[place])
    return total


def partner(bit):
    axis, mask, _ = bit
    return {axis: flip(lax.axis_index(axis), mask)}


def greet(bits):
    barrier = pltpu.get_barrier_semaphore()
    for bit in bits:
        pl.semaphore_signal(
            barrier, inc=1, device_id=partner(bit), device_id_type=pl.DeviceIdType.MESH
        )
    pl.semaphore_wait(barrier, len(bits))


def masks_of(size):
    return [2**place for place in reversed(range(size.bit_length() - 1))]


def plane_bits():
    return tuple(("seq", mask, mask) for mask in masks_of(lax.axis_size("seq")))


def pair_count():
    return 2 if lax.axis_size("dp") > 1 and 2 * lax.axis_size("seq") <= 16 else 1


def cube_bits():
    pair = (("dp", 1, lax.axis_size("seq")),) if pair_count() == 2 else ()
    return (*pair, *plane_bits())


def world_bits():
    dps = lax.axis_size("dp")
    return tuple(("dp", mask, mask) for mask in masks_of(dps)) + tuple(
        ("seq", mask, mask * dps) for mask in masks_of(lax.axis_size("seq"))
    )


def subsets(items):
    for size in range(len(items) + 1):
        yield from itertools.combinations(items, size)


def splits(width, count):
    tiles = width // LANES
    if tiles * LANES != width or tiles < count:
        return [(0, width)]
    cuts = [tiles * i // count * LANES for i in range(count + 1)]
    return [(cuts[i], cuts[i + 1] - cuts[i]) for i in range(count)]


def rotations(bits, width, fixed=0):
    begin, slow, last = list(range(fixed)), list(range(fixed, len(bits) - 1)), [len(bits) - 1]
    pieces = splits(width, len(slow))
    return [
        (first, size, tuple(begin + slow[turn:] + slow[:turn] + last))
        for turn, (first, size) in enumerate(pieces)
    ]


class Gathering:
    def __init__(self, bits, width, x_ref, o_ref, sems, fixed=0):
        self.bits, self.x_ref, self.o_ref = bits, x_ref, o_ref
        self.send_sems, self.recv_sems, self.local_sem = sems
        self.vals = bit_values(bits)
        self.parts = rotations(bits, width, fixed)
        self.numbers = {}
        for which in range(len(self.parts)):
            for stage in range(len(bits)):
                for held in subsets(range(stage)):
                    self.numbers[which, stage, held] = len(self.numbers)

    @staticmethod
    def semaphores(bits, width, fixed=0):
        copies = len(rotations(bits, width, fixed)) * (2 ** len(bits) - 1)
        return [
            pltpu.SemaphoreType.DMA((copies,)),
            pltpu.SemaphoreType.DMA((copies,)),
            pltpu.SemaphoreType.DMA,
        ]

    def own(self):
        slot = slot_number(self.bits, self.vals, ())
        return pltpu.make_async_copy(self.x_ref, self.o_ref.at[slot], self.local_sem)

    def transfer(self, which, stage, held):
        first, width, order = self.parts[which]
        cols = pl.ds(first, width)
        slot = slot_number(self.bits, self.vals, [order[place] for place in held])
        dst = self.o_ref.at[slot, :, cols]
        number = self.numbers[which, stage, held]
        in_place = held or self.x_ref is None
        return pltpu.make_async_remote_copy(
            src_ref=dst if in_place else self.x_ref.at[:, cols],
            dst_ref=dst,
            send_sem=self.send_sems.at[number],
            recv_sem=self.recv_sems.at[number],
            device_id=partner(self.bits[order[stage]]),
            device_id_type=pl.DeviceIdType.MESH,
        )

    def begin(self):
        if self.x_ref is not None:
            self.own().start()
        for stage in range(len(self.bits)):
            for which in range(len(self.parts)):
                self.transfer(which, stage, ()).start()

    def level(self, size):
        depth = len(self.bits)
        for held in itertools.combinations(range(depth), size):
            for which in range(len(self.parts)):
                self.transfer(which, held[-1], held[:-1]).wait_recv()
                for stage in range(held[-1] + 1, depth):
                    self.transfer(which, stage, held).start()

    def finish(self):
        for key in self.numbers:
            self.transfer(*key).wait_send()
        if self.x_ref is not None:
            self.own().wait()


class Fan:
    def __init__(self, source, target, sems):
        self.source, self.target = source, target
        self.send, self.recv = sems
        self.me, self.count = lax.axis_index("dp"), lax.axis_size("dp")

    @staticmethod
    def semaphores(count):
        return [pltpu.SemaphoreType.DMA((count,)), pltpu.SemaphoreType.DMA((count,))]

    def going(self, step):
        to = lax.rem(self.me + step, self.count)
        return remote(
            self.source(to), self.target(self.me), self.send.at[step], self.recv.at[step], {"dp": to}
        )

    def arriving(self, step):
        block = self.target(lax.rem(self.me - step + self.count, self.count))
        return remote(block, block, self.send.at[step], self.recv.at[step], {"dp": self.me})


class Scattering:
    def __init__(self, bits, x_ref, o_ref, scratch, fixed=0):
        self.bits, self.x_ref, self.o_ref = bits, x_ref, o_ref
        self.held, self.outgoing, self.incoming, self.load, self.send, self.recv = scratch
        self.rows, width = o_ref.shape
        self.chunk = 32 if self.rows % 32 == 0 else 16
        self.parts = [(at, size, order[::-1]) for at, size, order in rotations(bits, width, fixed)]
        self.vals = bit_values(bits)
        self.depth = len(bits)
        first_bit = self.parts[0][2][0]
        self.blocks = sorted(subsets(range(self.depth)), key=lambda s: (first_bit not in s, -len(s)))
        self.slots, self.numbers = {}, {}
        for stage in range(self.depth):
            for rest in subsets(range(stage + 1, self.depth)):
                self.slots[stage, rest] = len(self.slots)
        for which in range(len(self.parts)):
            for key in self.slots:
                self.numbers[(which, *key)] = len(self.numbers)
        self.loaded = set()

    @staticmethod
    def scratch(bits, value, wire, fixed=0):
        count, rows, width = value.shape
        copies = len(rotations(bits, width, fixed)) * (count - 1)
        return [
            pltpu.VMEM((count, rows, width), value.dtype),
            pltpu.VMEM((count - 1, rows, width), wire),
            pltpu.VMEM((count - 1, rows, width), wire),
            pltpu.SemaphoreType.DMA((count,)),
            pltpu.SemaphoreType.DMA((copies,)),
            pltpu.SemaphoreType.DMA((copies,)),
        ]

    def loading(self, members):
        key = sum(2**place for place in members)
        slot = slot_number(self.bits, self.vals, members)
        return pltpu.make_async_copy(self.x_ref.at[slot], self.held.at[key], self.load.at[key])

    def begin(self):
        for members in self.blocks:
            self.loading(members).start()

    def ready(self, members):
        key = sum(2**place for place in members)
        if key not in self.loaded:
            self.loaded.add(key)
            self.loading(members).wait()
        return key

    def transfer(self, which, stage, rest):
        first, width, order = self.parts[which]
        place = self.slots[stage, rest]
        number = self.numbers[which, stage, rest]
        return pltpu.make_async_remote_copy(
            src_ref=self.outgoing.at[place, :, pl.ds(first, width)],
            dst_ref=self.incoming.at[place, :, pl.ds(first, width)],
            send_sem=self.send.at[number],
            recv_sem=self.recv.at[number],
            device_id=partner(self.bits[order[stage]]),
            device_id_type=pl.DeviceIdType.MESH,
        )

    def add_up(self, which, key, arrived, store):
        first, width, _ = self.parts[which]
        cols = pl.ds(first, width)

        def body(step, carry):
            lines = pl.ds(pl.multiple_of(step * self.chunk, self.chunk), self.chunk)
            total = self.held[key, lines, cols].astype(fp32)
            for place in arrived:
                total = total + self.incoming[place, lines, cols].astype(fp32)
            store(lines, cols, total)
            return carry

        lax.fori_loop(0, self.rows // self.chunk, body, 0)

    def stage(self, stage):
        for rest in sorted(subsets(range(stage + 1, self.depth)), key=lambda s: (-len(s), s)):
            for which, (_, _, order) in enumerate(self.parts):
                going = (stage, *rest)
                key = self.ready([order[place] for place in going])
                for earlier in range(stage):
                    self.transfer(which, earlier, going).wait_recv()
                place = self.slots[stage, rest]

                def keep(lines, cols, total, place=place):
                    self.outgoing[place, lines, cols] = total.astype(self.outgoing.dtype)

                arrived = [self.slots[earlier, going] for earlier in range(stage)]
                self.add_up(which, key, arrived, keep)
                self.transfer(which, stage, rest).start()

    def finish(self):
        def keep(lines, cols, total):
            self.o_ref[lines, cols] = total

        key = self.ready(())
        for which in range(len(self.parts)):
            for stage in range(self.depth):
                self.transfer(which, stage, ()).wait_recv()
            self.add_up(which, key, [self.slots[stage, ()] for stage in range(self.depth)], keep)

    def close(self):
        for members in self.blocks:
            self.ready(members)
        for key in self.numbers:
            self.transfer(*key).wait_send()


def gather(value, bits, number, fixed=0):
    rows, width = value.shape

    def kernel(x_ref, o_ref, *sems):
        work = Gathering(bits, width, x_ref, o_ref, sems, fixed)
        greet(bits)
        work.begin()
        for size in range(1, len(bits) + 1):
            work.level(size)
        work.finish()

    return pl.pallas_call(
        kernel,
        out_shape=jax.ShapeDtypeStruct((2 ** len(bits), rows, width), value.dtype),
        in_specs=[pl.BlockSpec(memory_space=pltpu.VMEM)],
        out_specs=pl.BlockSpec(memory_space=pl.ANY),
        scratch_shapes=Gathering.semaphores(bits, width, fixed),
        compiler_params=pltpu.CompilerParams(collective_id=number, has_side_effects=True),
        name=f"gather_{number}",
    )(value)


def scatter_sum(value, bits, number, fixed=0):
    _, rows, width = value.shape

    def kernel(x_ref, o_ref, *scratch):
        work = Scattering(bits, x_ref, o_ref, scratch, fixed)
        work.begin()
        greet(bits)
        for stage in range(len(bits)):
            work.stage(stage)
        work.finish()
        work.close()

    return pl.pallas_call(
        kernel,
        out_shape=jax.ShapeDtypeStruct((rows, width), fp32),
        in_specs=[pl.BlockSpec(memory_space=pl.ANY)],
        out_specs=pl.BlockSpec(memory_space=pltpu.VMEM),
        scratch_shapes=Scattering.scratch(bits, value, half, fixed),
        compiler_params=pltpu.CompilerParams(
            collective_id=number, has_side_effects=True, vmem_limit_bytes=60 * 2**20
        ),
        name=f"scatter_{number}",
    )(value)


def remote(src, dst, send_sem, recv_sem, device):
    return pltpu.make_async_remote_copy(
        src_ref=src,
        dst_ref=dst,
        send_sem=send_sem,
        recv_sem=recv_sem,
        device_id=device,
        device_id_type=pl.DeviceIdType.MESH,
    )


class Exchange:
    def __init__(self, pieces, sems, across=False):
        self.pieces = [(*piece, None, None)[:4] for piece in pieces]
        self.send, self.recv, self.local = sems
        self.me, self.count = lax.axis_index("seq"), lax.axis_size("seq")
        self.other = {"dp": flip(lax.axis_index("dp"), 1)} if across else {}
        self.across = across

    @staticmethod
    def semaphores(pieces, count):
        return [
            pltpu.SemaphoreType.DMA((pieces, count)),
            pltpu.SemaphoreType.DMA((pieces, count)),
            pltpu.SemaphoreType.DMA((pieces,)),
        ]

    @staticmethod
    def where(needed, place, action):
        if needed is None:
            action()
        else:
            pl.when(needed(place))(action)

    def own(self, which):
        source, target = self.pieces[which][:2]
        return pltpu.make_async_copy(source(self.me), target(self.me), self.local.at[which])

    def each_own(self, action):
        for which, piece in enumerate(self.pieces):
            self.where(piece[3], self.me, lambda which=which: action(self.own(which)))

    def start_own(self):
        self.each_own(lambda copy: copy.start())

    def wait_own(self):
        self.each_own(lambda copy: copy.wait())

    def going(self, which, step):
        to = lax.rem(self.me + step, self.count)
        source, target = self.pieces[which][:2]
        return remote(
            source(to),
            target(self.me),
            self.send.at[which, step],
            self.recv.at[which, step],
            {"seq": to, **self.other},
        )

    def origin(self, step):
        return lax.rem(self.me - step + self.count, self.count)

    def each_going(self, step, action):
        to = lax.rem(self.me + step, self.count)
        for which, piece in enumerate(self.pieces):
            self.where(piece[3], to, lambda which=which: action(self.going(which, step)))

    def start(self, step):
        self.each_going(step, lambda copy: copy.start())

    def wait_sent(self, step):
        self.each_going(step, lambda copy: copy.wait_send())

    def wait_arrived(self, step):
        for which, (_, target, arrival, needed) in enumerate(self.pieces):
            block = (arrival or target)(self.origin(step))

            def wait(which=which, block=block):
                remote(
                    block,
                    block,
                    self.send.at[which, step],
                    self.recv.at[which, step],
                    {"seq": self.me},
                ).wait_recv()

            self.where(needed, self.me, wait)


class Channels:
    def __init__(self, width, places):
        tiles = width // LANES
        if places == 8 and tiles == 20:
            half_starts, half_counts = [0, 4, 2, 7], [2, 3, 2, 3]
            self.starts = half_starts + [start + 10 for start in half_starts]
            self.counts = half_counts * 2
        else:
            cuts = [tiles * i // places for i in range(places + 1)]
            self.starts = cuts[:places]
            self.counts = [cuts[i + 1] - cuts[i] for i in range(places)]
        self.places, self.total = places, width
        self.tiles = max(self.counts)
        self.width = self.tiles * LANES
        self.least = self.width - LANES
        per_block = BW // LANES
        lasts = [start + count - 1 for start, count in zip(self.starts, self.counts)]
        reach = [last // per_block - start // per_block + 1 for start, last in zip(self.starts, lasts)]
        self.blocks = max(reach)
        self.span = self.blocks * BW
        firsts = [min(start // per_block, NB - self.blocks) for start in self.starts]
        self.bases = [first * BW for first in firsts]
        self.full = [
            count == self.tiles or last // per_block > first
            for count, last, first in zip(self.counts, lasts, firsts)
        ]
        assert self.full == [count == self.tiles for count in self.counts]
        self.layer, taken = {}, []
        for part in range(2):
            for i in range(places):
                if part and not self.full[i]:
                    self.layer[i, part] = 0
                    continue
                held = {firsts[i]} if part == 0 else set(range(firsts[i] + 1, firsts[i] + self.blocks))
                free = [at for at, blocks in enumerate(taken) if not blocks & held]
                if not free:
                    free = [len(taken)]
                    taken.append(set())
                self.layer[i, part] = free[0]
                taken[free[0]] |= held
        self.taken = taken
        self.shifts = [start * LANES - base for start, base in zip(self.starts, self.bases)]
        assert all(shift + self.width <= self.span for shift in self.shifts)
        self.common = self.least + BW + self.least
        self.lanes = 2 * self.width + self.span

    def pick(self, table, place):
        out = table[0]
        for i in range(1, self.places):
            out = jnp.where(place == i, int(table[i]), out)
        return out

    def begin(self, place):
        return self.pick([start * LANES for start in self.starts], place)

    def base(self, place):
        return self.pick(self.bases, place)

    def layer_of(self, part, place):
        return self.pick([self.layer[i, part] for i in range(self.places)], place)

    def is_full(self, place):
        return self.pick([int(full) for full in self.full], place) == 1

    def owned(self, value, place):
        choices = sorted(set(self.shifts))
        shift = self.pick(self.shifts, place)
        out = value[..., choices[0] : choices[0] + self.width]
        for at in choices[1:]:
            out = jnp.where(shift == at, value[..., at : at + self.width], out)
        return out

    def widened(self, value, place):
        lead = [(0, 0)] * (value.ndim - 1)
        choices = sorted(set(self.shifts))
        shift = self.pick(self.shifts, place)
        out = jnp.pad(value, (*lead, (choices[0], self.span - self.width - choices[0])))
        for at in choices[1:]:
            padded = jnp.pad(value, (*lead, (at, self.span - self.width - at)))
            out = jnp.where(shift == at, padded, out)
        return out

    def mine(self, place):
        count = self.pick(self.counts, place)
        return lax.broadcasted_iota(jnp.int32, (1, self.width), 1) < count * LANES

    def place_in(self, at):
        if at < self.least:
            return "out", at
        if at >= self.lanes - LANES:
            return "out", at - (self.lanes - LANES) + self.least
        return "in", at - self.least

    def line_parts(self):
        common, inputs = self.common - self.least, self.span + self.width
        return [
            ("in", pl.ds(0, common), False),
            ("out", pl.ds(0, self.least), False),
            ("in", pl.ds(common, inputs - common), True),
            ("out", pl.ds(self.least, LANES), True),
        ]

    def rec_of(self, value):
        rec = jnp.concatenate([value[..., :BW], value[..., BW + self.width :]], axis=-1)
        return rec, value[..., BW : BW + self.width]

    def routes(self):
        least, common = self.least, self.common
        return [
            ("out", 0, least, 0, False),
            ("rec", 0, BW, least, False),
            ("gelu", 0, least, least + BW, False),
            ("gelu", least, LANES, common, True),
            ("rec", BW, self.span - BW, common + LANES, True),
            ("out", least, LANES, self.lanes - LANES, True),
        ]


def lanes(start, width):
    return pl.ds(pl.multiple_of(start, LANES) if width % LANES == 0 else start, width)


def opening(chans, arrays, mlps, package, tokens, number):
    seqs, dps, pairs = lax.axis_size("seq"), lax.axis_size("dp"), pair_count()
    plane = plane_bits()
    names = sorted(arrays)
    rows, lines = arrays["rec"].shape[0], package.shape[0]
    cols = mlps[0].shape[1] // (pairs * seqs)
    routes = chans.routes()
    parts = chans.line_parts()
    piece_counts = [len(routes), len(mlps), len(mlps)]
    x_sems = len(Exchange.semaphores(1, seqs))

    def kernel(*refs):
        array_refs, refs = dict(zip(names, refs)), refs[len(names) :]
        mlp_refs, refs = refs[: len(mlps)], refs[len(mlps) :]
        package_ref, tokens_ref, refs = refs[0], refs[1], refs[2:]
        fulls, refs = dict(zip(("in", "out"), refs)), refs[2:]
        mlp_all, shared_all, tokens_all, refs = *refs[:3], refs[3:]
        exchange_sems = [refs[x_sems * i : x_sems * (i + 1)] for i in range(3)]
        refs = refs[3 * x_sems :]
        line_send, line_recv, zeros, zero_sem, refs = *refs[:4], refs[4:]
        me_s, me_d = lax.axis_index("seq"), lax.axis_index("dp")
        is_full = chans.is_full(me_s)

        def route(name, skip, width, at, optional):
            def source(to):
                begin = chans.base(to) if name == "rec" else chans.begin(to)
                return array_refs[name].at[:, lanes(begin + skip, width)]

            which, inside = chans.place_in(at)
            target = lambda origin: fulls[which].at[origin, me_d, :, pl.ds(inside, width)]
            return source, target, target, chans.is_full if optional else None

        move = Exchange([route(*entry) for entry in routes], exchange_sems[0])
        low = lax.rem(me_d, pairs)

        def mlp_piece(which, target_low, here, there):
            return (
                lambda to: mlp_refs[which].at[:, lanes((to * pairs + target_low) * cols, cols)],
                lambda origin: mlp_all.at[origin, here, :, pl.ds(which * cols, cols)],
                lambda origin: mlp_all.at[origin, there, :, pl.ds(which * cols, cols)],
            )

        mlp_moves = [
            Exchange([mlp_piece(which, low, low, low) for which in range(len(mlps))], exchange_sems[1])
        ]
        if pairs == 2:
            mlp_moves.append(
                Exchange(
                    [mlp_piece(which, 1 - low, low, 1 - low) for which in range(len(mlps))],
                    exchange_sems[2],
                    across=True,
                )
            )
        shared = Gathering(plane, package.shape[1], None, shared_all, refs[:3])
        toks = Gathering(plane, tokens.shape[1], tokens_ref, tokens_all, refs[3:6])

        def package_slot(origin):
            return shared_all.at[me_s, pl.ds(pl.multiple_of(origin * lines, 16), lines), :]

        fan = Fan(lambda to: package_ref, package_slot, refs[6:8])
        package_own = pltpu.make_async_copy(package_ref, package_slot(me_d), refs[8])

        def greeted():
            barrier = pltpu.get_barrier_semaphore()
            targets = [{"seq": lax.rem(me_s + step, seqs)} for step in range(1, seqs)]
            targets += [{"dp": lax.rem(me_d + step, dps)} for step in range(1, dps)]
            if pairs == 2:
                targets += [
                    {"seq": lax.rem(me_s + step, seqs), "dp": flip(me_d, 1)}
                    for step in range(1, seqs)
                ]
            for target in targets:
                pl.semaphore_signal(
                    barrier, inc=1, device_id=target, device_id_type=pl.DeviceIdType.MESH
                )
            pl.semaphore_wait(barrier, len(targets))

        greeted()
        package_own.start()
        for step in range(1, dps):
            fan.going(step).start()
        move.start_own()
        for step in range(1, seqs):
            move.start(step)
        optional_parts = [(which, cut) for which, cut, optional in parts if optional]
        blanks = [
            pltpu.make_async_copy(
                zeros.at[:, :, :, pl.ds(0, cut.size)], fulls[which].at[:, :, :, cut], zero_sem.at[i]
            )
            for i, (which, cut) in enumerate(optional_parts)
        ]

        @pl.when(jnp.logical_not(is_full))
        def _():
            zeros[...] = jnp.zeros_like(zeros)
            for blank in blanks:
                blank.start()

        def line_copy(way, part, hop, step, number):
            sign = 1 if way == 0 else -1
            origin = jnp.clip(me_d - sign * hop, 0, dps - 1)
            which, cut, _ = parts[part]
            block = fulls[which].at[move.origin(step), origin, :, cut]
            return remote(
                block,
                block,
                line_send.at[2 * part + way, number, step],
                line_recv.at[2 * part + way, number, step],
                {"dp": jnp.clip(me_d + sign, 0, dps - 1)},
            )

        def has_next(way):
            return me_d < dps - 1 if way == 0 else me_d > 0

        def has_origin(way, hop):
            return me_d >= hop if way == 0 else me_d < dps - hop

        def each_line(test, action):
            for part, (_, _, optional) in enumerate(parts):
                for way in range(2):
                    condition = test(way)
                    if optional:
                        condition = condition & is_full
                    pl.when(condition)(lambda way=way, part=part: action(way, part))

        def pass_on(hop, step):
            each_line(
                lambda way: has_next(way) & has_origin(way, hop),
                lambda way, part: line_copy(way, part, hop, step, hop).start(),
            )

        move.wait_own()
        pass_on(0, 0)

        def first_round(step, carry):
            move.wait_arrived(step)
            pass_on(0, step)
            return carry

        lax.fori_loop(1, seqs, first_round, 0)
        package_own.wait()
        for step in range(1, dps):
            fan.arriving(step).wait_recv()
        shared.begin()
        levels = range(1, len(plane) + 1)
        for size in levels:
            shared.level(size)
        mlp_moves[0].start_own()
        for mlp_move in mlp_moves:
            for step in range(0 if mlp_move.across else 1, seqs):
                mlp_move.start(step)
        toks.begin()
        for hop in range(1, dps):

            def round_of(step, carry, hop=hop):
                each_line(
                    lambda way: has_origin(way, hop),
                    lambda way, part: line_copy(way, part, hop, step, hop - 1).wait_recv(),
                )
                if hop < dps - 1:
                    pass_on(hop, step)
                return carry

            lax.fori_loop(0, seqs, round_of, 0)
            if hop == min(2, dps - 1):
                for size in levels:
                    toks.level(size)

        def last_round(step, carry):
            move.wait_sent(step)
            for mlp_move in mlp_moves:
                mlp_move.wait_sent(step)
                mlp_move.wait_arrived(step)
            return carry

        lax.fori_loop(1, seqs, last_round, 0)
        mlp_moves[0].wait_own()
        if pairs == 2:
            mlp_moves[1].wait_sent(0)
            mlp_moves[1].wait_arrived(0)

        def close_round(step, carry):
            for hop in range(dps - 1):
                each_line(
                    lambda way: has_next(way) & has_origin(way, hop),
                    lambda way, part: line_copy(way, part, hop, step, hop).wait_send(),
                )
            return carry

        lax.fori_loop(0, seqs, close_round, 0)
        for step in range(1, dps):
            fan.going(step).wait_send()

        @pl.when(jnp.logical_not(is_full))
        def _():
            for blank in blanks:
                blank.wait()

        shared.finish()
        toks.finish()

    vmem, anywhere = pl.BlockSpec(memory_space=pltpu.VMEM), pl.BlockSpec(memory_space=pl.ANY)
    return pl.pallas_call(
        kernel,
        out_shape=[
            jax.ShapeDtypeStruct((seqs, dps, rows, chans.span + chans.width), half),
            jax.ShapeDtypeStruct((seqs, dps, rows, chans.width), half),
            jax.ShapeDtypeStruct((seqs, pairs, rows, len(mlps) * cols), half),
            jax.ShapeDtypeStruct((seqs, dps * lines, package.shape[1]), half),
            jax.ShapeDtypeStruct((seqs, *tokens.shape), half),
        ],
        in_specs=[anywhere] * (len(names) + len(mlps)) + [vmem] * 2,
        out_specs=[anywhere] * 5,
        scratch_shapes=[
            *itertools.chain.from_iterable(
                Exchange.semaphores(pieces, seqs) for pieces in piece_counts
            ),
            pltpu.SemaphoreType.DMA((2 * len(parts), max(dps - 1, 1), seqs)),
            pltpu.SemaphoreType.DMA((2 * len(parts), max(dps - 1, 1), seqs)),
            pltpu.VMEM((seqs, dps, rows, chans.span + LANES - BW), half),
            pltpu.SemaphoreType.DMA((len(parts),)),
            *Gathering.semaphores(plane, package.shape[1]),
            *Gathering.semaphores(plane, tokens.shape[1]),
            *Fan.semaphores(dps),
            pltpu.SemaphoreType.DMA,
        ],
        compiler_params=pltpu.CompilerParams(
            collective_id=number, has_side_effects=True, vmem_limit_bytes=63 * 2**20
        ),
        name="opening",
    )(*(arrays[name] for name in names), *mlps, package, tokens)


def closing(chans, in_part, grad_in, grad_out, mlp, mats, small, number):
    seqs, dps, pairs = lax.axis_size("seq"), lax.axis_size("dp"), pair_count()
    plane = plane_bits()
    rows = grad_in.shape[2]
    links = max(dps - 1, 1)
    cols = mlp.shape[3] // MLPS
    routes = chans.routes()
    names = sorted({route[0] for route in routes})
    wide = chans.total
    backs = {"rec": (len(chans.taken), rows, wide), "gelu": (rows, wide), "out": (rows, wide)}
    halves = [pl.ds(0, chans.common), pl.ds(chans.common, chans.lanes - chans.common)]
    piece_counts = [len(routes), MLPS, MLPS]
    x_sems = len(Exchange.semaphores(1, seqs))
    shape = jax.ShapeDtypeStruct
    shared = [(small, fp32), (mats, half)]
    jobs = [(plane, in_part, half), *((plane, value, wire) for value, wire in shared)]
    tall = [value.shape[1] // dps for value, _ in shared]
    s_count = len(Scattering.scratch(plane, in_part, half))

    def kernel(*refs):
        part_ref, in_ref, out_ref, mlp_ref, mats_ref, small_ref, refs = *refs[:6], refs[6:]
        part_out, refs = refs[0], refs[1:]
        back_refs, refs = dict(zip(names, refs)), refs[len(names) :]
        mlp_outs, refs = refs[:MLPS], refs[MLPS:]
        mats_out, small_out, refs = refs[0], refs[1], refs[2:]
        sums, outs, fans_out, fans_in = refs[:2], [small_out, mats_out], refs[2:4], refs[4:6]
        fan_sems, refs = [refs[6:8], refs[8:10]], refs[10:]
        works = []
        for (bits, _, _), x_ref, o_ref in zip(
            jobs, (part_ref, small_ref, mats_ref), (part_out, *sums)
        ):
            works.append(Scattering(bits, x_ref, o_ref, refs[:s_count]))
            refs = refs[s_count:]
        held, outgoing, incoming, totals, load, line_send, line_recv, refs = *refs[:7], refs[7:]
        exchange_sems = [refs[x_sems * i : x_sems * (i + 1)] for i in range(3)]
        me_s, me_d = lax.axis_index("seq"), lax.axis_index("dp")
        is_full = chans.is_full(me_s)

        def route(name, skip, width, at, optional):
            def target(origin):
                if name == "rec":
                    layer = chans.layer_of(int(skip > 0), origin)
                    return back_refs[name].at[layer, :, lanes(chans.base(origin) + skip, width)]
                return back_refs[name].at[:, lanes(chans.begin(origin) + skip, width)]

            return lambda to: totals.at[to, :, pl.ds(at, width)], target, None, optional

        low = lax.rem(me_d, pairs)

        class Owners(Exchange):
            def each_own(self, action):
                for which, piece in enumerate(self.pieces):
                    test = is_full if piece[3] else None
                    self.where(test, None, lambda which=which: action(self.own(which)))

            @staticmethod
            def where(test, place, action):
                if test is None:
                    action()
                else:
                    pl.when(test)(action)

            def each_going(self, step, action):
                for which, piece in enumerate(self.pieces):
                    test = is_full if piece[3] else None
                    self.where(test, None, lambda which=which: action(self.going(which, step)))

            def wait_arrived(self, step):
                origin = self.origin(step)
                for which, (_, target, _, optional) in enumerate(self.pieces):
                    block = target(origin)

                    def wait(which=which, block=block):
                        remote(
                            block,
                            block,
                            self.send.at[which, step],
                            self.recv.at[which, step],
                            {"seq": self.me},
                        ).wait_recv()

                    self.where(chans.is_full(origin) if optional else None, None, wait)

        move = Owners([route(*entry) for entry in routes], exchange_sems[0])

        def mlp_piece(which, source_low, here, there):
            def columns(origin, part):
                return mlp_outs[which].at[:, lanes((origin * pairs + part) * cols, cols)]

            return (
                lambda to: mlp_ref.at[to, source_low, :, pl.ds(which * cols, cols)],
                lambda origin: columns(origin, here),
                lambda origin: columns(origin, there),
            )

        mlp_moves = [
            Exchange([mlp_piece(which, low, low, low) for which in range(MLPS)], exchange_sems[1])
        ]
        if pairs == 2:
            mlp_moves.append(
                Exchange(
                    [mlp_piece(which, 1 - low, low, 1 - low) for which in range(MLPS)],
                    exchange_sems[2],
                    across=True,
                )
            )

        input_lanes = pl.ds(chans.least, chans.lanes - LANES - chans.least)
        out_lanes = [
            (pl.ds(0, chans.least), pl.ds(0, chans.least)),
            (pl.ds(chans.least, LANES), pl.ds(chans.lanes - LANES, LANES)),
        ]

        def loading(chunk):
            copies = [(in_ref.at[chunk], held.at[chunk, :, :, input_lanes])]
            copies += [
                (out_ref.at[chunk, :, :, source], held.at[chunk, :, :, target])
                for source, target in out_lanes
            ]
            return [
                pltpu.make_async_copy(source, target, load.at[which, chunk])
                for which, (source, target) in enumerate(copies)
            ]

        fans = [
            Fan(
                lambda to, ref=fans_out[i]: ref.at[to],
                lambda origin, ref=fans_in[i]: ref.at[origin],
                fan_sems[i],
            )
            for i in range(2)
        ]

        def fan_lines(which, block, line):
            chunk = 16
            return pl.ds(pl.multiple_of(block * tall[which] + line * chunk, chunk), chunk)

        def fan_send():
            for which in range(2):
                for step in range(1, dps):
                    to = lax.rem(me_d + step, dps)

                    def body(line, carry, which=which, to=to):
                        part = sums[which][fan_lines(which, to, line), :]
                        fans_out[which][to, fan_lines(which, 0, line), :] = part.astype(
                            fans_out[which].dtype
                        )
                        return carry

                    lax.fori_loop(0, tall[which] // 16, body, 0)
                    fans[which].going(step).start()

        def fan_total():
            for which in range(2):
                for step in range(1, dps):
                    fans[which].arriving(step).wait_recv()

                def body(line, carry, which=which):
                    total = sums[which][fan_lines(which, me_d, line), :]
                    for step in range(1, dps):
                        origin = lax.rem(me_d - step + dps, dps)
                        part = fans_in[which][origin, fan_lines(which, 0, line), :]
                        total = total + part.astype(fp32)
                    outs[which][fan_lines(which, 0, line), :] = total
                    return carry

                lax.fori_loop(0, tall[which] // 16, body, 0)
                for step in range(1, dps):
                    fans[which].going(step).wait_send()

        def chunk_of(step):
            return lax.rem(me_s + step, seqs)

        for step in range(seqs):
            for copy in loading(chunk_of(step)):
                copy.start()
        for work in works:
            work.begin()
        barrier = pltpu.get_barrier_semaphore()
        targets = [{"seq": lax.rem(me_s + step, seqs)} for step in range(1, seqs)]
        targets += [{"dp": lax.rem(me_d + step, dps)} for step in range(1, dps)]
        if pairs == 2:
            targets += [
                {"seq": lax.rem(me_s + step, seqs), "dp": flip(me_d, 1)} for step in range(1, seqs)
            ]
        for target in targets:
            pl.semaphore_signal(
                barrier, inc=1, device_id=target, device_id_type=pl.DeviceIdType.MESH
            )
        pl.semaphore_wait(barrier, len(targets))

        def behind(way):
            return me_d > 0 if way == 0 else me_d < dps - 1

        def target_of(way, hop):
            sign = 1 if way == 0 else -1
            return jnp.clip(me_d + sign * hop, 0, dps - 1)

        def has_target(way, hop):
            return me_d < dps - hop if way == 0 else me_d >= hop

        def line_copy(way, part, hop, chunk):
            return remote(
                outgoing.at[way, hop % 2, chunk, :, halves[part]],
                incoming.at[way, hop - 1, chunk, :, halves[part]],
                line_send.at[2 * part + way, hop - 1, chunk],
                line_recv.at[2 * part + way, hop - 1, chunk],
                {"dp": target_of(way, 1)},
            )

        def combine(store, terms):
            def body(step, carry):
                lines = pl.ds(pl.multiple_of(step * 16, 16), 16)
                total = terms[0](lines)
                for term in terms[1:]:
                    total = total + term(lines)
                store(lines, total)
                return carry

            lax.fori_loop(0, rows // 16, body, 0)

        def own_term(part, chunk, block):
            return lambda lines: held[chunk, block, lines, halves[part]]

        def far_term(part, way, hop, chunk):
            return lambda lines: incoming[way, hop - 1, chunk, lines, halves[part]].astype(fp32)

        def each_line(test, action):
            for part in range(2):
                for way in range(2):
                    condition = test(way)
                    if part == 1:
                        condition = condition & is_full
                    pl.when(condition)(lambda way=way, part=part: action(way, part))

        def line_round(hop, first):
            def body(step, carry):
                chunk = chunk_of(step)
                if first:
                    for copy in loading(chunk):
                        copy.wait()
                if hop + 2 < dps:
                    each_line(
                        lambda way: has_target(way, hop + 2),
                        lambda way, part: line_copy(way, part, hop + 2, chunk).wait_send(),
                    )

                def send(way, part, far):
                    def keep(lines, total):
                        outgoing[way, hop % 2, chunk, lines, halves[part]] = total.astype(half)

                    terms = [own_term(part, chunk, target_of(way, hop))]
                    if far:
                        line_copy(way, part, hop + 1, chunk).wait_recv()
                        terms.append(far_term(part, way, hop + 1, chunk))
                    combine(keep, terms)
                    line_copy(way, part, hop, chunk).start()

                if hop == dps - 1:
                    each_line(
                        lambda way: has_target(way, hop), lambda way, part: send(way, part, False)
                    )
                else:
                    each_line(
                        lambda way: has_target(way, hop) & behind(way),
                        lambda way, part: send(way, part, True),
                    )
                    each_line(
                        lambda way: has_target(way, hop) & jnp.logical_not(behind(way)),
                        lambda way, part: send(way, part, False),
                    )
                return carry

            lax.fori_loop(0, seqs, body, 0)

        def line_total(step, carry):
            chunk = chunk_of(step)
            if dps == 1:
                for copy in loading(chunk):
                    copy.wait()
            for part in range(2):
                for ups, downs in ((True, True), (True, False), (False, True), (False, False)):
                    condition = behind(0) if ups else jnp.logical_not(behind(0))
                    condition &= behind(1) if downs else jnp.logical_not(behind(1))
                    if part == 1:
                        condition &= is_full

                    @pl.when(condition)
                    def _():
                        def keep(lines, total):
                            totals[chunk, lines, halves[part]] = total.astype(half)

                        terms = [own_term(part, chunk, me_d)]
                        for way in [way for way, far in ((0, ups), (1, downs)) if far and dps > 1]:
                            line_copy(way, part, 1, chunk).wait_recv()
                            terms.append(far_term(part, way, 1, chunk))
                        combine(keep, terms)

            @pl.when(step > 0)
            def _():
                move.start(step)

            @pl.when(step == 0)
            def _():
                move.start_own()

            return carry

        depth = len(plane)
        first_total = max(dps - 2, 0)
        for turn in range(max(depth, dps - 1)):
            if turn < dps - 1:
                line_round(dps - 1 - turn, turn == 0)
            if turn == 0:
                for work in works[1:]:
                    for stage in range(depth):
                        work.stage(stage)
                    work.finish()
                fan_send()
                mlp_moves[0].start_own()
                for mlp_move in mlp_moves:
                    for step in range(0 if mlp_move.across else 1, seqs):
                        mlp_move.start(step)
            if turn == first_total:
                lax.fori_loop(0, seqs, line_total, 0)
            if turn < depth:
                works[0].stage(turn)
        works[0].finish()
        fan_total()

        def last_round(step, carry):
            for each in [move, *mlp_moves]:
                each.wait_arrived(step)
                each.wait_sent(step)
            return carry

        lax.fori_loop(1, seqs, last_round, 0)
        move.wait_own()
        mlp_moves[0].wait_own()
        if pairs == 2:
            mlp_moves[1].wait_arrived(0)
            mlp_moves[1].wait_sent(0)

        def close_round(step, carry):
            for hop in range(1, min(dps, 3)):
                each_line(
                    lambda way: has_target(way, hop),
                    lambda way, part: line_copy(way, part, hop, step).wait_send(),
                )
            return carry

        lax.fori_loop(0, seqs, close_round, 0)
        for work in works:
            work.close()

    vmem, anywhere = pl.BlockSpec(memory_space=pltpu.VMEM), pl.BlockSpec(memory_space=pl.ANY)
    results = pl.pallas_call(
        kernel,
        out_shape=[
            shape(in_part.shape[1:], fp32),
            *(shape(backs[name], half) for name in names),
            *[shape((rows, seqs * pairs * cols), half)] * MLPS,
            shape((tall[1], mats.shape[2]), fp32),
            shape((tall[0], small.shape[2]), fp32),
        ],
        in_specs=[anywhere, anywhere, anywhere, vmem, anywhere, anywhere],
        out_specs=[vmem, *[anywhere] * (len(names) + MLPS), vmem, vmem],
        scratch_shapes=[
            *(pltpu.VMEM(value.shape[1:], fp32) for value, _ in shared),
            *(
                pltpu.VMEM((dps, lines, value.shape[2]), wire)
                for _ in range(2)
                for (value, wire), lines in zip(shared, tall)
            ),
            *(Fan.semaphores(dps) * 2),
            *itertools.chain.from_iterable(
                Scattering.scratch(bits, value, wire) for bits, value, wire in jobs
            ),
            pltpu.VMEM((seqs, dps, rows, chans.lanes), fp32),
            pltpu.VMEM((2, 2, seqs, rows, chans.lanes), half),
            pltpu.VMEM((2, links, seqs, rows, chans.lanes), half),
            pltpu.VMEM((seqs, rows, chans.lanes), half),
            pltpu.SemaphoreType.DMA((3, seqs)),
            pltpu.SemaphoreType.DMA((4, links, seqs)),
            pltpu.SemaphoreType.DMA((4, links, seqs)),
            *itertools.chain.from_iterable(
                Exchange.semaphores(pieces, seqs) for pieces in piece_counts
            ),
        ],
        compiler_params=pltpu.CompilerParams(
            collective_id=number, has_side_effects=True, vmem_limit_bytes=63 * 2**20
        ),
        name="closing",
    )(in_part, grad_in, grad_out, mlp, mats, small)
    backs = dict(zip(names, results[1:]))
    return results[0], backs, *results[1 + len(names) :]


SUBLANES = 8


def scan_kernel(forward, decay_ref, other_ref, out_ref):
    steps, width = decay_ref.shape
    tiles = steps // SUBLANES
    row = lax.broadcasted_iota(jnp.int32, (SUBLANES, width), 0)

    def tile(step, carry):
        at = step if forward else tiles - 1 - step
        lines = pl.ds(pl.multiple_of(at * SUBLANES, SUBLANES), SUBLANES)
        decay, other = decay_ref[lines, :], other_ref[lines, :]
        product, total = decay, other if forward else decay * other
        for reach in (1, 2, 4):
            shift = reach if forward else SUBLANES - reach
            inside = row >= reach if forward else row < SUBLANES - reach
            total = jnp.where(inside, product * pltpu.roll(total, shift, 0) + total, total)
            product = jnp.where(inside, product * pltpu.roll(product, shift, 0), product)
        total = product * carry + total
        if forward:
            out_ref[lines, :] = total
            last = total[SUBLANES - 1 :]
        else:
            after = jnp.where(row == SUBLANES - 1, carry, pltpu.roll(total, SUBLANES - 1, 0))
            out_ref[lines, :] = other + after
            last = total[:1]
        return jnp.broadcast_to(last, (SUBLANES, width))

    lax.fori_loop(0, tiles, tile, jnp.zeros((SUBLANES, width), fp32), unroll=4)


def time_scan(forward, decays, other):
    vmem = pl.BlockSpec(memory_space=pltpu.VMEM)
    return pl.pallas_call(
        functools.partial(scan_kernel, forward),
        out_shape=jax.ShapeDtypeStruct(decays.shape, fp32),
        in_specs=[vmem, vmem],
        out_specs=vmem,
        name="forward_scan" if forward else "backward_scan",
    )(decays, other)


def swap(value, axis, mask):
    return lax.ppermute(value, axis, [(i, i ^ mask) for i in range(lax.axis_size(axis))])


def far_masks(axis):
    mask, masks = pair_count(), []
    while mask < lax.axis_size(axis):
        masks.append(mask)
        mask *= 2
    return masks


def share_gather(value, axis):
    me = lax.axis_index(axis)
    for mask in far_masks(axis):
        other = swap(value, axis, mask)
        low = (me // mask) % 2 == 0
        value = jnp.concatenate(
            [jnp.where(low, value, other), jnp.where(low, other, value)], axis=1
        )
    return value


def share_scatter(value, axis):
    pairs = pair_count()
    sources, count, rows, width = value.shape
    groups = [list(range(low, count, pairs)) for low in range(pairs)]
    value = value.reshape(sources, count // pairs, pairs, rows, width)
    return lax.psum_scatter(value, axis, scatter_dimension=1, axis_index_groups=groups)


def rms_norm(values, gain_vec):
    return (
        values * lax.rsqrt(jnp.mean(values * values, axis=-1, keepdims=True) + norm_eps) * gain_vec
    )


def gate_terms(gate_rec, gate_inp, conv_val, rec_vals):
    recur_gate = jax.nn.sigmoid(gate_rec)
    admit_gate = jax.nn.sigmoid(gate_inp)
    log_decay = -gate_power * recur_gate * jax.nn.softplus(-rec_vals)
    decays = jnp.exp(log_decay)
    scaler = jnp.sqrt(jnp.maximum(-jnp.expm1(2.0 * log_decay), floor_square))
    return (decays, scaler * admit_gate * conv_val)


def contract_rows(left, right):
    return lax.dot_general(left, right, (((0,), (0,)), ((), ())), preferred_element_type=fp32)


def times_trans(left, right):
    return lax.dot_general(left, right, (((1,), (1,)), ((), ())), preferred_element_type=fp32)


def part_of_sum(left, right):
    return times_trans(left, right).astype(half)


def times(left, right):
    return jnp.dot(left, right, preferred_element_type=fp32)


def gelu_product(first, second):
    return jax.nn.gelu(first, approximate=True) * second


def on_device(
    tokens,
    valid_mask,
    teacher,
    norm_one,
    proj_gelu,
    proj_rec,
    conv_taps,
    conv_bias,
    gate_rec_w,
    gate_rec_b,
    gate_inp_w,
    gate_inp_b,
    rec_param,
    proj_out,
    norm_two,
    mlp_gate,
    mlp_up,
    mlp_down,
):
    seqs, dps = lax.axis_size("seq"), lax.axis_size("dp")
    everyone = seqs * dps
    me_seq = lax.axis_index("seq")
    local_len, model = tokens.shape[-2:]
    rec_width = proj_rec.shape[1]
    hidden_width = mlp_gate.shape[1]
    rows_w = proj_rec.shape[0]
    rows_c = gate_rec_w.shape[0]
    steps = seqs * local_len

    plane, cube, pairs = plane_bits(), cube_bits(), pair_count()

    chans = Channels(rec_width, seqs)
    width_r, span, span_blocks = chans.width, chans.span, chans.blocks
    base = chans.base(me_seq)
    cols = hidden_width // (pairs * seqs)

    mask_val = valid_mask.reshape(local_len).astype(fp32)
    own_count = jnp.sum(mask_val)
    count_high = jnp.floor(own_count / 128.0)
    count_pair = jnp.stack([count_high, own_count - 128.0 * count_high]).astype(half)

    def row_of(value):
        return jnp.pad(value, ((0, 0), (0, 2 * BW - value.shape[1])))

    block_rows = -(-rows_c // 16) * 16
    package = jnp.concatenate(
        [
            jnp.pad(
                jnp.concatenate([gate_rec_w, gate_inp_w], axis=1),
                ((0, block_rows - rows_c), (0, 0)),
            ),
            row_of(conv_taps),
            row_of(jnp.stack([conv_bias, gate_rec_b, gate_inp_b, rec_param])),
            row_of(jnp.stack([norm_one, norm_two])),
            row_of(count_pair[None, :]),
            jnp.zeros((5, 2 * BW), half),
        ],
        axis=0,
    )
    w_in, w_out, mlp_own, shared, tokens_all = opening(
        chans,
        {"rec": proj_rec, "gelu": proj_gelu, "out": proj_out.T},
        [mlp_gate, mlp_up, mlp_down.T],
        package,
        tokens.reshape(local_len, model),
        1,
    )
    shared = shared.reshape(everyone, *package.shape)
    w_in, w_out = w_in.reshape(model, span + width_r), w_out.reshape(model, width_r)
    w_mlp = share_gather(mlp_own, "dp").reshape(model, 3 * cols)
    w_two, w_down = w_mlp[:, : 2 * cols], w_mlp[:, 2 * cols :]
    blocks_all = shared[:, :rows_c].reshape(rec_width, 2 * BW)
    vectors = shared[:, block_rows:].astype(fp32)
    channel_vecs = vectors[:, : CONV + 4, :rows_c].transpose(1, 0, 2).reshape(CONV + 4, rec_width)
    gains = vectors[:, CONV + 4 : CONV + 6, :rows_w].transpose(1, 0, 2).reshape(2, model)
    counts = jnp.sum(vectors[:, CONV + 6, :2], axis=0)
    valid_total = 128.0 * counts[0] + counts[1]

    span_vecs = lax.dynamic_slice(channel_vecs, (0, base), (CONV + 4, span))
    tap_vals, bias_vals = span_vecs[:CONV], span_vecs[CONV]
    rec_bias, inp_bias, rec_vals = (
        chans.owned(span_vecs[CONV + 1 + i], me_seq) for i in range(3)
    )
    mine = chans.mine(me_seq)
    span_mats = lax.dynamic_slice(blocks_all, (base, 0), (span, 2 * BW))

    def block_diagonal(value):
        rows = []
        for place in range(span_blocks):
            block = value[place * BW : (place + 1) * BW]
            rows.append(jnp.pad(block, ((0, 0), (place * BW, (span_blocks - 1 - place) * BW))))
        return chans.owned(jnp.concatenate(rows, axis=0), me_seq)

    w_gates = jnp.concatenate(
        [block_diagonal(span_mats[:, :BW]), block_diagonal(span_mats[:, BW:])], axis=1
    )
    gain_one, gain_two = gains[0], gains[1]

    flat_in = tokens.reshape(local_len, model).astype(fp32)
    tokens_all = tokens_all.reshape(steps, model).astype(fp32)
    normed_all = rms_norm(tokens_all, gain_one).astype(half)
    pre = times(normed_all, w_in)
    rec_pre, gelu_pre = chans.rec_of(pre)
    padded = jnp.concatenate([jnp.zeros((CONV - 1, span), fp32), rec_pre], axis=0)
    conv_sum = bias_vals + jnp.zeros_like(rec_pre)
    for offset in range(CONV):
        conv_sum = conv_sum + tap_vals[offset] * padded[CONV - 1 - offset : CONV - 1 - offset + steps]
    conv_low = conv_sum.astype(half)
    conv_val = chans.owned(conv_low, me_seq).astype(fp32)
    gates = times(conv_low, w_gates)
    gate_rec = gates[:, :width_r] + rec_bias
    gate_inp = gates[:, width_r:] + inp_bias
    decays, drives = gate_terms(gate_rec, gate_inp, conv_val, rec_vals)
    states = time_scan(True, decays, drives)
    mixed_low = jnp.where(mine, gelu_product(gelu_pre, states), 0.0).astype(half)
    mixed_part = part_of_sum(mixed_low, w_out).reshape(seqs, local_len, model)
    middle = flat_in + scatter_sum(mixed_part, plane, 3)

    normed_two_low = rms_norm(middle, gain_two).astype(half)
    group = pairs * seqs
    tall = group * local_len
    normed_two_all = gather(normed_two_low, cube, 4).reshape(tall, model)
    pre_two = times(normed_two_all, w_two)
    gate_pre, up_pre = pre_two[:, :cols], pre_two[:, cols:]
    hidden_low = gelu_product(gate_pre, up_pre).astype(half)
    down_part = part_of_sum(hidden_low, w_down).reshape(group, local_len, model)
    result = middle + scatter_sum(down_part, cube, 5)
    differ = result - teacher.reshape(local_len, model).astype(fp32)
    own_loss = 0.5 * jnp.sum(mask_val[:, None] * differ * differ)
    token_total = local_len * everyone
    grad_result = mask_val[:, None] * (token_total / valid_total) * differ
    output = result.reshape(tokens.shape).astype(half)

    down_all = gather(grad_result.astype(half), cube, 6).reshape(tall, model)
    grad_down = contract_rows(down_all, hidden_low)
    grad_hidden = times(down_all, w_down)
    _, pull_mlp = jax.vjp(gelu_product, gate_pre, up_pre)
    two_low = jnp.concatenate(pull_mlp(grad_hidden), axis=1).astype(half)
    grad_two = contract_rows(normed_two_all, two_low)
    two_part = part_of_sum(two_low, w_two).reshape(group, local_len, model)

    grad_normed_two = scatter_sum(two_part, cube, 7)
    grad_normed_two, grad_two, grad_down = lax.optimization_barrier(
        (grad_normed_two, grad_two, grad_down)
    )
    grad_mlp = jnp.concatenate([grad_two, grad_down], axis=1).astype(half)
    sent_mlp = share_scatter(grad_mlp.reshape(seqs, dps, rows_w, 3 * cols), "dp")

    _, pull_norm_two = jax.vjp(rms_norm, middle, gain_two)
    grad_middle_norm, grad_norm_two = pull_norm_two(grad_normed_two)
    grad_middle = grad_result + grad_middle_norm

    middle_low = gather(grad_middle.astype(half), plane, 8).reshape(steps, model)
    grad_out = contract_rows(middle_low, mixed_low)
    grad_mixed = jnp.where(mine, times(middle_low, w_out), 0.0)
    _, pull_mix = jax.vjp(gelu_product, gelu_pre, states)
    grad_gelu_pre, grad_states = pull_mix(grad_mixed)
    adjoint = time_scan(False, decays, grad_states)
    prior_state = jnp.concatenate([jnp.zeros_like(states[:1]), states[:-1]], axis=0)
    _, pull_gates = jax.vjp(gate_terms, gate_rec, gate_inp, conv_val, rec_vals)
    grad_rec_gate, grad_inp_gate, grad_conv_direct, grad_rec_param = pull_gates(
        (adjoint * prior_state, adjoint)
    )
    gates_low = jnp.concatenate([grad_rec_gate, grad_inp_gate], axis=1).astype(half)
    grad_gate_bias = jnp.sum(gates_low.astype(fp32), axis=0)
    grad_gates = contract_rows(conv_low, gates_low)
    grad_conv = times_trans(gates_low, w_gates) + chans.widened(grad_conv_direct, me_seq)
    grad_conv_bias = jnp.sum(grad_conv, axis=0)
    ahead = jnp.concatenate([grad_conv, jnp.zeros((CONV - 1, span), fp32)], axis=0)
    tap_grads = []
    rec_back = jnp.zeros_like(grad_conv)
    for offset in range(CONV):
        window = padded[CONV - 1 - offset : CONV - 1 - offset + steps]
        tap_grads.append(jnp.sum(grad_conv * window, axis=0))
        rec_back = rec_back + tap_vals[offset] * ahead[offset : offset + steps]
    rec_low = rec_back.astype(half)
    in_low = jnp.concatenate(
        [rec_low[:, :BW], grad_gelu_pre.astype(half), rec_low[:, BW:]], axis=1
    )
    grad_in = contract_rows(normed_all, in_low)
    in_part = part_of_sum(in_low, w_in).reshape(seqs, local_len, model)
    grad_norm_one = jnp.sum(w_in.astype(fp32) * grad_in, axis=1) / gain_one

    def spread(value):
        return lax.dynamic_update_slice(
            jnp.zeros((value.shape[0], rec_width), fp32), value, (0, base)
        )

    def diagonal_blocks(value):
        wide = chans.widened(value, me_seq)
        block = lax.broadcasted_iota(jnp.int32, (span, BW), 0) // BW
        picked = wide[:, :BW]
        for i in range(1, span_blocks):
            picked = jnp.where(block == i, wide[:, i * BW : (i + 1) * BW], picked)
        return picked

    mats = jnp.concatenate(
        [diagonal_blocks(grad_gates[:, :width_r]), diagonal_blocks(grad_gates[:, width_r:])], axis=1
    )
    mats = lax.dynamic_update_slice(jnp.zeros((rec_width, 2 * BW), fp32), mats, (base, 0))
    mats = jnp.pad(
        mats.reshape(everyone, rows_c, 2 * BW), ((0, 0), (0, block_rows - rows_c), (0, 0))
    )

    def widen(value):
        return chans.widened(value[None, :], me_seq)

    lines = jnp.concatenate(
        [
            jnp.stack(tap_grads),
            grad_conv_bias[None, :],
            widen(grad_gate_bias[:width_r]),
            widen(grad_gate_bias[width_r:]),
            widen(grad_rec_param),
        ],
        axis=0,
    )
    lines = spread(lines).reshape(CONV + 4, everyone, rows_c).transpose(1, 0, 2)
    gain_lines = jnp.stack([grad_norm_one, grad_norm_two]).reshape(2, everyone, rows_w)
    gain_lines = gain_lines.transpose(1, 0, 2)

    def lane_pad(value):
        return jnp.pad(value, ((0, 0), (0, 0), (0, LANES - value.shape[2])))

    small = jnp.concatenate(
        [
            lane_pad(lines),
            lane_pad(gain_lines),
            jnp.full((everyone, 1, LANES), own_loss),
            jnp.zeros((everyone, 5, LANES), fp32),
        ],
        axis=1,
    )
    grad_normed, backs, out_gate, out_up, out_down, mats, small = closing(
        chans,
        in_part,
        grad_in.reshape(seqs, dps, rows_w, span + width_r),
        grad_out.reshape(seqs, dps, rows_w, width_r),
        sent_mlp,
        mats.astype(half).reshape(seqs, -1, 2 * BW),
        small.reshape(seqs, -1, LANES),
        2,
    )
    mean_loss = small[CONV + 6, 0] / (valid_total * model)

    _, pull_norm_one = jax.vjp(lambda values: rms_norm(values, gain_one), flat_in)
    grad_tokens = (grad_middle + pull_norm_one(grad_normed)[0]).reshape(tokens.shape).astype(half)

    block_of = lax.broadcasted_iota(jnp.int32, (1, rec_width), 1) // BW

    def layer_sum(at, blocks):
        has = functools.reduce(jnp.logical_or, [block_of == block for block in sorted(blocks)])
        return jnp.where(has, backs["rec"][at].astype(fp32), 0.0)

    out_gate, out_up = out_gate.astype(fp32), out_up.astype(fp32)
    out_down = out_down.T.astype(fp32)
    out_proj_out = backs["out"].T.astype(fp32)
    out_proj_gelu = backs["gelu"].astype(fp32)
    layers = [layer_sum(at, blocks) for at, blocks in enumerate(chans.taken)]
    out_proj_rec = functools.reduce(jnp.add, layers)

    return (
        output,
        mean_loss,
        grad_tokens,
        small[CONV + 4, :rows_w],
        out_proj_gelu,
        out_proj_rec,
        small[:CONV, :rows_c],
        small[CONV, :rows_c],
        mats[:rows_c, :BW],
        small[CONV + 1, :rows_c],
        mats[:rows_c, BW:],
        small[CONV + 2, :rows_c],
        small[CONV + 3, :rows_c],
        out_proj_out,
        small[CONV + 5, :rows_w],
        out_gate,
        out_up,
        out_down,
    )


def solution(mesh):
    both = ("seq", "dp")
    rows, cols, flat = P(both, None), P(None, both), P(both)
    acts = P("dp", "seq", None)
    in_specs = (
        acts,
        P("dp", "seq"),
        acts,
        flat,
        rows,
        rows,
        cols,
        flat,
        rows,
        flat,
        rows,
        flat,
        flat,
        cols,
        flat,
        rows,
        rows,
        cols,
    )
    out_specs = (
        acts,
        P(),
        acts,
        flat,
        rows,
        rows,
        cols,
        flat,
        rows,
        flat,
        rows,
        flat,
        flat,
        cols,
        flat,
        rows,
        rows,
        cols,
    )
    return jax.shard_map(
        on_device, mesh=mesh, in_specs=in_specs, out_specs=out_specs, check_vma=False
    )
```

time: 854 us -> 694 us (0.81); the launches traced: 840 us -> 690 us
  waiting for transfers between devices: 99.7 us -> 17.8 us
  local copies, waits for them, and re-layouts: 105 us -> 42.3 us
  between operations: 7.84 us -> 20.5 us
  matrix products: 103 us -> 93.6 us
    ppermute x6 -> x1, waiting for transfers between devices: 99.7 us -> 0.01 us  [swap(): lax.ppermute(value, axis, [(i, i ^ mask) for i in range(lax.axis_size(axi...]
    pallas_call x3, Pallas kernels: 146 us -> 122 us  [the longest x1 112 us: opening(): pl.pallas_call(kernel, out_shape=[jax.ShapeDtypeStruct((seqs, dps, rows,...]
    slice x23 -> x4, local copies, waits for them, and re-layouts: 19.2 us -> 1.39 us  [the longest x1 1.08 us: on_device(): vectors = shared[:, block_rows:].astype(fp32)]
    reduce_scatter x0 -> x1, waiting for transfers between devices: none -> 17.7 us  [share_scatter(): lax.psum_scatter(value, axis, scatter_dimension=1, axis_index_groups=groups)]
    convert_element_type x8 -> x0, local copies, waits for them, and re-layouts: 16.8 us -> none  [the longest x4 9.33 us: on_device(): out_gate, out_up = (out_gate.astype(fp32), out_up.astype(fp32))]
    pallas_call x3, Pallas kernels: 92 us -> 108 us  [gather(): pl.pallas_call(kernel, out_shape=jax.ShapeDtypeStruct((2 ** len(bits), ro...]
    squeeze x6 -> x0, local copies, waits for them, and re-layouts: 9.97 us -> none  [the longest x4 7.88 us: block(): lax.dynamic_index_in_dim(v, where, axis=1, keepdims=False)]
  transfers between devices with their start and end apart: 6 -> 2, of which waited for: 4 -> 1; matrix products, arithmetic and copies ran while one was open for 11% -> 14% of each run, Pallas kernels for 8% -> 15%
where the time goes in v2:
time: 694 us; the launch traced here: 690 us
  Pallas kernels  445 us (64%)
  matrix products  93.6 us (13%)
  other arithmetic  65.4 us (9%)
  local copies, waits for them, and re-layouts  42.3 us (6%)
  between operations  20.5 us (3%)
  waiting for transfers between devices  17.8 us (3%)
    pallas_call x1, Pallas kernels, closing(): pl.pallas_call(kernel, out_shape=[shape(in_part.shape[1:], fp32), *(shape...  123 us
    pallas_call x1, Pallas kernels, opening(): pl.pallas_call(kernel, out_shape=[jax.ShapeDtypeStruct((seqs, dps, rows,...  112 us
    pallas_call x3, Pallas kernels, gather(): pl.pallas_call(kernel, out_shape=jax.ShapeDtypeStruct((2 ** len(bits), ro...  108 us
    pallas_call x3, Pallas kernels, scatter_sum(): pl.pallas_call(kernel, out_shape=jax.ShapeDtypeStruct((rows, width), fp32...  92.5 us
    dot_general x5, matrix products, contract_rows(): lax.dot_general(left, right, (((0,), (0,)), ((), ())), preferred_element_...  33.1 us
    dot_general x5, matrix products, times(): return jnp.dot(left, right, preferred_element_type=fp32)  31.2 us
    dot_general x5, matrix products, times_trans(): lax.dot_general(left, right, (((1,), (1,)), ((), ())), preferred_element_...  29.4 us
    reduce_scatter x1, waiting for transfers between devices, share_scatter(): lax.psum_scatter(value, axis, scatter_dimension=1, axis_index_groups=groups)  17.7 us
  transfers between devices with their start and end apart: 2, of which 1 were waited for; matrix products, arithmetic and copies ran while one was open for 14% of the time, Pallas kernels for 15%

profile of v2, /device:TPU:11, one launch (start us, length us, event | category | flops | bytes accessed | tf_op | source)
XLA Modules:
  0.0 690.4 jit_solution(5314476914630709422)
XLA Ops:
  7.2 1.3 convert_reduce_fusion.1
  12.8 1.9 concatenate.69.refs_6_
  14.7 111.9 %opening.1 = (bf16[8,4,64,896]{3,2,1,0:T(8,128)(2,1)}, bf16[8,4,64,384]{3,2,1,0:T(8,128)(2,1)}, bf16[8,2,64,1152]{3,2,1,0:T(8,128)(2,1)}, bf16[8,384,512]{2,1,0:T(8,128)(2,1)}, bf16[8,128,2048]{2,1,0:T(8,128)(2,1)}) custom-call(bf16[64,2560]{1,0:T(8,128)(2,1)} %refs_0_.1, bf16[64,2560]{1,0:T(8,128)(2,1)} %bitcast.166, bf16[64,2560]{1,0:T(8,128)(2,1)} %refs_2_.1, ...), custom_call_target="tpu_custom_call" | custom-call | tf_op jit(solution)/shard_map/opening/pallas_call | solution.py:753
  126.5 5.6 collective-permute-start
  132.2 1.1 slice.311
  134.6 3.5 slice.318
  138.7 3.2 multiply_reduce_fusion
  142.6 1.0 multiply_convert_fusion
  143.6 1.0 copy-done.76
  144.6 4.5 fusion.123
  149.1 1.8 copy-done.22
  151.3 1.7 constant_dynamic-slice_fusion.1
  156.7 1.0 add_convert_fusion.1
  157.8 1.0 fusion.54
  158.8 3.8 convert_multiply_fusion.1
  162.6 5.0 forward_scan.1
  167.6 2.6 select_convert_fusion
  170.2 4.4 convolution_convert_fusion.2
  174.6 20.8 %scatter_3.1 = f32[128,2048]{1,0:T(8,128)} custom-call(bf16[8,128,2048]{2,1,0:T(8,128)(2,1)} %bitcast.154), custom_call_target="tpu_custom_call" | custom-call | tf_op jit(solution)/shard_map/scatter_3/pallas_call | solution.py:327
  196.2 1.6 multiply_reduce_fusion.9
  199.7 50.6 %gather_4.1 = bf16[16,128,2048]{2,1,0:T(8,128)(2,1)} custom-call(bf16[128,2048]{1,0:T(8,128)(2,1)} %multiply_convert_fusion.3.x_ref), custom_call_target="tpu_custom_call" | custom-call | tf_op jit(solution)/shard_map/gather_4/pallas_call | solution.py:304
  253.6 1.2 convert_bitcast_fusion.3
  255.4 5.3 fusion.1
  260.8 2.3 broadcast_select_fusion.1
  263.1 2.9 pad_maximum_fusion
  265.9 1.2 slice-done.1
  267.1 9.1 %fusion.10 = f32[2048,768]{0,1:T(8,128)S(1)} fusion(bf16[2048,2048]{1,0:T(8,128)(2,1)S(1)} %bitcast.139, bf16[2048,1152]{1,0:T(8,128)(2,1)} %bitcast.147), kind=kOutput, calls=%fused_computation.27 | convolution fusion | flops 6442450944 | bytes 17825792 | tf_op jit(solution)/shard_map/dot_general | solution.py:1283
  276.3 1.1 multiply_convert_fusion.2
  277.4 1.5 copy-done.16
  278.9 8.7 %convolution_convert_fusion.1 = bf16[2048,2048]{1,0:T(8,128)(2,1)} fusion(bf16[2048,384]{0,1:T(8,128)(2,1)S(1)} %multiply_convert_fusion.2, bf16[2048,1152]{1,0:T(8,128)(2,1)} %bitcast.148), kind=kOutput, calls=%fused_computation.6 | convolution fusion | flops 3225419776 | bytes 11534336 | tf_op jit(solution)/shard_map/dot_general | solution.py:1275
  287.7 37.7 %scatter_5.1 = f32[128,2048]{1,0:T(8,128)} custom-call(bf16[16,128,2048]{2,1,0:T(8,128)(2,1)} %bitcast.136), custom_call_target="tpu_custom_call" | custom-call | tf_op jit(solution)/shard_map/scatter_5/pallas_call | solution.py:327
  325.4 2.5 multiply_convert_fusion.4.x_ref
  327.9 33.9 %gather_6.1 = bf16[16,128,2048]{2,1,0:T(8,128)(2,1)} custom-call(bf16[128,2048]{1,0:T(8,128)(2,1)} %multiply_convert_fusion.4.x_ref), custom_call_target="tpu_custom_call" | custom-call | tf_op jit(solution)/shard_map/gather_6/pallas_call | solution.py:304
  361.8 9.6 %fusion.124 = bf16[2048,384]{1,0:T(8,128)(2,1)} fusion(bf16[2048,2048]{1,0:T(8,128)(2,1)} %bitcast.143, bf16[2048,384]{0,1:T(8,128)(2,1)} %copy-done.30), kind=kOutput, calls=%fused_computation.253 | convolution fusion | flops 3221225472 | bytes 11534336 | tf_op jit(solution)/shard_map/dot_general | solution.py:1271
  371.4 8.3 %fusion.8 = (bf16[2048,384]{0,1:T(8,128)(2,1)S(1)}, bf16[2048,384]{0,1:T(8,128)(2,1)S(1)}) fusion(f32[2048,768]{0,1:T(8,128)} %copy-done.16, bf16[2048,2048]{1,0:T(8,128)(2,1)S(1)} %bitcast.144, bf16[2048,1152]{1,0:T(8,128)(2,1)} %bitcast.149), kind=kOutput, calls=%fused_computation.20 | convolution fusion | flops 3240099840 | bytes 19398656 | tf_op jit(solution)/shard_map/dot_general | solution.py:1283
  379.8 8.4 %fusion.12 = bf16[2048,768]{1,0:T(8,128)(2,1)} fusion(bf16[2048,2048]{1,0:T(8,128)(2,1)S(1)} %bitcast.142, bf16[2048,384]{0,1:T(8,128)(2,1)S(1)} %get-tuple-element.75, bf16[2048,384]{0,1:T(8,128)(2,1)S(1)} %get-tuple-element.74), kind=kOutput, calls=%fused_computation.43 | convolution fusion | flops 6448742400 | bytes 14680064 | tf_op jit(solution)/shard_map/dot_general | solution.py:1271
  388.2 9.1 %convolution_convert_fusion = bf16[2048,2048]{1,0:T(8,128)(2,1)} fusion(bf16[2048,1152]{1,0:T(8,128)(2,1)S(1)} %bitcast.152, bf16[2048,384]{0,1:T(8,128)(2,1)S(1)} %get-tuple-element.75, bf16[2048,384]{0,1:T(8,128)(2,1)S(1)} %get-tuple-element.74), kind=kOutput, calls=%fused_computation.5 | convolution fusion | flops 6452936704 | bytes 14680064 | tf_op jit(solution)/shard_map/dot_general | solution.py:1275
  397.4 34.1 %scatter_7.1 = f32[128,2048]{1,0:T(8,128)} custom-call(bf16[16,128,2048]{2,1,0:T(8,128)(2,1)} %bitcast.135), custom_call_target="tpu_custom_call" | custom-call | tf_op jit(solution)/shard_map/scatter_7/pallas_call | solution.py:327
  431.4 2.9 pad_maximum_fusion.1
  434.4 2.6 copy.53
  438.8 3.2 multiply_reduce_fusion.7
  442.1 1.8 fusion.112
  443.9 23.4 %gather_8.1 = bf16[8,128,2048]{2,1,0:T(8,128)(2,1)} custom-call(bf16[128,2048]{1,0:T(8,128)(2,1)} %get-tuple-element.66.x_ref), custom_call_target="tpu_custom_call" | custom-call | tf_op jit(solution)/shard_map/gather_8/pallas_call | solution.py:304
  467.2 8.2 %fusion.19 = (bf16[1024,384]{1,0:T(8,128)(2,1)}, f32[1024,384]{1,0:T(8,128)}) fusion(f32[1024,384]{1,0:T(8,128)} %forward_scan.1, f32[1024,896]{1,0:T(8,128)} %copy-done.22, pred[384]{0:T(512)(128)(4,1)S(1)} %copy-done.71, bf16[1024,2048]{1,0:T(8,128)(2,1)} %bitcast.131, bf16[2048,384]{1,0:T(8,128)(2,1)} %bitcast.189), kind=kOutput, calls=%fused_computation.59 | convolution fusion | flops 1620049920 | bytes 11272576 | tf_op jit(solution)/shard_map/dot_general | solution.py:1283
  475.5 4.9 backward_scan.1
  480.3 4.8 multiply_reduce_fusion.6
  486.7 1.0 select_add_fusion
  488.8 2.1 multiply_reduce_fusion.2
  492.0 9.9 %multiply_reduce_fusion.1 = (f32[2048]{0:T(1024)S(1)}, f32[2048,896]{1,0:T(8,128)}) fusion(bf16[8,4,64,896]{3,2,1,0:T(8,128)(2,1)} %get-tuple-element.37, bf16[1024,2048]{1,0:T(8,128)(2,1)} %fusion.1, bf16[1024,256]{1,0:T(8,128)(2,1)S(1)} %get-tuple-element.92, bf16[1024,384]{1,0:T(8,128)(2,1)S(1)} %copy-done.79, bf16[1024,256]{1,0:T(8,128)(2,1)S(1)} %get-tuple-element.91), kind=kOutput, calls=%fused_computation.7 | convolution fusion | flops 3769104384 | bytes 17047552 | tf_op jit(solution)/shard_map/dot_general | solution.py:1271
  503.9 6.6 copy.46
  510.4 1.0 fusion.55
  512.7 2.6 copy-done.20
  515.6 4.0 fusion.47.refs_2_
  519.6 6.2 convolution_convert_fusion.3
  525.8 17.7 %reduce-scatter.2.cloned.1.call-done = bf16[8,1,2,64,1152]{4,3,2,0,1:T(8,128)(2,1)} async-done(((bf16[8,2,2,64,1152]{4,3,2,0,1:T(8,128)(2,1)}), bf16[8,1,2,64,1152]{4,3,2,0,1:T(8,128)(2,1)}) %reduce-scatter.2.cloned.1.call-update) | async-done | bytes 2359312 | tf_op jit(solution)/shard_map/reduce_scatter | solution.py:1252
  543.5 123.1 %closing.1 = (f32[128,2048]{1,0:T(8,128)}, bf16[64,2560]{1,0:T(8,128)(2,1)}, bf16[64,2560]{1,0:T(8,128)(2,1)}, bf16[2,64,2560]{2,1,0:T(8,128)(2,1)}, bf16[64,614...) custom-call(bf16[8,128,2048]{2,1,0:T(8,128)(2,1)} %bitcast.153, ...), custom_call_target="tpu_custom_call" | custom-call | tf_op jit(solution)/shard_map/closing/pallas_call | solution.py:1140
  666.7 1.3 slice_bitcast_fusion.3
  668.0 1.2 slice.303
  669.3 1.2 slice.299
  670.4 1.3 slice_bitcast_fusion.2
  671.7 2.5 convert_bitcast_fusion
  674.2 1.2 convert_element_type.227
  675.4 1.2 convert_element_type.228
  681.1 1.1 fusion.53
  (241 shorter events, 26.8 us)
Async XLA Ops:
  7.2 536.3 %reduce-scatter.2.cloned.1.call-start = ((), (), s32[]{:S(2)}) async-start(), calls=%async_computation.1 | async-start | bytes 7077888 | tf_op jit(solution)/shard_map/reduce_scatter | solution.py:1252
  126.5 134.2 %collective-permute-start = (bf16[8,2,64,1152]{3,2,1,0:T(8,128)(2,1)}, bf16[8,2,64,1152]{3,2,1,0:T(8,128)(2,1)}, u32[]{:S(2)}, u32[]{:S(2)}) collective-permute-start(bf16[8,2,64,1152]{3,2,1,0:T(8,128)(2,1)} %get-tuple-element.39), channel_id=1, source_target_pairs={{0,2},{1,3},{2,0},{3,1},{4,6},{5,7},{6,4},{7,5},{8,10},{9,11},{10,... | collective-permute-start | bytes 7077896 | tf_op jit(solution)/shard_map/ppermute | solution.py:1225
  134.6 3.5 copy-start.41
  138.7 3.8 copy-start
  151.1 4.6 copy-start.10
  151.1 4.6 copy-start.12
  154.6 4.2 copy-start.44
  154.6 4.2 copy-start.47
  156.0 2.8 copy-start.3
  162.6 5.0 copy-start.70
  167.6 2.6 copy-start.78
  170.2 4.4 copy-start.32
  255.4 69.9 %copy-start.67 = (f32[128]{0:T(128)}, f32[128]{0:T(128)S(1)}, u32[]{:S(2)}) copy-start(f32[128]{0:T(128)S(1)} %broadcast_multiply_fusion.1) | copy-start | bytes 1540
  255.4 5.3 copy-start.27
  260.8 5.2 slice-start
  263.1 4.0 slice-start.1
  276.3 2.6 copy-start.16
  278.9 8.8 %copy-start.30 = (bf16[2048,384]{0,1:T(8,128)(2,1)}, bf16[2048,384]{0,1:T(8,128)(2,1)S(1)}, u32[]{:S(2)}) copy-start(bf16[2048,384]{0,1:T(8,128)(2,1)S(1)} %multiply_convert_fusion.2) | copy-start | bytes 4718596
  287.7 37.7 %copy-start.17 = (bf16[1,128,2048]{2,1,0:T(8,128)(2,1)S(1)}, bf16[1,128,2048]{2,1,0:T(8,128)(2,1)}, u32[]{:S(2)}) copy-start(bf16[1,128,2048]{2,1,0:T(8,128)(2,1)} %param.20) | copy-start | bytes 1572868
  361.8 9.7 %copy-start.14 = (bf16[16,128,2048]{2,1,0:T(8,128)(2,1)S(1)}, bf16[16,128,2048]{2,1,0:T(8,128)(2,1)}, u32[]{:S(2)}) copy-start(bf16[16,128,2048]{2,1,0:T(8,128)(2,1)} %gather_6.1) | copy-start | bytes 25165828
  361.8 18.0 %slice-start.2 = ((s8[8388608]{0:T(1024)(128)(4,1)}), s8[4194304]{0:T(1024)(128)(4,1)S(1)}, s32[]{:S(2)}) async-start(s8[8388608]{0:T(1024)(128)(4,1)} %bitcast.140), calls=%async_computation.4 | async-start | bytes 8388608
  371.4 8.3 %slice-start.3 = ((s8[8388608]{0:T(1024)(128)(4,1)}), s8[4194304]{0:T(1024)(128)(4,1)S(1)}, s32[]{:S(2)}) async-start(s8[8388608]{0:T(1024)(128)(4,1)} %bitcast.140), calls=%async_computation.5 | async-start | bytes 8388608
  371.4 16.8 %slice-start.4 = ((s8[4718592]{0:T(1024)(128)(4,1)}), s8[524288]{0:T(1024)(128)(4,1)S(1)}, s32[]{:S(2)}) async-start(s8[4718592]{0:T(1024)(128)(4,1)} %bitcast.150), calls=%async_computation.6 | async-start | bytes 1048576
  379.8 8.4 %slice-start.5 = ((s8[4718592]{0:T(1024)(128)(4,1)}), s8[4194304]{0:T(1024)(128)(4,1)S(1)}, s32[]{:S(2)}) async-start(s8[4718592]{0:T(1024)(128)(4,1)} %bitcast.150), calls=%async_computation.7 | async-start | bytes 8388608
  437.0 5.0 copy-start.75
  437.0 5.0 copy-start.2
  437.0 5.0 copy-start.5
  437.0 5.0 copy-start.9
  437.0 5.0 copy-start.18
  437.0 5.0 copy-start.66
  437.1 5.0 copy-start.68
  443.9 23.4 %copy-start.71 = (pred[384]{0:T(512)(128)(4,1)S(1)}, pred[384]{0:T(512)(128)(4,1)}, u32[]{:S(2)}) copy-start(pred[384]{0:T(512)(128)(4,1)} %iota_compare_fusion.7) | copy-start | bytes 1156
  475.5 4.9 copy-start.45
  475.5 4.9 copy-start.48
  480.3 4.8 copy-start.51
  486.6 2.2 copy-start.13
  486.6 2.2 copy-start.53
  486.7 2.2 copy-start.55
  486.7 2.1 copy-start.57
  486.7 2.1 copy-start.59
  491.1 10.8 %copy-start.37 = (bf16[1024,256]{1,0:T(8,128)(2,1)}, bf16[1024,256]{1,0:T(8,128)(2,1)S(1)}, u32[]{:S(2)}) copy-start(bf16[1024,256]{1,0:T(8,128)(2,1)S(1)} %get-tuple-element.92) | copy-start | bytes 1572868
  492.0 10.0 %copy-start.46 = (f32[2048]{0:T(1024)S(1)}, f32[2048]{0:T(1024)}, u32[]{:S(2)}) copy-start(f32[2048]{0:T(1024)} %get-tuple-element.57) | copy-start | bytes 24580
  492.0 10.8 %copy-start.42 = (f32[2,32,64]{2,1,0:T(8,128)S(1)}, f32[2,32,64]{2,1,0:T(8,128)}, u32[]{:S(2)}) copy-start(f32[2,32,64]{2,1,0:T(8,128)} %copy-done.41) | copy-start | bytes 49156
  492.0 10.9 %copy-start.72 = (f32[16]{0:T(128)S(1)}, f32[16]{0:T(128)}, u32[]{:S(2)}) copy-start(f32[16]{0:T(128)} %pad.107.clone) | copy-start | bytes 196
  503.8 6.6 copy-start.7
  503.8 6.6 copy-start.24
  503.8 6.6 copy-start.26
  512.2 3.1 copy-start.20
  512.4 3.1 copy-start.33
  512.7 6.9 %copy-start.8 = (bf16[2560,512]{1,0:T(8,128)(2,1)}, bf16[2560,512]{1,0:T(8,128)(2,1)S(1)}, u32[]{:S(2)}) copy-start(bf16[2560,512]{1,0:T(8,128)(2,1)S(1)} %maximum_dynamic-update-slice_fusion) | copy-start | bytes 7864324
  515.6 4.0 copy-start.38
  515.6 4.0 copy-start.77
  515.6 4.0 copy-start.80
  666.6 7.5 %copy-start.35 = (bf16[64,6144]{1,0:T(8,128)(2,1)S(1)}, bf16[64,6144]{1,0:T(8,128)(2,1)}, u32[]{:S(2)}) copy-start(bf16[64,6144]{1,0:T(8,128)(2,1)} %get-tuple-element.49) | copy-start | bytes 2359300
  671.7 3.7 copy-start.34
  674.2 2.5 copy-start.40
  675.4 2.2 copy-start.39
  675.4 3.0 copy-start.15
  675.4 3.0 copy-start.21
  676.7 2.1 copy-start.43
  676.7 3.4 copy-start.36
  676.7 3.4 copy-start.60
  676.7 3.5 copy-start.61
  677.6 3.5 copy-start.19
  (25 other events, 26.4 us)
Sparse Core Ops, SparseCore 0:
  437.1 106.3 reduce-scatter.1

commit v3 on v2

--- a/solution.py
+++ b/solution.py
@@ -1236,10 +1236,12 @@
 def share_gather(value, axis):
     me = lax.axis_index(axis)
     for mask in far_masks(axis):
-        other = swap(value, axis, mask)
-        low = (me // mask) % 2 == 0
-        value = jnp.concatenate(
-            [jnp.where(low, value, other), jnp.where(low, other, value)], axis=1
+        sources, size, rows, width = value.shape
+        high = (me // mask) % 2
+        whole = jnp.zeros((sources, 2 * size, rows, width), value.dtype)
+        whole = lax.dynamic_update_slice(whole, value, (0, high * size, 0, 0))
+        value = lax.dynamic_update_slice(
+            whole, swap(value, axis, mask), (0, (1 - high) * size, 0, 0)
         )
     return value
 
@@ -1359,7 +1361,6 @@
     w_in, w_out = w_in.reshape(model, span + width_r), w_out.reshape(model, width_r)
     w_mlp = share_gather(mlp_own, "dp").reshape(model, 3 * cols)
     w_two, w_down = w_mlp[:, : 2 * cols], w_mlp[:, 2 * cols :]
-    blocks_all = shared[:, :rows_c].reshape(rec_width, 2 * BW)
     vectors = shared[:, block_rows:].astype(fp32)
     channel_vecs = vectors[:, : CONV + 4, :rows_c].transpose(1, 0, 2).reshape(CONV + 4, rec_width)
     gains = vectors[:, CONV + 4 : CONV + 6, :rows_w].transpose(1, 0, 2).reshape(2, model)
@@ -1372,7 +1373,12 @@
         chans.owned(span_vecs[CONV + 1 + i], me_seq) for i in range(3)
     )
     mine = chans.mine(me_seq)
-    span_mats = lax.dynamic_slice(blocks_all, (base, 0), (span, 2 * BW))
+    touched = min(everyone, -(-(span - 1) // rows_c) + 1)
+    from_device = jnp.minimum(base // rows_c, everyone - touched)
+    near = lax.dynamic_slice(shared, (from_device, 0, 0), (touched, rows_c, 2 * BW))
+    span_mats = lax.dynamic_slice(
+        near.reshape(touched * rows_c, 2 * BW), (base - from_device * rows_c, 0), (span, 2 * BW)
+    )
 
     def block_diagonal(value):
         rows = []
@@ -1388,7 +1394,7 @@
 
     flat_in = tokens.reshape(local_len, model).astype(fp32)
     tokens_all = tokens_all.reshape(steps, model).astype(fp32)
-    normed_all = rms_norm(tokens_all, gain_one).astype(half)
+    normed_all = lax.optimization_barrier(rms_norm(tokens_all, gain_one).astype(half))
     pre = times(normed_all, w_in)
     rec_pre, gelu_pre = chans.rec_of(pre)
     padded = jnp.concatenate([jnp.zeros((CONV - 1, span), fp32), rec_pre], axis=0)

time: 694 us -> 686 us (0.988)
  other arithmetic: 65.4 us -> 54 us
  transfers between devices with their start and end apart: 2 -> 2, of which waited for: 1 -> 1; matrix products, arithmetic and copies ran while one was open for 14% -> 13% of each run, Pallas kernels for 15% -> 16%
where the time goes in v3:
time: 686 us; the launch traced here: 682 us
  Pallas kernels  450 us (66%)
  matrix products  90.3 us (13%)
  other arithmetic  54 us (8%)
  local copies, waits for them, and re-layouts  44.1 us (6%)
  between operations  20.9 us (3%)
  waiting for transfers between devices  17.7 us (3%)
    pallas_call x1, Pallas kernels, closing(): pl.pallas_call(kernel, out_shape=[shape(in_part.shape[1:], fp32), *(shape...  123 us
    pallas_call x3, Pallas kernels, gather(): pl.pallas_call(kernel, out_shape=jax.ShapeDtypeStruct((2 ** len(bits), ro...  113 us
    pallas_call x1, Pallas kernels, opening(): pl.pallas_call(kernel, out_shape=[jax.ShapeDtypeStruct((seqs, dps, rows,...  112 us
    pallas_call x3, Pallas kernels, scatter_sum(): pl.pallas_call(kernel, out_shape=jax.ShapeDtypeStruct((rows, width), fp32...  92.4 us
    dot_general x5, matrix products, contract_rows(): lax.dot_general(left, right, (((0,), (0,)), ((), ())), preferred_element_...  32.9 us
    dot_general x5, matrix products, times(): return jnp.dot(left, right, preferred_element_type=fp32)  29.4 us
    dot_general x5, matrix products, times_trans(): lax.dot_general(left, right, (((1,), (1,)), ((), ())), preferred_element_...  28 us
    reduce_scatter x1, waiting for transfers between devices, share_scatter(): lax.psum_scatter(value, axis, scatter_dimension=1, axis_index_groups=groups)  17.7 us
  transfers between devices with their start and end apart: 2, of which 1 were waited for; matrix products, arithmetic and copies ran while one was open for 13% of the time, Pallas kernels for 16%

profile of v3, /device:TPU:11, one launch (start us, length us, event | category | flops | bytes accessed | tf_op | source)
XLA Modules:
  0.0 682.3 jit_solution(9125989232209022911)
XLA Ops:
  7.2 1.3 convert_reduce_fusion.1
  12.8 1.9 concatenate.66.refs_6_
  14.7 111.9 %opening.1 = (bf16[8,4,64,896]{3,2,1,0:T(8,128)(2,1)}, bf16[8,4,64,384]{3,2,1,0:T(8,128)(2,1)}, bf16[8,2,64,1152]{3,2,1,0:T(8,128)(2,1)}, bf16[8,384,512]{2,1,0:T(8,128)(2,1)}, bf16[8,128,2048]{2,1,0:T(8,128)(2,1)}) custom-call(bf16[64,2560]{1,0:T(8,128)(2,1)} %refs_0_.1, bf16[64,2560]{1,0:T(8,128)(2,1)} %bitcast.162, bf16[64,2560]{1,0:T(8,128)(2,1)} %refs_2_.1, ...), custom_call_target="tpu_custom_call" | custom-call | tf_op jit(solution)/shard_map/opening/pallas_call | solution.py:753
  126.5 5.6 collective-permute-start
  132.2 1.1 slice.307
  133.6 1.0 copy-done.34
  134.6 1.1 constant_dynamic-slice_fusion.3
  137.5 3.2 multiply_reduce_fusion
  141.0 1.0 fusion.1
  142.0 1.1 copy-done.78
  143.1 4.5 fusion.122
  147.6 1.8 copy-done.25
  152.2 1.0 add_convert_fusion.1
  153.2 1.0 fusion.54
  154.2 3.8 convert_multiply_fusion.1
  158.0 4.8 forward_scan.1
  162.8 2.6 select_convert_fusion
  165.4 4.4 convolution_convert_fusion.2
  169.8 20.8 %scatter_3.1 = f32[128,2048]{1,0:T(8,128)} custom-call(bf16[8,128,2048]{2,1,0:T(8,128)(2,1)} %bitcast.151), custom_call_target="tpu_custom_call" | custom-call | tf_op jit(solution)/shard_map/scatter_3/pallas_call | solution.py:327
  191.4 1.6 multiply_reduce_fusion.9
  195.0 55.3 %gather_4.1 = bf16[16,128,2048]{2,1,0:T(8,128)(2,1)} custom-call(bf16[128,2048]{1,0:T(8,128)(2,1)} %multiply_convert_fusion.2.x_ref), custom_call_target="tpu_custom_call" | custom-call | tf_op jit(solution)/shard_map/gather_4/pallas_call | solution.py:304
  253.6 1.2 convert_bitcast_fusion.3
  256.1 1.0 copy-done.30
  257.5 2.3 constant_dynamic-update-slice_fusion.1
  259.8 2.4 copy-done.14
  262.2 7.2 %fusion.10 = f32[2048,768]{0,1:T(8,128)S(1)} fusion(bf16[2048,2048]{1,0:T(8,128)(2,1)S(1)} %bitcast.136, bf16[2048,1152]{1,0:T(8,128)(2,1)S(1)} %bitcast.144), kind=kOutput, calls=%fused_computation.25 | convolution fusion | flops 6442450944 | bytes 17825792 | tf_op jit(solution)/shard_map/dot_general | solution.py:1285
  269.4 1.1 multiply_convert_fusion.1
  270.5 1.6 copy-done.17
  272.1 7.3 %convolution_convert_fusion.1 = bf16[2048,2048]{1,0:T(8,128)(2,1)} fusion(bf16[2048,384]{0,1:T(8,128)(2,1)S(1)} %multiply_convert_fusion.1, bf16[2048,1152]{1,0:T(8,128)(2,1)S(1)} %bitcast.145), kind=kOutput, calls=%fused_computation.5 | convolution fusion | flops 3225419776 | bytes 11534336 | tf_op jit(solution)/shard_map/dot_general | solution.py:1277
  279.3 37.7 %scatter_5.1 = f32[128,2048]{1,0:T(8,128)} custom-call(bf16[16,128,2048]{2,1,0:T(8,128)(2,1)} %bitcast.135), custom_call_target="tpu_custom_call" | custom-call | tf_op jit(solution)/shard_map/scatter_5/pallas_call | solution.py:327
  317.1 2.5 multiply_convert_fusion.3.x_ref
  319.6 33.8 %gather_6.1 = bf16[16,128,2048]{2,1,0:T(8,128)(2,1)} custom-call(bf16[128,2048]{1,0:T(8,128)(2,1)} %multiply_convert_fusion.3.x_ref), custom_call_target="tpu_custom_call" | custom-call | tf_op jit(solution)/shard_map/gather_6/pallas_call | solution.py:304
  353.4 9.6 %fusion.123 = bf16[2048,384]{1,0:T(8,128)(2,1)} fusion(bf16[2048,2048]{1,0:T(8,128)(2,1)} %bitcast.140, bf16[2048,384]{0,1:T(8,128)(2,1)} %copy-done.33), kind=kOutput, calls=%fused_computation.251 | convolution fusion | flops 3221225472 | bytes 11534336 | tf_op jit(solution)/shard_map/dot_general | solution.py:1273
  363.1 8.5 %fusion.8 = (bf16[2048,384]{0,1:T(8,128)(2,1)S(1)}, bf16[2048,384]{0,1:T(8,128)(2,1)S(1)}) fusion(f32[2048,768]{0,1:T(8,128)} %copy-done.17, bf16[2048,2048]{1,0:T(8,128)(2,1)S(1)} %bitcast.141, bf16[2048,1152]{1,0:T(8,128)(2,1)} %bitcast.146), kind=kOutput, calls=%fused_computation.18 | convolution fusion | flops 3240099840 | bytes 19398656 | tf_op jit(solution)/shard_map/dot_general | solution.py:1285
  371.6 8.2 %fusion.12 = bf16[2048,768]{1,0:T(8,128)(2,1)} fusion(bf16[2048,2048]{1,0:T(8,128)(2,1)S(1)} %bitcast.139, bf16[2048,384]{0,1:T(8,128)(2,1)S(1)} %get-tuple-element.75, bf16[2048,384]{0,1:T(8,128)(2,1)S(1)} %get-tuple-element.74), kind=kOutput, calls=%fused_computation.39 | convolution fusion | flops 6448742400 | bytes 14680064 | tf_op jit(solution)/shard_map/dot_general | solution.py:1273
  379.8 9.2 %convolution_convert_fusion = bf16[2048,2048]{1,0:T(8,128)(2,1)} fusion(bf16[2048,1152]{1,0:T(8,128)(2,1)S(1)} %bitcast.149, bf16[2048,384]{0,1:T(8,128)(2,1)S(1)} %get-tuple-element.75, bf16[2048,384]{0,1:T(8,128)(2,1)S(1)} %get-tuple-element.74), kind=kOutput, calls=%fused_computation.4 | convolution fusion | flops 6452936704 | bytes 14680064 | tf_op jit(solution)/shard_map/dot_general | solution.py:1277
  388.9 33.9 %scatter_7.1 = f32[128,2048]{1,0:T(8,128)} custom-call(bf16[16,128,2048]{2,1,0:T(8,128)(2,1)} %bitcast.134), custom_call_target="tpu_custom_call" | custom-call | tf_op jit(solution)/shard_map/scatter_7/pallas_call | solution.py:327
  422.8 2.9 pad_maximum_fusion
  425.8 2.6 copy.53
  430.2 3.2 multiply_reduce_fusion.7
  433.4 1.8 fusion.111
  435.2 23.4 %gather_8.1 = bf16[8,128,2048]{2,1,0:T(8,128)(2,1)} custom-call(bf16[128,2048]{1,0:T(8,128)(2,1)} %get-tuple-element.66.x_ref), custom_call_target="tpu_custom_call" | custom-call | tf_op jit(solution)/shard_map/gather_8/pallas_call | solution.py:304
  458.7 8.2 %fusion.19 = (bf16[1024,384]{1,0:T(8,128)(2,1)}, f32[1024,384]{1,0:T(8,128)}) fusion(f32[1024,384]{1,0:T(8,128)} %forward_scan.1, f32[1024,896]{1,0:T(8,128)} %copy-done.25, pred[384]{0:T(512)(128)(4,1)S(1)} %copy-done.73, bf16[1024,2048]{1,0:T(8,128)(2,1)} %bitcast.130, bf16[2048,384]{1,0:T(8,128)(2,1)} %bitcast.185), kind=kOutput, calls=%fused_computation.55 | convolution fusion | flops 1620049920 | bytes 11272576 | tf_op jit(solution)/shard_map/dot_general | solution.py:1285
  466.9 4.8 backward_scan.1
  471.8 4.8 multiply_reduce_fusion.6
  478.1 1.0 select_add_fusion
  480.2 2.1 multiply_reduce_fusion.2
  483.4 10.0 %multiply_reduce_fusion.1 = (f32[2048]{0:T(1024)S(1)}, f32[2048,896]{1,0:T(8,128)}) fusion(bf16[8,4,64,896]{3,2,1,0:T(8,128)(2,1)} %get-tuple-element.37, bf16[1024,2048]{1,0:T(8,128)(2,1)} %copy-done.22, bf16[1024,256]{1,0:T(8,128)(2,1)S(1)} %get-tuple-element.86, bf16[1024,384]{1,0:T(8,128)(2,1)S(1)} %copy-done.81, bf16[1024,256]{1,0:T(8,128)(2,1)S(1)} %get-tuple-element.85), kind=kOutput, calls=%fused_computation.6 | convolution fusion | flops 3769104384 | bytes 17047552 | tf_op jit(solution)/shard_map/dot_general | solution.py:1273
  495.4 6.6 copy.46
  501.9 1.0 fusion.55
  504.2 2.6 copy-done.23
  507.1 4.0 fusion.47.refs_2_
  511.1 6.2 convolution_convert_fusion.3
  517.3 17.7 %reduce-scatter.2.cloned.1.call-done = bf16[8,1,2,64,1152]{4,3,2,0,1:T(8,128)(2,1)} async-done(((bf16[8,2,2,64,1152]{4,3,2,0,1:T(8,128)(2,1)}), bf16[8,1,2,64,1152]{4,3,2,0,1:T(8,128)(2,1)}) %reduce-scatter.2.cloned.1.call-update) | async-done | bytes 2359312 | tf_op jit(solution)/shard_map/reduce_scatter | solution.py:1254
  535.0 123.2 %closing.1 = (f32[128,2048]{1,0:T(8,128)}, bf16[64,2560]{1,0:T(8,128)(2,1)}, bf16[64,2560]{1,0:T(8,128)(2,1)}, bf16[2,64,2560]{2,1,0:T(8,128)(2,1)}, bf16[64,614...) custom-call(bf16[8,128,2048]{2,1,0:T(8,128)(2,1)} %bitcast.150, ...), custom_call_target="tpu_custom_call" | custom-call | tf_op jit(solution)/shard_map/closing/pallas_call | solution.py:1140
  658.2 1.4 slice_bitcast_fusion.3
  659.5 1.3 slice.299
  660.8 1.2 slice.295
  662.0 1.3 slice_bitcast_fusion.2
  663.3 2.5 convert_bitcast_fusion
  665.7 1.2 convert_element_type.219
  667.0 1.2 convert_element_type.220
  671.7 1.0 fusion.50
  672.7 1.1 fusion.53
  (240 shorter events, 25.1 us)
Async XLA Ops:
  7.2 527.8 %reduce-scatter.2.cloned.1.call-start = ((), (), s32[]{:S(2)}) async-start(), calls=%async_computation.1 | async-start | bytes 7077888 | tf_op jit(solution)/shard_map/reduce_scatter | solution.py:1254
  126.5 131.0 %collective-permute-start = (bf16[8,2,64,1152]{3,2,1,0:T(8,128)(2,1)}, bf16[8,2,64,1152]{3,2,1,0:T(8,128)(2,1)}, u32[]{:S(2)}, u32[]{:S(2)}) collective-permute-start(bf16[8,2,64,1152]{3,2,1,0:T(8,128)(2,1)} %get-tuple-element.39), channel_id=1, source_target_pairs={{0,2},{1,3},{2,0},{3,1},{4,6},{5,7},{6,4},{7,5},{8,10},{9,11},{10,... | collective-permute-start | bytes 7077896 | tf_op jit(solution)/shard_map/ppermute | solution.py:1225
  134.6 2.3 copy-start.44
  137.5 3.2 copy-start.47
  137.5 3.5 copy-start.7
  141.0 2.1 copy-start.78
  142.0 5.6 copy-start.22
  150.6 3.6 copy-start.50
  151.4 2.7 copy-start.2
  158.0 4.8 copy-start.72
  162.8 2.6 copy-start.80
  165.4 4.4 copy-start.35
  255.4 61.6 %copy-start.69 = (f32[128]{0:T(128)}, f32[128]{0:T(128)S(1)}, u32[]{:S(2)}) copy-start(f32[128]{0:T(128)S(1)} %broadcast_multiply_fusion.1) | copy-start | bytes 1540
  257.1 5.1 copy-start.14
  259.8 10.7 %copy-start.20 = (bf16[8,4,64,1152]{3,2,1,0:T(8,128)(2,1)}, bf16[8,4,64,1152]{3,2,1,0:T(8,128)(2,1)S(1)}, u32[]{:S(2)}) copy-start(bf16[8,4,64,1152]{3,2,1,0:T(8,128)(2,1)S(1)} %constant_dynamic-update-slice_fusion.1) | copy-start | bytes 14155780
  269.4 2.7 copy-start.17
  272.1 7.3 %copy-start.33 = (bf16[2048,384]{0,1:T(8,128)(2,1)}, bf16[2048,384]{0,1:T(8,128)(2,1)S(1)}, u32[]{:S(2)}) copy-start(bf16[2048,384]{0,1:T(8,128)(2,1)S(1)} %multiply_convert_fusion.1) | copy-start | bytes 4718596
  279.3 37.7 %copy-start.18 = (bf16[1,128,2048]{2,1,0:T(8,128)(2,1)S(1)}, bf16[1,128,2048]{2,1,0:T(8,128)(2,1)}, u32[]{:S(2)}) copy-start(bf16[1,128,2048]{2,1,0:T(8,128)(2,1)} %param.20) | copy-start | bytes 1572868
  353.4 9.7 %copy-start.15 = (bf16[16,128,2048]{2,1,0:T(8,128)(2,1)S(1)}, bf16[16,128,2048]{2,1,0:T(8,128)(2,1)}, u32[]{:S(2)}) copy-start(bf16[16,128,2048]{2,1,0:T(8,128)(2,1)} %gather_6.1) | copy-start | bytes 25165828
  353.4 18.1 %slice-start = ((s8[8388608]{0:T(1024)(128)(4,1)}), s8[4194304]{0:T(1024)(128)(4,1)S(1)}, s32[]{:S(2)}) async-start(s8[8388608]{0:T(1024)(128)(4,1)} %bitcast.137), calls=%async_computation.2 | async-start | bytes 8388608
  363.1 8.5 %slice-start.1 = ((s8[8388608]{0:T(1024)(128)(4,1)}), s8[4194304]{0:T(1024)(128)(4,1)S(1)}, s32[]{:S(2)}) async-start(s8[8388608]{0:T(1024)(128)(4,1)} %bitcast.137), calls=%async_computation.3 | async-start | bytes 8388608
  363.1 16.7 %slice-start.2 = ((s8[4718592]{0:T(1024)(128)(4,1)}), s8[524288]{0:T(1024)(128)(4,1)S(1)}, s32[]{:S(2)}) async-start(s8[4718592]{0:T(1024)(128)(4,1)} %bitcast.147), calls=%async_computation.4 | async-start | bytes 1048576
  371.6 8.2 %slice-start.3 = ((s8[4718592]{0:T(1024)(128)(4,1)}), s8[4194304]{0:T(1024)(128)(4,1)S(1)}, s32[]{:S(2)}) async-start(s8[4718592]{0:T(1024)(128)(4,1)} %bitcast.147), calls=%async_computation.5 | async-start | bytes 8388608
  428.4 5.0 copy-start.77
  428.4 5.0 copy-start.1
  428.4 5.0 copy-start.4
  428.4 5.0 copy-start.9
  428.5 5.0 copy-start.19
  428.5 5.0 copy-start.68
  428.5 5.0 copy-start.70
  435.2 23.4 %copy-start.73 = (pred[384]{0:T(512)(128)(4,1)S(1)}, pred[384]{0:T(512)(128)(4,1)}, u32[]{:S(2)}) copy-start(pred[384]{0:T(512)(128)(4,1)} %iota_compare_fusion.7) | copy-start | bytes 1156
  466.9 4.9 copy-start.51
  471.8 4.8 copy-start.53
  478.1 1.9 copy-start.11
  478.1 2.2 copy-start.13
  478.1 2.2 copy-start.55
  478.1 2.2 copy-start.57
  478.1 2.1 copy-start.59
  478.1 2.1 copy-start.61
  482.6 10.9 %copy-start.40 = (bf16[1024,256]{1,0:T(8,128)(2,1)}, bf16[1024,256]{1,0:T(8,128)(2,1)S(1)}, u32[]{:S(2)}) copy-start(bf16[1024,256]{1,0:T(8,128)(2,1)S(1)} %get-tuple-element.86) | copy-start | bytes 1572868
  483.4 10.1 %copy-start.49 = (f32[2048]{0:T(1024)S(1)}, f32[2048]{0:T(1024)}, u32[]{:S(2)}) copy-start(f32[2048]{0:T(1024)} %get-tuple-element.57) | copy-start | bytes 24580
  483.4 10.9 %copy-start.45 = (f32[2,32,64]{2,1,0:T(8,128)S(1)}, f32[2,32,64]{2,1,0:T(8,128)}, u32[]{:S(2)}) copy-start(f32[2,32,64]{2,1,0:T(8,128)} %copy-done.44) | copy-start | bytes 49156
  483.4 10.9 %copy-start.74 = (f32[16]{0:T(128)S(1)}, f32[16]{0:T(128)}, u32[]{:S(2)}) copy-start(f32[16]{0:T(128)} %pad.107.clone) | copy-start | bytes 196
  495.4 6.6 copy-start.6
  495.4 6.6 copy-start.27
  495.4 6.6 copy-start.29
  503.7 3.1 copy-start.23
  503.9 3.1 copy-start.36
  504.2 6.9 %copy-start.8 = (bf16[2560,512]{1,0:T(8,128)(2,1)}, bf16[2560,512]{1,0:T(8,128)(2,1)S(1)}, u32[]{:S(2)}) copy-start(bf16[2560,512]{1,0:T(8,128)(2,1)S(1)} %maximum_dynamic-update-slice_fusion) | copy-start | bytes 7864324
  507.1 4.0 copy-start.41
  507.1 4.0 copy-start.79
  507.1 4.0 copy-start.82
  658.2 7.6 %copy-start.38 = (bf16[64,6144]{1,0:T(8,128)(2,1)S(1)}, bf16[64,6144]{1,0:T(8,128)(2,1)}, u32[]{:S(2)}) copy-start(bf16[64,6144]{1,0:T(8,128)(2,1)} %get-tuple-element.49) | copy-start | bytes 2359300
  663.3 3.7 copy-start.37
  665.7 2.5 copy-start.43
  667.0 2.2 copy-start.42
  667.0 3.1 copy-start.16
  667.0 3.1 copy-start.24
  667.0 3.1 copy-start.48
  668.2 2.1 copy-start.46
  668.2 3.4 copy-start.39
  668.2 3.4 copy-start.62
  668.2 3.5 copy-start.63
  669.1 3.5 copy-start.21
  (25 other events, 26.2 us)
Sparse Core Ops, SparseCore 0:
  428.5 106.4 reduce-scatter.1

commit v4 on v3

--- a/solution.py
+++ b/solution.py
@@ -696,10 +696,11 @@
         for size in levels:
             shared.level(size)
         mlp_moves[0].start_own()
-        for mlp_move in mlp_moves:
-            for step in range(0 if mlp_move.across else 1, seqs):
-                mlp_move.start(step)
+        for step in range(1, seqs):
+            mlp_moves[0].start(step)
         toks.begin()
+        if dps == 1:
+            assert pairs == 1
         for hop in range(1, dps):
 
             def round_of(step, carry, hop=hop):
@@ -712,6 +713,9 @@
                 return carry
 
             lax.fori_loop(0, seqs, round_of, 0)
+            if hop == 1 and pairs == 2:
+                for step in range(seqs):
+                    mlp_moves[1].start(step)
             if hop == min(2, dps - 1):
                 for size in levels:
                     toks.level(size)

time: 686 us -> 683 us (level)
  no operation moved by 1% of the time
where the time goes in v4:
time: 683 us; the launch traced here: 679 us
  Pallas kernels  447 us (65%)
  matrix products  90.3 us (13%)
  other arithmetic  54 us (8%)
  local copies, waits for them, and re-layouts  44.1 us (6%)
  between operations  20.9 us (3%)
  waiting for transfers between devices  18 us (3%)
    pallas_call x1, Pallas kernels, closing(): pl.pallas_call(kernel, out_shape=[shape(in_part.shape[1:], fp32), *(shape...  123 us
    pallas_call x3, Pallas kernels, gather(): pl.pallas_call(kernel, out_shape=jax.ShapeDtypeStruct((2 ** len(bits), ro...  111 us
    pallas_call x1, Pallas kernels, opening(): pl.pallas_call(kernel, out_shape=[jax.ShapeDtypeStruct((seqs, dps, rows,...  110 us
    pallas_call x3, Pallas kernels, scatter_sum(): pl.pallas_call(kernel, out_shape=jax.ShapeDtypeStruct((rows, width), fp32...  93.2 us
    dot_general x5, matrix products, contract_rows(): lax.dot_general(left, right, (((0,), (0,)), ((), ())), preferred_element_...  32.9 us
    dot_general x5, matrix products, times(): return jnp.dot(left, right, preferred_element_type=fp32)  29.4 us
    dot_general x5, matrix products, times_trans(): lax.dot_general(left, right, (((1,), (1,)), ((), ())), preferred_element_...  28 us
    reduce_scatter x1, waiting for transfers between devices, share_scatter(): lax.psum_scatter(value, axis, scatter_dimension=1, axis_index_groups=groups)  18 us
  transfers between devices with their start and end apart: 2, of which 1 were waited for; matrix products, arithmetic and copies ran while one was open for 13% of the time, Pallas kernels for 16%

profile of v4, /device:TPU:11, one launch (start us, length us, event | category | flops | bytes accessed | tf_op | source)
XLA Modules:
  0.0 679.0 jit_solution(14010319753341636054)
XLA Ops:
  7.2 1.3 convert_reduce_fusion.1
  12.8 1.9 concatenate.66.refs_6_
  14.7 110.2 %opening.1 = (bf16[8,4,64,896]{3,2,1,0:T(8,128)(2,1)}, bf16[8,4,64,384]{3,2,1,0:T(8,128)(2,1)}, bf16[8,2,64,1152]{3,2,1,0:T(8,128)(2,1)}, bf16[8,384,512]{2,1,0:T(8,128)(2,1)}, bf16[8,128,2048]{2,1,0:T(8,128)(2,1)}) custom-call(bf16[64,2560]{1,0:T(8,128)(2,1)} %refs_0_.1, bf16[64,2560]{1,0:T(8,128)(2,1)} %bitcast.162, bf16[64,2560]{1,0:T(8,128)(2,1)} %refs_2_.1, ...), custom_call_target="tpu_custom_call" | custom-call | tf_op jit(solution)/shard_map/opening/pallas_call | solution.py:757
  124.9 4.3 collective-permute-start
  129.2 1.1 slice.307
  130.6 1.0 copy-done.34
  131.6 1.1 constant_dynamic-slice_fusion.3
  134.5 3.2 multiply_reduce_fusion
  138.0 1.0 fusion.1
  139.0 1.1 copy-done.78
  140.1 4.5 fusion.122
  144.6 1.8 copy-done.25
  149.2 1.0 add_convert_fusion.1
  150.2 1.0 fusion.54
  151.2 3.8 convert_multiply_fusion.1
  155.0 4.8 forward_scan.1
  159.8 2.6 select_convert_fusion
  162.4 4.4 convolution_convert_fusion.2
  166.8 21.5 %scatter_3.1 = f32[128,2048]{1,0:T(8,128)} custom-call(bf16[8,128,2048]{2,1,0:T(8,128)(2,1)} %bitcast.151), custom_call_target="tpu_custom_call" | custom-call | tf_op jit(solution)/shard_map/scatter_3/pallas_call | solution.py:327
  189.1 1.6 multiply_reduce_fusion.9
  192.6 53.8 %gather_4.1 = bf16[16,128,2048]{2,1,0:T(8,128)(2,1)} custom-call(bf16[128,2048]{1,0:T(8,128)(2,1)} %multiply_convert_fusion.2.x_ref), custom_call_target="tpu_custom_call" | custom-call | tf_op jit(solution)/shard_map/gather_4/pallas_call | solution.py:304
  249.7 1.2 convert_bitcast_fusion.3
  252.2 1.0 copy-done.30
  253.7 2.3 constant_dynamic-update-slice_fusion.1
  255.9 2.4 copy-done.14
  258.3 7.2 %fusion.10 = f32[2048,768]{0,1:T(8,128)S(1)} fusion(bf16[2048,2048]{1,0:T(8,128)(2,1)S(1)} %bitcast.136, bf16[2048,1152]{1,0:T(8,128)(2,1)S(1)} %bitcast.144), kind=kOutput, calls=%fused_computation.25 | convolution fusion | flops 6442450944 | bytes 17825792 | tf_op jit(solution)/shard_map/dot_general | solution.py:1289
  265.6 1.1 multiply_convert_fusion.1
  266.7 1.6 copy-done.17
  268.2 7.3 %convolution_convert_fusion.1 = bf16[2048,2048]{1,0:T(8,128)(2,1)} fusion(bf16[2048,384]{0,1:T(8,128)(2,1)S(1)} %multiply_convert_fusion.1, bf16[2048,1152]{1,0:T(8,128)(2,1)S(1)} %bitcast.145), kind=kOutput, calls=%fused_computation.5 | convolution fusion | flops 3225419776 | bytes 11534336 | tf_op jit(solution)/shard_map/dot_general | solution.py:1281
  275.5 37.6 %scatter_5.1 = f32[128,2048]{1,0:T(8,128)} custom-call(bf16[16,128,2048]{2,1,0:T(8,128)(2,1)} %bitcast.135), custom_call_target="tpu_custom_call" | custom-call | tf_op jit(solution)/shard_map/scatter_5/pallas_call | solution.py:327
  313.1 2.5 multiply_convert_fusion.3.x_ref
  315.6 33.8 %gather_6.1 = bf16[16,128,2048]{2,1,0:T(8,128)(2,1)} custom-call(bf16[128,2048]{1,0:T(8,128)(2,1)} %multiply_convert_fusion.3.x_ref), custom_call_target="tpu_custom_call" | custom-call | tf_op jit(solution)/shard_map/gather_6/pallas_call | solution.py:304
  349.4 9.6 %fusion.123 = bf16[2048,384]{1,0:T(8,128)(2,1)} fusion(bf16[2048,2048]{1,0:T(8,128)(2,1)} %bitcast.140, bf16[2048,384]{0,1:T(8,128)(2,1)} %copy-done.33), kind=kOutput, calls=%fused_computation.251 | convolution fusion | flops 3221225472 | bytes 11534336 | tf_op jit(solution)/shard_map/dot_general | solution.py:1277
  359.1 8.5 %fusion.8 = (bf16[2048,384]{0,1:T(8,128)(2,1)S(1)}, bf16[2048,384]{0,1:T(8,128)(2,1)S(1)}) fusion(f32[2048,768]{0,1:T(8,128)} %copy-done.17, bf16[2048,2048]{1,0:T(8,128)(2,1)S(1)} %bitcast.141, bf16[2048,1152]{1,0:T(8,128)(2,1)} %bitcast.146), kind=kOutput, calls=%fused_computation.18 | convolution fusion | flops 3240099840 | bytes 19398656 | tf_op jit(solution)/shard_map/dot_general | solution.py:1289
  367.6 8.2 %fusion.12 = bf16[2048,768]{1,0:T(8,128)(2,1)} fusion(bf16[2048,2048]{1,0:T(8,128)(2,1)S(1)} %bitcast.139, bf16[2048,384]{0,1:T(8,128)(2,1)S(1)} %get-tuple-element.75, bf16[2048,384]{0,1:T(8,128)(2,1)S(1)} %get-tuple-element.74), kind=kOutput, calls=%fused_computation.39 | convolution fusion | flops 6448742400 | bytes 14680064 | tf_op jit(solution)/shard_map/dot_general | solution.py:1277
  375.8 9.2 %convolution_convert_fusion = bf16[2048,2048]{1,0:T(8,128)(2,1)} fusion(bf16[2048,1152]{1,0:T(8,128)(2,1)S(1)} %bitcast.149, bf16[2048,384]{0,1:T(8,128)(2,1)S(1)} %get-tuple-element.75, bf16[2048,384]{0,1:T(8,128)(2,1)S(1)} %get-tuple-element.74), kind=kOutput, calls=%fused_computation.4 | convolution fusion | flops 6452936704 | bytes 14680064 | tf_op jit(solution)/shard_map/dot_general | solution.py:1281
  385.0 34.2 %scatter_7.1 = f32[128,2048]{1,0:T(8,128)} custom-call(bf16[16,128,2048]{2,1,0:T(8,128)(2,1)} %bitcast.134), custom_call_target="tpu_custom_call" | custom-call | tf_op jit(solution)/shard_map/scatter_7/pallas_call | solution.py:327
  419.2 2.9 pad_maximum_fusion
  422.1 2.6 copy.53
  426.5 3.2 multiply_reduce_fusion.7
  429.8 1.8 fusion.111
  431.6 23.4 %gather_8.1 = bf16[8,128,2048]{2,1,0:T(8,128)(2,1)} custom-call(bf16[128,2048]{1,0:T(8,128)(2,1)} %get-tuple-element.66.x_ref), custom_call_target="tpu_custom_call" | custom-call | tf_op jit(solution)/shard_map/gather_8/pallas_call | solution.py:304
  455.0 8.2 %fusion.19 = (bf16[1024,384]{1,0:T(8,128)(2,1)}, f32[1024,384]{1,0:T(8,128)}) fusion(f32[1024,384]{1,0:T(8,128)} %forward_scan.1, f32[1024,896]{1,0:T(8,128)} %copy-done.25, pred[384]{0:T(512)(128)(4,1)S(1)} %copy-done.73, bf16[1024,2048]{1,0:T(8,128)(2,1)} %bitcast.130, bf16[2048,384]{1,0:T(8,128)(2,1)} %bitcast.185), kind=kOutput, calls=%fused_computation.55 | convolution fusion | flops 1620049920 | bytes 11272576 | tf_op jit(solution)/shard_map/dot_general | solution.py:1289
  463.3 4.8 backward_scan.1
  468.1 4.8 multiply_reduce_fusion.6
  474.4 1.0 select_add_fusion
  476.6 2.1 multiply_reduce_fusion.2
  479.8 10.0 %multiply_reduce_fusion.1 = (f32[2048]{0:T(1024)S(1)}, f32[2048,896]{1,0:T(8,128)}) fusion(bf16[8,4,64,896]{3,2,1,0:T(8,128)(2,1)} %get-tuple-element.37, bf16[1024,2048]{1,0:T(8,128)(2,1)} %copy-done.22, bf16[1024,256]{1,0:T(8,128)(2,1)S(1)} %get-tuple-element.86, bf16[1024,384]{1,0:T(8,128)(2,1)S(1)} %copy-done.81, bf16[1024,256]{1,0:T(8,128)(2,1)S(1)} %get-tuple-element.85), kind=kOutput, calls=%fused_computation.6 | convolution fusion | flops 3769104384 | bytes 17047552 | tf_op jit(solution)/shard_map/dot_general | solution.py:1277
  491.7 6.6 copy.46
  498.3 1.0 fusion.55
  500.5 2.6 copy-done.23
  503.4 4.0 fusion.47.refs_2_
  507.4 6.2 convolution_convert_fusion.3
  513.6 18.0 %reduce-scatter.2.cloned.1.call-done = bf16[8,1,2,64,1152]{4,3,2,0,1:T(8,128)(2,1)} async-done(((bf16[8,2,2,64,1152]{4,3,2,0,1:T(8,128)(2,1)}), bf16[8,1,2,64,1152]{4,3,2,0,1:T(8,128)(2,1)}) %reduce-scatter.2.cloned.1.call-update) | async-done | bytes 2359312 | tf_op jit(solution)/shard_map/reduce_scatter | solution.py:1258
  531.6 123.2 %closing.1 = (f32[128,2048]{1,0:T(8,128)}, bf16[64,2560]{1,0:T(8,128)(2,1)}, bf16[64,2560]{1,0:T(8,128)(2,1)}, bf16[2,64,2560]{2,1,0:T(8,128)(2,1)}, bf16[64,614...) custom-call(bf16[8,128,2048]{2,1,0:T(8,128)(2,1)} %bitcast.150, ...), custom_call_target="tpu_custom_call" | custom-call | tf_op jit(solution)/shard_map/closing/pallas_call | solution.py:1144
  654.8 1.4 slice_bitcast_fusion.3
  656.2 1.3 slice.299
  657.5 1.2 slice.295
  658.7 1.3 slice_bitcast_fusion.2
  659.9 2.5 convert_bitcast_fusion
  662.4 1.2 convert_element_type.219
  663.7 1.2 convert_element_type.220
  668.4 1.0 fusion.50
  669.4 1.1 fusion.53
  (240 shorter events, 25.1 us)
Async XLA Ops:
  7.2 524.5 %reduce-scatter.2.cloned.1.call-start = ((), (), s32[]{:S(2)}) async-start(), calls=%async_computation.1 | async-start | bytes 7077888 | tf_op jit(solution)/shard_map/reduce_scatter | solution.py:1258
  124.9 128.8 %collective-permute-start = (bf16[8,2,64,1152]{3,2,1,0:T(8,128)(2,1)}, bf16[8,2,64,1152]{3,2,1,0:T(8,128)(2,1)}, u32[]{:S(2)}, u32[]{:S(2)}) collective-permute-start(bf16[8,2,64,1152]{3,2,1,0:T(8,128)(2,1)} %get-tuple-element.39), channel_id=1, source_target_pairs={{0,2},{1,3},{2,0},{3,1},{4,6},{5,7},{6,4},{7,5},{8,10},{9,11},{10,... | collective-permute-start | bytes 7077896 | tf_op jit(solution)/shard_map/ppermute | solution.py:1229
  131.5 2.3 copy-start.44
  134.5 3.2 copy-start.47
  134.5 3.5 copy-start.7
  138.0 2.1 copy-start.78
  139.0 5.6 copy-start.22
  147.6 3.6 copy-start.50
  148.4 2.7 copy-start.2
  155.0 4.8 copy-start.72
  159.8 2.6 copy-start.80
  162.4 4.4 copy-start.35
  251.6 61.5 %copy-start.69 = (f32[128]{0:T(128)}, f32[128]{0:T(128)S(1)}, u32[]{:S(2)}) copy-start(f32[128]{0:T(128)S(1)} %broadcast_multiply_fusion.1) | copy-start | bytes 1540
  253.2 5.1 copy-start.14
  255.9 10.7 %copy-start.20 = (bf16[8,4,64,1152]{3,2,1,0:T(8,128)(2,1)}, bf16[8,4,64,1152]{3,2,1,0:T(8,128)(2,1)S(1)}, u32[]{:S(2)}) copy-start(bf16[8,4,64,1152]{3,2,1,0:T(8,128)(2,1)S(1)} %constant_dynamic-update-slice_fusion.1) | copy-start | bytes 14155780
  265.6 2.7 copy-start.17
  268.2 7.3 %copy-start.33 = (bf16[2048,384]{0,1:T(8,128)(2,1)}, bf16[2048,384]{0,1:T(8,128)(2,1)S(1)}, u32[]{:S(2)}) copy-start(bf16[2048,384]{0,1:T(8,128)(2,1)S(1)} %multiply_convert_fusion.1) | copy-start | bytes 4718596
  275.5 37.6 %copy-start.18 = (bf16[1,128,2048]{2,1,0:T(8,128)(2,1)S(1)}, bf16[1,128,2048]{2,1,0:T(8,128)(2,1)}, u32[]{:S(2)}) copy-start(bf16[1,128,2048]{2,1,0:T(8,128)(2,1)} %param.20) | copy-start | bytes 1572868
  349.4 9.7 %copy-start.15 = (bf16[16,128,2048]{2,1,0:T(8,128)(2,1)S(1)}, bf16[16,128,2048]{2,1,0:T(8,128)(2,1)}, u32[]{:S(2)}) copy-start(bf16[16,128,2048]{2,1,0:T(8,128)(2,1)} %gather_6.1) | copy-start | bytes 25165828
  349.4 18.1 %slice-start = ((s8[8388608]{0:T(1024)(128)(4,1)}), s8[4194304]{0:T(1024)(128)(4,1)S(1)}, s32[]{:S(2)}) async-start(s8[8388608]{0:T(1024)(128)(4,1)} %bitcast.137), calls=%async_computation.2 | async-start | bytes 8388608
  359.1 8.5 %slice-start.1 = ((s8[8388608]{0:T(1024)(128)(4,1)}), s8[4194304]{0:T(1024)(128)(4,1)S(1)}, s32[]{:S(2)}) async-start(s8[8388608]{0:T(1024)(128)(4,1)} %bitcast.137), calls=%async_computation.3 | async-start | bytes 8388608
  359.1 16.7 %slice-start.2 = ((s8[4718592]{0:T(1024)(128)(4,1)}), s8[524288]{0:T(1024)(128)(4,1)S(1)}, s32[]{:S(2)}) async-start(s8[4718592]{0:T(1024)(128)(4,1)} %bitcast.147), calls=%async_computation.4 | async-start | bytes 1048576
  367.6 8.2 %slice-start.3 = ((s8[4718592]{0:T(1024)(128)(4,1)}), s8[4194304]{0:T(1024)(128)(4,1)S(1)}, s32[]{:S(2)}) async-start(s8[4718592]{0:T(1024)(128)(4,1)} %bitcast.147), calls=%async_computation.5 | async-start | bytes 8388608
  424.7 5.0 copy-start.77
  424.7 5.0 copy-start.1
  424.8 5.0 copy-start.4
  424.8 5.0 copy-start.9
  424.8 5.0 copy-start.19
  424.8 5.0 copy-start.68
  424.8 5.0 copy-start.70
  431.6 23.4 %copy-start.73 = (pred[384]{0:T(512)(128)(4,1)S(1)}, pred[384]{0:T(512)(128)(4,1)}, u32[]{:S(2)}) copy-start(pred[384]{0:T(512)(128)(4,1)} %iota_compare_fusion.7) | copy-start | bytes 1156
  463.3 4.9 copy-start.51
  468.1 4.8 copy-start.53
  474.4 1.9 copy-start.11
  474.4 2.2 copy-start.13
  474.4 2.2 copy-start.55
  474.4 2.2 copy-start.57
  474.4 2.1 copy-start.59
  474.4 2.1 copy-start.61
  478.9 10.9 %copy-start.40 = (bf16[1024,256]{1,0:T(8,128)(2,1)}, bf16[1024,256]{1,0:T(8,128)(2,1)S(1)}, u32[]{:S(2)}) copy-start(bf16[1024,256]{1,0:T(8,128)(2,1)S(1)} %get-tuple-element.86) | copy-start | bytes 1572868
  479.8 10.1 %copy-start.49 = (f32[2048]{0:T(1024)S(1)}, f32[2048]{0:T(1024)}, u32[]{:S(2)}) copy-start(f32[2048]{0:T(1024)} %get-tuple-element.57) | copy-start | bytes 24580
  479.8 10.9 %copy-start.45 = (f32[2,32,64]{2,1,0:T(8,128)S(1)}, f32[2,32,64]{2,1,0:T(8,128)}, u32[]{:S(2)}) copy-start(f32[2,32,64]{2,1,0:T(8,128)} %copy-done.44) | copy-start | bytes 49156
  479.8 10.9 %copy-start.74 = (f32[16]{0:T(128)S(1)}, f32[16]{0:T(128)}, u32[]{:S(2)}) copy-start(f32[16]{0:T(128)} %pad.107.clone) | copy-start | bytes 196
  491.7 6.6 copy-start.6
  491.7 6.6 copy-start.27
  491.7 6.6 copy-start.29
  500.0 3.1 copy-start.23
  500.3 3.1 copy-start.36
  500.5 6.9 %copy-start.8 = (bf16[2560,512]{1,0:T(8,128)(2,1)}, bf16[2560,512]{1,0:T(8,128)(2,1)S(1)}, u32[]{:S(2)}) copy-start(bf16[2560,512]{1,0:T(8,128)(2,1)S(1)} %maximum_dynamic-update-slice_fusion) | copy-start | bytes 7864324
  503.4 4.0 copy-start.41
  503.4 4.0 copy-start.79
  503.4 4.0 copy-start.82
  654.8 7.6 %copy-start.38 = (bf16[64,6144]{1,0:T(8,128)(2,1)S(1)}, bf16[64,6144]{1,0:T(8,128)(2,1)}, u32[]{:S(2)}) copy-start(bf16[64,6144]{1,0:T(8,128)(2,1)} %get-tuple-element.49) | copy-start | bytes 2359300
  659.9 3.7 copy-start.37
  662.4 2.5 copy-start.43
  663.6 2.2 copy-start.42
  663.7 3.1 copy-start.16
  663.7 3.1 copy-start.24
  663.7 3.1 copy-start.48
  664.9 2.1 copy-start.46
  664.9 3.4 copy-start.39
  664.9 3.4 copy-start.62
  664.9 3.5 copy-start.63
  665.8 3.5 copy-start.21
  (25 other events, 26.2 us)
Sparse Core Ops, SparseCore 0:
  424.9 106.7 reduce-scatter.1
